TPU v7x, 768 devices: a whole 4x8x12 slice. The times are simulated.
768 devices in a mesh: ctx: 96 (over x, z_lo, y), tp: 8 (over z_hi, core).
Axes of the slice: x: 4, y: 8, z: 12 (z_hi: 4, z_lo: 3; z = z_hi * 3 + z_lo), core: 2. Of those that a mesh axis runs over, the one named last changes fastest.
Arguments:
- features: bfloat16 [3, 24576, 8192], P(None, 'ctx', 'tp'), may hold values from -6 to 6
- short_taps: bfloat16 [3, 512, 7], P(None, 'tp'), may hold values from -2 to 2
- long_taps: bfloat16 [512, 128], P('tp'), may hold values from -0.5 to 0.5
- skip_gain: bfloat16 [8192], P('tp'), may hold values from -4 to 4
- cotangent: bfloat16 [24576, 8192], P('ctx', 'tp'), may hold values from -6 to 6
Outputs:
- gated: bfloat16 [24576, 8192], P('ctx', 'tp')
- feature_grad: bfloat16 [3, 24576, 8192], P(None, 'ctx', 'tp')
- short_grad: float32 [3, 512, 7], P(None, 'tp')
- long_grad: float32 [512, 128], P('tp')
- skip_grad: float32 [8192], P('tp')
All inputs are finite; a program needn't handle non-finite values.
Results may differ from a plain program's by a relative error of at most 0.0074.
Values may be sent and summed in bfloat16 or wider, within the bound.
No kernel may reach another device: no remote copies, remote signals or barrier semaphores. Data moves between devices by JAX's collectives and lax.ppermute only.
A program may use at most 128 MiB of HBM per device.

v0:
```python
import functools
import math

import jax
import jax.numpy as jnp
from jax import lax
from jax.sharding import Mesh
from jax.sharding import PartitionSpec as P

CTX = ("ctx_0", "ctx_1", "ctx_2")


def passed_along(block, axis, distance):
    devices = range(lax.axis_size(axis))
    route = [(i - distance, i) for i in devices if i - distance in devices]
    return lax.ppermute(block, axis, route)


def one_axis_at_a_time(shard, axes):
    return functools.reduce(lax.psum, axes, shard)


def settle(values):
    return lax.optimization_barrier(values)


def short_filter(padded, taps, rows):
    total = jnp.zeros((padded.shape[0], rows, padded.shape[2]), jnp.float32)
    for offset in range(7):
        total = total + taps[:, None, :, offset] * padded[:, 6 - offset : 6 - offset + rows].astype(
            jnp.float32
        )
    return total


def toeplitz_blocks(filt):
    groups = filt.shape[0]
    extra = jnp.concatenate([filt, jnp.zeros((groups, 1), filt.dtype)], axis=1)
    row_pos = jnp.arange(128, dtype=jnp.int32)[:, None]
    col_pos = jnp.arange(256, dtype=jnp.int32)[None, :]
    shift_lag = row_pos + 128 - col_pos
    valid = (shift_lag >= 0) & (shift_lag < 128)
    picks = jnp.where(valid, shift_lag, 128)
    return jnp.take(extra, picks, axis=1)


def diagonal_sums(grid):
    groups = grid.shape[0]
    padded = jnp.pad(grid, ((0, 0), (0, 0), (0, 126)))
    flat = jnp.pad(padded.reshape(groups, 128 * 382), ((0, 0), (0, 128)))
    folded = flat.reshape(groups, 128, 383).sum(axis=1)
    return folded[:, 1:129][:, ::-1]


def to_blocks(rows_first, groups):
    return rows_first.T.reshape(groups, 16, rows_first.shape[0])


def body(features, short_taps, long_taps, skip_gain, cotangent):
    rows = features.shape[1]
    width = features.shape[2]
    groups = width // 16
    blocks = rows // 128
    taps = jnp.repeat(short_taps, 16, axis=1).astype(jnp.float32)
    gain = skip_gain.astype(jnp.float32)
    zero_row = jnp.zeros((1, width), jnp.bfloat16)
    edge = passed_along(features[:, rows - 133 :], CTX, 1)
    wide = jnp.concatenate([edge, features], axis=1)
    mixed_all = settle(short_filter(wide, taps, rows + 127).astype(jnp.bfloat16))
    product_all = settle(
        (mixed_all[1].astype(jnp.float32) * mixed_all[2].astype(jnp.float32)).astype(jnp.bfloat16)
    )
    mixed = mixed_all[:, 127:]
    product = product_all[127:]
    extended = jnp.concatenate([zero_row, product_all], axis=0)
    padded = wide[:, 127:]
    query = mixed[0].astype(jnp.float32)
    key = mixed[1].astype(jnp.float32)
    value = mixed[2].astype(jnp.float32)
    kernel = toeplitz_blocks(long_taps)
    earlier = kernel[:, :, :128]
    current = kernel[:, :, 128:]
    ext_t = to_blocks(extended, groups)
    before = ext_t[:, :, :rows].reshape(groups, 16 * blocks, 128)
    present = ext_t[:, :, 128:].reshape(groups, 16 * blocks, 128)
    conv = jnp.einsum("gts,gns->gnt", earlier, before, preferred_element_type=jnp.float32)
    conv = conv + jnp.einsum("gts,gns->gnt", current, present, preferred_element_type=jnp.float32)
    conv = conv.reshape(width, rows).T
    prod_f = product.astype(jnp.float32)
    inner = conv + gain * prod_f
    gated = (query * inner).astype(jnp.bfloat16)
    grad_in = cotangent.astype(jnp.float32)
    grad_query = grad_in * inner
    grad_inner = settle((grad_in * query).astype(jnp.bfloat16))
    ahead = passed_along(grad_inner[:127], CTX, -1)
    later = jnp.concatenate([grad_inner, ahead, zero_row], axis=0)
    later_t = to_blocks(later, groups)
    this_block = later_t[:, :, :rows].reshape(groups, 16 * blocks, 128)
    next_block = later_t[:, :, 128:].reshape(groups, 16 * blocks, 128)
    back = jnp.einsum("gts,gnt->gns", current, this_block, preferred_element_type=jnp.float32)
    back = back + jnp.einsum(
        "gts,gnt->gns", earlier, next_block, preferred_element_type=jnp.float32
    )
    back = back.reshape(width, rows).T
    inner_f = grad_inner.astype(jnp.float32)
    grad_product = settle((back + gain * inner_f).astype(jnp.bfloat16))
    product_g = grad_product.astype(jnp.float32)
    grad_mixed = settle(
        jnp.stack([grad_query, product_g * value, product_g * key], axis=0).astype(jnp.bfloat16)
    )
    head = passed_along(grad_mixed[:, :6], CTX, -1)
    trailing = jnp.concatenate([grad_mixed, head], axis=1)
    feature_grad = jnp.zeros((3, rows, width), jnp.float32)
    for offset in range(7):
        feature_grad = feature_grad + taps[:, None, :, offset] * trailing[
            :, offset : offset + rows
        ].astype(jnp.float32)
    grid = jnp.concatenate(
        [
            jnp.einsum("gnt,gns->gts", this_block, before, preferred_element_type=jnp.float32),
            jnp.einsum("gnt,gns->gts", this_block, present, preferred_element_type=jnp.float32),
        ],
        axis=2,
    )
    long_local = diagonal_sums(grid)
    skip_local = jnp.sum(inner_f * prod_f, axis=0)
    mixed_g = grad_mixed.astype(jnp.float32)
    short_all = jnp.stack(
        [
            jnp.sum(mixed_g * padded[:, 6 - offset : 6 - offset + rows].astype(jnp.float32), axis=1)
            for offset in range(7)
        ],
        axis=-1,
    )
    short_local = short_all.reshape(3, groups, 16, 7).sum(axis=2)
    long_sum, skip_sum, short_sum = (
        one_axis_at_a_time(long_local, CTX),
        one_axis_at_a_time(skip_local, CTX),
        one_axis_at_a_time(short_local, CTX),
    )
    total = rows * lax.axis_size(CTX)
    group_scale = 1.0 / math.sqrt(16.0 * total)
    token_scale = 1.0 / math.sqrt(1.0 * total)
    return (
        gated,
        feature_grad.astype(jnp.bfloat16),
        short_sum * group_scale,
        long_sum * group_scale,
        skip_sum * token_scale,
    )


def solution(mesh):
    torus = Mesh(mesh.devices.reshape(4, 3, 8, mesh.shape["tp"]), ("ctx_0", "ctx_1", "ctx_2", "tp"))
    return jax.shard_map(
        body,
        mesh=torus,
        in_specs=(P(None, CTX, "tp"), P(None, "tp", None), P("tp", None), P("tp"), P(CTX, "tp")),
        out_specs=(P(CTX, "tp"), P(None, CTX, "tp"), P(None, "tp", None), P("tp", None), P("tp")),
        check_vma=False,
    )
```

profile of v0, /device:TPU:192, one launch (start us, length us, event | category | flops | bytes accessed | tf_op | source)
XLA Modules:
  0.0 371.7 jit_solution(217943937078530003)
XLA Ops:
  2.1 3.5 collective-permute-start
  5.6 2.6 copy.49
  9.5 114.2 %gather_fusion = bf16[32768,64]{1,0:T(8,128)(2,1)} fusion(bf16[64,129]{0,1:T(8,128)(2,1)S(1)} %concatenate.21, s32[32768]{0:T(1024)S(1)} %broadcast_clamp_fusion), kind=kCustom, calls=%fused_computation | custom fusion | bytes 8519680 | tf_op jit(solution)/shard_map/jit(_take)/gather | solution.py:44
  123.7 10.1 %copy.60 = bf16[128,256,64]{1,0,2:T(8,128)(2,1)} copy(bf16[128,256,64]{2,1,0:T(8,128)(2,1)} %bitcast.76) | data formatting | bytes 8388608 | tf_op jit(solution)/shard_map/jit(_take)/gather | solution.py:44
  134.1 4.5 %select_bitcast_fusion = bf16[64,128,256]{2,1,0:T(8,128)(2,1)} fusion(bf16[128,256,64]{1,0,2:T(8,128)(2,1)} %copy.60, pred[128,256]{1,0:T(8,128)(4,1)S(1)} %fusion.65), kind=kLoop, calls=%fused_computation.40 | loop fusion | flops 2097152 | bytes 8421376 | tf_op jit(solution)/shard_map/jit(_take)/select_n | solution.py:44
  140.1 14.9 %add_convert_fusion = bf16[3,383,1024]{1,2,0:T(8,128)(2,1)S(1)} fusion(bf16[3,133,1024]{1,2,0:T(8,128)(2,1)} %copy.48, bf16[3,256,1024]{1,2,0:T(8,128)(2,1)} %copy.49, f32[3,1024]{1,0:T(4,128)S(1)} %get-tuple-element.52, f32[3,1024]{1,0:T(4,128)S(1)} %get-tuple-element.53, f32[3,1024]{1,0:T(4,128)S(1)} %get-tuple-element.54, ...), kind=kLoop, calls=%fused_computation.34 | loop fusion | flops 49416192 | bytes 4829184 | tf_op jit(solution)/shard_map/convert_element_type | solution.py:69
  160.4 2.2 reshape.150
  162.7 2.8 fusion.23
  165.5 3.8 %fusion.39 = f32[64,32,128]{2,1,0:T(8,128)} fusion(f32[64,32,128]{2,1,0:T(8,128)S(1)} %fusion.23, bf16[64,32,128]{2,1,0:T(8,128)(2,1)S(1)} %copy-done.7, bf16[64,128,256]{2,1,0:T(8,128)(2,1)} %select_bitcast_fusion), kind=kOutput, calls=%fused_computation.89 | convolution fusion | flops 67371008 | bytes 4718592 | tf_op jit(solution)/shard_map/gts,gns->gnt/dot_general | solution.py:86
  169.3 2.6 reshape.152
  175.3 3.2 fusion.21
  178.5 2.0 reshape.155
  180.5 3.6 fusion.42
  184.2 2.5 reshape.156
  188.1 3.9 %fusion.56 = (bf16[1,256,1024]{1,2,0:T(8,128)(2,1)S(1)}, bf16[1,256,1024]{1,2,0:T(8,128)(2,1)S(1)}, bf16[256,1024]{0,1:T(8,128)(2,1)}, bf16[1,256,1024]{1,2,0:T(8,128)(2,1)S(1)}, f32[1024]{0:T(1024)S(1)}) fusion(bf16[256,1024]{0,1:T(8,128)(2,1)S(1)} %fusion.48, bf16[3,383,1024]{1,2,0:T(8,128)(2,1)S(1)} %add_convert_fusion, bf16[383,1024]{0,1:T(8,128)(2,1)} %copy-done.4, ...), kind=kLoop, calls=%fused_computation.111 | loop fusion | flops 4979712 | bytes 6823936 | tf_op jit(solution)/shard_map/stack | solution.py:109
  192.2 1.8 copy-done.2
  194.4 7.6 %fusion.13 = (f32[3,1024]{1,0:T(4,128)S(1)}, f32[3,1024]{1,0:T(4,128)S(1)}, f32[3,1024]{1,0:T(4,128)S(1)}, f32[3,1024]{1,0:T(4,128)S(1)}, f32[3,1024]{1,0:T(4,12...) fusion(bf16[3,256,1024]{1,2,0:T(8,128)(2,1)S(1)} %pad_maximum_fusion.3, bf16[3,256,1024]{1,2,0:T(8,128)(2,1)S(1)} %copy-done.2, ...), kind=kLoop, calls=%fused_computation.54 | loop fusion | flops 31435776 | bytes 4048896 | tf_op jit(solution)/shard_map/reduce_sum | solution.py:130
  202.1 2.7 fusion.72
  204.8 2.8 fusion.71
  207.9 1.5 collective-permute-start.2
  210.1 7.8 %pad_maximum_fusion = f32[64,128,256]{1,2,0:T(8,128)} fusion(f32[64,128,128]{1,2,0:T(8,128)} %fusion.72, f32[64,128,128]{1,2,0:T(8,128)} %fusion.71), kind=kLoop, calls=%fused_computation.9 | loop fusion | flops 2097152 | bytes 16777216 | tf_op jit(solution)/shard_map/concatenate | solution.py:118
  217.9 9.1 %copy.68 = f32[64,128,256]{2,1,0:T(8,128)} copy(f32[64,128,256]{1,2,0:T(8,128)} %pad_maximum_fusion) | data formatting | bytes 16777216
  227.3 9.6 %pad.10.clone = f32[64,128,382]{2,1,0:T(8,128)} pad(f32[64,128,256]{2,1,0:T(8,128)} %copy.68, f32[]{:T(128)} %constant.13.clone.1), padding=0_0x0_0x0_126 | pad | bytes 20905988 | tf_op jit(solution)/shard_map/jit(_pad)/pad | solution.py:49
  236.9 14.0 %reshape.157 = f32[64,48896]{1,0:T(8,128)} reshape(f32[64,128,382]{2,1,0:T(8,128)} %pad.10.clone) | data formatting | bytes 25034752 | tf_op jit(solution)/shard_map/reshape | solution.py:50
  251.0 9.9 %pad.11 = f32[64,49024]{1,0:T(8,128)} pad(f32[64,48896]{1,0:T(8,128)} %reshape.157, f32[]{:T(128)} %constant.13.clone.1), padding=0_0x0_128 | pad | bytes 25067524 | tf_op jit(solution)/shard_map/jit(_pad)/pad | solution.py:50
  260.9 17.2 %reshape.158 = f32[64,128,383]{2,1,0:T(8,128)} reshape(f32[64,49024]{1,0:T(8,128)} %pad.11) | data formatting | bytes 25100288 | tf_op jit(solution)/shard_map/reshape | solution.py:51
  278.1 6.1 %reduce_sum.98 = f32[64,383]{1,0:T(8,128)S(1)} reduce(f32[64,128,383]{2,1,0:T(8,128)} %reshape.158, f32[]{:T(128)} %constant.13.clone.1), dimensions={1}, to_apply=%region_11.12 | reduce | flops 3113024 | bytes 12648196 | tf_op jit(solution)/shard_map/reduce_sum | solution.py:51
  284.4 27.8 %all-reduce.5 = (f32[3,64,7]{1,0,2:T(4,128)S(1)}, f32[64,128]{1,0:T(8,128)S(1)}, f32[1024]{0:T(1024)S(1)}) all-reduce(f32[3,64,7]{1,0,2:T(4,128)S(1)} %reduce_sum.97, f32[64,128]{1,0:T(8,128)S(1)} %rev.3, f32[1024]{0:T(1024)S(1)} %get-tuple-element.40), channel_id=1, replica_groups=mesh['ctx_0'=4,'ctx_1'=3,'ctx_2'=8,'tp'=8] {'ctx_0'}, use_global_device_ids=true, to_apply=%region_8.9 | all-reduce | flops 10560 | bytes 84480 | tf_op jit(solution)/shard_map/psum | solution.py:20
  312.2 13.2 %all-reduce.6 = (f32[3,64,7]{1,0,2:T(4,128)S(1)}, f32[64,128]{1,0:T(8,128)S(1)}, f32[1024]{0:T(1024)S(1)}) all-reduce(f32[3,64,7]{1,0,2:T(4,128)S(1)} %get-tuple-element.30, f32[64,128]{1,0:T(8,128)S(1)} %get-tuple-element.31, f32[1024]{0:T(1024)S(1)} %get-tuple-element.32), channel_id=1, replica_groups=mesh['ctx_0'=4,'ctx_1'=3,'ctx_2'=8,'tp'=8] {'ctx_1'}, use_global_device_ids=true, to_apply=%region_9.10 | all-reduce | flops 10560 | bytes 84480 | tf_op jit(solution)/shard_map/psum | solution.py:20
  325.4 27.5 %all-reduce.4 = (f32[3,64,7]{1,0,2:T(4,128)S(1)}, f32[64,128]{1,0:T(8,128)S(1)}, f32[1024]{0:T(1024)S(1)}) all-reduce(f32[3,64,7]{1,0,2:T(4,128)S(1)} %get-tuple-element.33, f32[64,128]{1,0:T(8,128)S(1)} %get-tuple-element.34, f32[1024]{0:T(1024)S(1)} %get-tuple-element.35), channel_id=1, replica_groups=mesh['ctx_0'=4,'ctx_1'=3,'ctx_2'=8,'tp'=8] {'ctx_2'}, use_global_device_ids=true, to_apply=%region_10.11 | all-reduce | flops 10560 | bytes 84480 | tf_op jit(solution)/shard_map/psum | solution.py:20
  357.0 13.0 %fusion.6 = bf16[3,256,1024]{1,2,0:T(8,128)(2,1)S(1)} fusion(bf16[3,256,1024]{1,2,0:T(8,128)(2,1)S(1)} %copy-done.1, bf16[3,6,1024]{1,2,0:T(8,128)(2,1)} %copy.54, f32[3,1024]{1,0:T(4,128)S(1)} %get-tuple-element.52, f32[3,1024]{1,0:T(4,128)S(1)} %get-tuple-element.53, f32[3,1024]{1,0:T(4,128)S(1)} %get-tuple-element.54, ...), kind=kLoop, calls=%fused_computation.47 | loop fusion | flops 30670848 | bytes 3268608 | tf_op jit(solution)/shard_map/convert_element_type | solution.py:146
  370.0 1.7 copy.58
  (89 shorter events, 20.8 us)
Async XLA Ops:
  0.6 7.6 %copy-start.11 = (bf16[256,1024]{1,0:T(8,128)(2,1)S(1)}, bf16[256,1024]{1,0:T(8,128)(2,1)}, u32[]{:S(2)}) copy-start(bf16[256,1024]{1,0:T(8,128)(2,1)} %param.9) | copy-start | bytes 1572868
  0.6 7.8 %copy-start.13 = (bf16[3,64,7]{1,2,0:T(8,128)(2,1)S(1)}, bf16[3,64,7]{1,2,0:T(8,128)(2,1)}, u32[]{:S(2)}) copy-start(bf16[3,64,7]{1,2,0:T(8,128)(2,1)} %param.6) | copy-start | bytes 8068
  2.1 7.1 %copy-start.12 = (bf16[64,128]{1,0:T(8,128)(2,1)S(1)}, bf16[64,128]{1,0:T(8,128)(2,1)}, u32[]{:S(2)}) copy-start(bf16[64,128]{1,0:T(8,128)(2,1)} %param.7) | copy-start | bytes 49156
  2.1 136.5 %collective-permute-start = (bf16[3,133,1024]{2,1,0:T(8,128)(2,1)S(1)}, bf16[3,133,1024]{2,1,0:T(8,128)(2,1)S(1)}, u32[]{:S(2)}, u32[]{:S(2)}) collective-permute-start(bf16[3,133,1024]{2,1,0:T(8,128)(2,1)S(1)} %slice.147), channel_id=1, source_target_pairs={{0,8},{8,16},{16,24},{24,32},{32,40},{40,48},{48,56},{56,64},{64,7... | collective-permute-start | bytes 2451464 | tf_op jit(solution)/shard_map/ppermute | solution.py:16
  8.5 146.7 %copy-start.9 = (bf16[256,1024]{0,1:T(8,128)(2,1)}, bf16[256,1024]{0,1:T(8,128)(2,1)S(1)}, u32[]{:S(2)}) copy-start(bf16[256,1024]{0,1:T(8,128)(2,1)S(1)} %copy.52) | copy-start | bytes 1572868
  123.7 10.1 %copy-start.14 = (bf16[1024]{0:T(1024)(128)(2,1)S(1)}, bf16[1024]{0:T(1024)(128)(2,1)}, u32[]{:S(2)}) copy-start(bf16[1024]{0:T(1024)(128)(2,1)} %param.8) | copy-start | bytes 6148
  155.2 2.6 copy-start.4
  156.3 15.6 %collective-permute-start.1 = (bf16[127,1024]{0,1:T(8,128)(2,1)}, bf16[127,1024]{0,1:T(8,128)(2,1)}, u32[]{:S(2)}, u32[]{:S(2)}) collective-permute-start(bf16[127,1024]{0,1:T(8,128)(2,1)} %slice.219), channel_id=1, source_target_pairs={{8,0},{16,8},{24,16},{32,24},{40,32},{48,40},{56,48},{64,56},{72,6... | collective-permute-start | bytes 780296 | tf_op jit(solution)/shard_map/ppermute | solution.py:16
  160.4 8.9 %copy-start.5 = (bf16[64,32,128]{2,1,0:T(8,128)(2,1)}, bf16[64,32,128]{2,1,0:T(8,128)(2,1)S(1)}, u32[]{:S(2)}) copy-start(bf16[64,32,128]{2,1,0:T(8,128)(2,1)S(1)} %reshape.151) | copy-start | bytes 1572868
  162.7 2.8 copy-start.7
  192.0 2.0 copy-start.2
  192.0 2.4 copy-start.3
  192.1 9.9 %copy-start = (bf16[3,256,1024]{1,2,0:T(8,128)(2,1)}, bf16[3,256,1024]{1,2,0:T(8,128)(2,1)S(1)}, u32[]{:S(2)}) copy-start(bf16[3,256,1024]{1,2,0:T(8,128)(2,1)S(1)} %pad_maximum_fusion.3) | copy-start | bytes 4718596
  192.1 9.9 %copy-start.6 = (bf16[64,32,128]{2,1,0:T(8,128)(2,1)S(1)}, bf16[64,32,128]{2,1,0:T(8,128)(2,1)}, u32[]{:S(2)}) copy-start(bf16[64,32,128]{2,1,0:T(8,128)(2,1)} %copy-done.5) | copy-start | bytes 1572868
  202.1 2.7 copy-start.8
  204.8 2.8 slice-start
  207.9 147.9 %collective-permute-start.2 = (bf16[3,6,1024]{2,1,0:T(8,128)(2,1)S(1)}, bf16[3,6,1024]{2,1,0:T(8,128)(2,1)S(1)}, u32[]{:S(2)}, u32[]{:S(2)}) collective-permute-start(bf16[3,6,1024]{2,1,0:T(8,128)(2,1)S(1)} %copy.53), channel_id=1, source_target_pairs={{8,0},{16,8},{24,16},{32,24},{40,32},{48,40},{56,48},{64,56},{72,6... | collective-permute-start | bytes 110600 | tf_op jit(solution)/shard_map/ppermute | solution.py:16
  278.1 76.1 %copy-start.10 = (bf16[256,1024]{0,1:T(8,128)(2,1)S(1)}, bf16[256,1024]{0,1:T(8,128)(2,1)}, u32[]{:S(2)}) copy-start(bf16[256,1024]{0,1:T(8,128)(2,1)} %get-tuple-element.38) | copy-start | bytes 1572868
  284.2 72.8 %copy-start.1 = (bf16[3,256,1024]{1,2,0:T(8,128)(2,1)S(1)}, bf16[3,256,1024]{1,2,0:T(8,128)(2,1)}, u32[]{:S(2)}) copy-start(bf16[3,256,1024]{1,2,0:T(8,128)(2,1)} %copy-done) | copy-start | bytes 4718596
where the time goes:
time: 374 us; the launch traced here: 372 us
  local copies, waits for them, and re-layouts  214 us (57%)
  blocking collectives  68.5 us (18%)
  other arithmetic  62.9 us (17%)
  matrix products  19 us (5%)
  starting transfers between devices  6.5 us (2%)
    gather x2, local copies, waits for them, and re-layouts, toeplitz_blocks(): return jnp.take(extra, picks, axis=1)  124 us
    psum x3, blocking collectives, one_axis_at_a_time(): return functools.reduce(lax.psum, axes, shard)  68.5 us
    unnamed x48, local copies, waits for them, and re-layouts  17.8 us
    reshape x1, local copies, waits for them, and re-layouts, diagonal_sums(): folded = flat.reshape(groups, 128, 383).sum(axis=1)  17.2 us
    convert_element_type x1, other arithmetic, body(): short_filter(wide, taps, rows + 127).astype(jnp.bfloat16)  14.9 us
    reshape x1, local copies, waits for them, and re-layouts, diagonal_sums(): flat = jnp.pad(padded.reshape(groups, 128 * 382), ((0, 0), (0, 128)))  14 us
    convert_element_type x1, other arithmetic, body(): feature_grad.astype(jnp.bfloat16)  13 us
    pad x1, local copies, waits for them, and re-layouts, diagonal_sums(): flat = jnp.pad(padded.reshape(groups, 128 * 382), ((0, 0), (0, 128)))  9.9 us
  transfers between devices with their start and end apart: 3, of which 0 were waited for; matrix products, arithmetic and copies ran while one was open for 60% of the time, Pallas kernels for 0%

commit v1 on v0

v1 whole, which is shorter than its diff:
```python
import functools
import math

import jax
import jax.numpy as jnp
from jax import lax
from jax.experimental import pallas as pl
from jax.experimental.pallas import tpu as pltpu
from jax.sharding import Mesh
from jax.sharding import PartitionSpec as P

CTX = ("ctx_0", "ctx_1", "ctx_2")
SPLIT = (4, 3, 8)
LANES = 128
GROUPS = 8
STEP = 16
WINDOW = 144
BF16 = jnp.bfloat16
F32 = jnp.float32


def passed_along(block, axis, distance):
    devices = range(lax.axis_size(axis))
    route = [(i - distance, i) for i in devices if i - distance in devices]
    return lax.ppermute(block, axis, route)


def iota(shape, dim):
    return lax.broadcasted_iota(jnp.int32, shape, dim)


def channel_taps(taps_ref, out_ref, block):
    groups = taps_ref.shape[2]
    spread = iota((groups, LANES), 0) == GROUPS * block + iota((groups, LANES), 1) // 16
    spread = spread.astype(F32).astype(BF16)
    for i in range(3):
        out_ref[8 * i : 8 * i + 7, :] = jnp.dot(
            taps_ref[i], spread, preferred_element_type=F32
        )


def causal(ref, i, start, rows, taps):
    total = None
    for j in range(7):
        term = taps[8 * i + j : 8 * i + j + 1, :] * ref[i, start - j : start - j + rows, :]
        total = term if total is None else total + term
    return total.astype(BF16)


def edge_kernel(feat_ref, cot_ref, taps_ref, up_ref, down_ref, taps, raw):
    rows = feat_ref.shape[1]
    channel_taps(taps_ref, taps, pl.program_id(0))
    weights = taps[...]
    raw[0, 0:8, :] = jnp.zeros((8, LANES), F32)
    raw[0, 8:152, :] = feat_ref[0, 0:144, :].astype(F32)
    for i in (1, 2):
        raw[i, 0:144, :] = feat_ref[i, rows - 144 : rows, :].astype(F32)
    key = causal(raw, 1, 16, 128, weights).astype(F32)
    value = causal(raw, 2, 16, 128, weights).astype(F32)
    up_ref[0:128, :] = (key * value).astype(BF16)
    last = [feat_ref[i, rows - 16 : rows, :].astype(F32)[8:16] for i in range(3)]
    blank = jnp.zeros((8, LANES), F32)
    up_ref[128:160, :] = jnp.concatenate(last + [blank], axis=0).astype(BF16)
    query = causal(raw, 0, 8, 136, weights).astype(F32)
    grad = cot_ref[0:144, :].astype(F32)
    inner = grad[0:136] * query
    first = jnp.where(iota((8, LANES), 0) < 6, grad[0:8], inner[0:8])
    begin = [feat_ref[i, 0:16, :].astype(F32)[0:8] for i in range(3)]
    down_ref[...] = jnp.concatenate([first, inner[8:136]] + begin, axis=0).astype(BF16)


def local_kernel(
    feat_ref, cot_ref, taps_ref, long_ref,
    mixed_ref, product_ref, inner_ref, ahead_ref, behind_ref, taps_out, raw, filt, spread,
):
    step = pl.program_id(0)
    rows = feat_ref.shape[1]

    @pl.when(step == 0)
    def _():
        groups = long_ref.shape[0]
        flip = iota((128, 256), 0) + iota((128, 256), 1) == 128
        flip = flip.astype(F32).astype(BF16)
        filt[0] = jnp.dot(long_ref[...], flip, preferred_element_type=F32)
        filt[1, :, 0:128] = long_ref[...].astype(F32)
        filt[1, :, 128:256] = jnp.zeros((groups, 128), F32)

    taps_out[...] = jnp.zeros(taps_out.shape, F32)
    channel_taps(taps_ref, taps_out, step)
    weights = taps_out[...]
    for which, out in ((0, ahead_ref), (1, behind_ref)):
        base = filt[which, pl.ds(pl.multiple_of(GROUPS * step, GROUPS), GROUPS), :]
        for r in range(STEP):
            moved = base if r == 0 else pltpu.roll(base, r, 1)
            for half in (0, 1):
                lanes = moved[:, 128 * half : 128 * half + 128]
                spread[half, pl.ds(r, GROUPS, stride=STEP), :] = lanes
        for half in (0, 1):
            out[:, 128 * half : 128 * half + 128] = spread[half].astype(BF16)
    for i in range(3):
        raw[i, 0:8, :] = jnp.zeros((8, LANES), F32)
        raw[i, 8 : 8 + rows, :] = feat_ref[i].astype(F32)
    query, key, value = [causal(raw, i, 8, rows, weights) for i in range(3)]
    mixed_ref[0] = query
    mixed_ref[1] = key
    mixed_ref[2] = value
    product_ref[...] = (key.astype(F32) * value.astype(F32)).astype(BF16)
    inner_ref[...] = (cot_ref[...].astype(F32) * query.astype(F32)).astype(BF16)


def pick_groups(full, masks):
    total = full[0:STEP]
    for g in range(1, GROUPS):
        total = jnp.where(masks[g], full[STEP * g : STEP * g + STEP], total)
    return total


def main_kernel(
    feat_ref, cot_ref, gain_ref, mixed_ref, product_ref, inner_ref, ahead_ref, behind_ref, taps_ref,
    up_ref, down_ref,
    gated_ref, grad_ref, sums_ref,
    raw, mix, prod, ginn, gmix, cot, corr,
):
    step = pl.program_id(0)
    rows = feat_ref.shape[1]
    chunks = rows // STEP
    weights = taps_ref[...]
    gain = gain_ref[...].astype(F32)
    group_of = iota((STEP, LANES), 1) // 16
    masks = [group_of == g for g in range(GROUPS)]

    before = up_ref[128:160, :].astype(F32)
    tail = down_ref[128:160, :].astype(F32)
    for i in range(3):
        raw[i, 0:8, :] = before[8 * i : 8 * i + 8]
        raw[i, 8 : 8 + rows, :] = feat_ref[i].astype(F32)
        raw[i, 8 + rows : 16 + rows, :] = tail[8 + 8 * i : 16 + 8 * i]
    for i in range(3):
        mix[i, 8:rows, :] = mixed_ref[i].astype(F32)[8:rows]
        mix[i, 0:8, :] = causal(raw, i, 8, 8, weights).astype(F32)
        mix[i, rows : rows + 8, :] = causal(raw, i, 8 + rows, 8, weights).astype(F32)
        mix[i, rows + 8 : rows + 16, :] = jnp.zeros((8, LANES), F32)
    opening = down_ref[0:16, :].astype(F32)
    past = iota((STEP, LANES), 0) < 6
    after = jnp.where(past, opening, 0.0)
    cot[0:rows, :] = cot_ref[...].astype(F32)
    cot[rows : rows + 16, :] = after

    prod[0:128, :] = up_ref[0:128, :]
    prod[128 : 128 + rows, :] = product_ref[...]
    prod[128:144, :] = (mix[1, 0:16, :] * mix[2, 0:16, :]).astype(BF16)
    prod[128 + rows : 144 + rows, :] = (
        mix[1, rows : rows + 16, :] * mix[2, rows : rows + 16, :]
    ).astype(BF16)
    ginn[0:rows, :] = inner_ref[...]
    ginn[0:16, :] = (cot[0:16, :] * mix[0, 0:16, :]).astype(BF16)
    ginn[rows : rows + 128, :] = down_ref[0:128, :]
    ginn[rows : rows + 16, :] = jnp.where(
        past, after * mix[0, rows : rows + 16, :], opening
    ).astype(BF16)
    ginn[rows + 128 : rows + 144, :] = jnp.concatenate(
        [tail[0:8], jnp.zeros((8, LANES), F32)], axis=0
    ).astype(BF16)

    ahead = ahead_ref[:, 0:WINDOW]
    behind = behind_ref[:, 0:WINDOW]
    skip = jnp.zeros((STEP, LANES), F32)
    grid = jnp.zeros((LANES, WINDOW), F32)
    keep = [m.astype(F32).astype(BF16) for m in masks]
    for pair in range(0, chunks + 1, 2):
        own = [b for b in (pair, pair + 1) if b <= chunks]

        def windows(ref):
            parts = [ref[STEP * b : STEP * b + WINDOW, :] for b in own]
            return parts[0] if len(parts) == 1 else jnp.concatenate(parts, axis=1)

        forward = jnp.dot(ahead, windows(prod), preferred_element_type=F32)
        inn_windows = windows(ginn)
        backward = jnp.dot(behind, inn_windows, preferred_element_type=F32)
        if pair < chunks:
            pieces = [prod[128 + STEP * b : 144 + STEP * b, :] for b in own]
            left = jnp.concatenate(
                [jnp.concatenate([k * p for p in pieces], axis=1) for k in keep], axis=0
            )
            grid = grid + lax.dot_general(
                left, inn_windows, (((1,), (1,)), ((), ())), preferred_element_type=F32
            )
        for n, b in enumerate(own):
            lo, hi = STEP * b, STEP * b + STEP
            conv = pick_groups(forward[:, LANES * n : LANES * n + LANES], masks)
            back = pick_groups(backward[:, LANES * n : LANES * n + LANES], masks)
            p = prod[128 + lo : 128 + hi, :].astype(F32)
            q = ginn[lo:hi, :].astype(F32)
            inner = conv + gain * p
            gprod = (back + gain * q).astype(BF16).astype(F32)
            gmix[0, lo:hi, :] = (cot[lo:hi, :] * inner).astype(BF16).astype(F32)
            gmix[1, lo:hi, :] = (gprod * mix[2, lo:hi, :]).astype(BF16).astype(F32)
            gmix[2, lo:hi, :] = (gprod * mix[1, lo:hi, :]).astype(BF16).astype(F32)
            if b < chunks:
                gated_ref[lo:hi, :] = (mix[0, lo:hi, :] * inner).astype(BF16)
                skip = skip + p * q

    for i in range(3):
        total = None
        for j in range(7):
            term = weights[8 * i + j : 8 * i + j + 1, :] * gmix[i, j : j + rows, :]
            total = term if total is None else total + term
        grad_ref[i] = total.astype(BF16)

    lines = []
    for i in range(3):
        for j in range(7):
            both = gmix[i, 0:rows, :] * raw[i, 8 - j : 8 - j + rows, :]
            lines.append(jnp.sum(both, axis=0, keepdims=True))
        lines.append(jnp.zeros((1, LANES), F32))
    lines = jnp.concatenate(lines, axis=0)
    gather = iota((LANES, LANES), 1) == GROUPS * step + iota((LANES, LANES), 0) // 16
    gather = gather.astype(F32)
    short = jnp.dot(lines, gather, precision=lax.Precision.HIGHEST, preferred_element_type=F32)

    @pl.when(step == 0)
    def _():
        sums_ref[72:96, :] = short

    @pl.when(step > 0)
    def _():
        sums_ref[72:96, :] += short

    sums_ref[pl.ds(64 + step, 1), :] = jnp.sum(skip, axis=0, keepdims=True)
    corr[0] = grid[:, 0:128]
    corr[1, :, 0 : WINDOW - 128] = grid[:, 128:WINDOW]
    corr[1, :, WINDOW - 128 : 128] = jnp.zeros((LANES, 256 - WINDOW), F32)
    total = None
    for r in range(STEP):
        line = jnp.concatenate(
            [corr[half, pl.ds(r, GROUPS, stride=STEP), :] for half in (0, 1)], axis=1
        )
        line = line if r == 0 else pltpu.roll(line, 256 - r, 1)
        total = line[:, 0:128] if total is None else total + line[:, 0:128]
    sums_ref[pl.ds(pl.multiple_of(GROUPS * step, GROUPS), GROUPS), :] = total


def blocks3(rows):
    return pl.BlockSpec((3, rows, LANES), lambda b: (0, 0, b))


def blocks2(rows):
    return pl.BlockSpec((rows, LANES), lambda b: (0, b))


def whole(shape):
    return pl.BlockSpec(shape, lambda b: (0,) * len(shape))


def swap(values, axes):
    return lax.all_to_all(values, axes, 0, 0, tiled=True)


def summed(local):
    near, far = CTX[:2], CTX[2]
    parts = lax.axis_size(near)
    size = lax.axis_size(far)
    share = local.reshape(parts, -1, LANES)
    share = swap(share, near).sum(axis=0)
    every = jnp.broadcast_to(share[None], (size,) + share.shape)
    share = swap(every, far).sum(axis=0)
    every = jnp.broadcast_to(share[None], (parts,) + share.shape)
    return swap(every, near).reshape(local.shape)


def body(features, short_taps, long_taps, skip_gain, cotangent):
    rows, width = features.shape[1:]
    groups = width // 16
    steps = width // LANES
    shape = jax.ShapeDtypeStruct
    params = pltpu.CompilerParams(
        dimension_semantics=("arbitrary",), vmem_limit_bytes=16 * 2**20
    )
    short_taps = short_taps.transpose(0, 2, 1)
    up, down = pl.pallas_call(
        edge_kernel,
        grid=(steps,),
        in_specs=[blocks3(rows), blocks2(rows), whole((3, 7, groups))],
        out_specs=[blocks2(160), blocks2(160)],
        out_shape=[shape((160, width), BF16), shape((160, width), BF16)],
        scratch_shapes=[pltpu.VMEM((24, LANES), F32), pltpu.VMEM((3, 152, LANES), F32)],
        compiler_params=params,
        cost_estimate=pl.CostEstimate(flops=10**7, bytes_accessed=3 * 10**6, transcendentals=0),
        name="edge",
    )(features, cotangent, short_taps)
    from_last = passed_along(up, CTX, 1)
    from_next = passed_along(down, CTX, -1)
    mixed, product, inner, ahead, behind, taps = pl.pallas_call(
        local_kernel,
        grid=(steps,),
        in_specs=[
            blocks3(rows), blocks2(rows), whole((3, 7, groups)), whole((groups, 128)),
        ],
        out_specs=[
            blocks3(rows), blocks2(rows), blocks2(rows),
            pl.BlockSpec((128, 256), lambda b: (b, 0)),
            pl.BlockSpec((128, 256), lambda b: (b, 0)),
            blocks2(24),
        ],
        out_shape=[
            shape((3, rows, width), BF16), shape((rows, width), BF16), shape((rows, width), BF16),
            shape((groups * 16, 256), BF16), shape((groups * 16, 256), BF16),
            shape((24, width), F32),
        ],
        scratch_shapes=[
            pltpu.VMEM((3, rows + 8, LANES), F32),
            pltpu.VMEM((2, groups, 256), F32),
            pltpu.VMEM((2, 128, LANES), F32),
        ],
        compiler_params=params,
        cost_estimate=pl.CostEstimate(
            flops=2 * 10**7, bytes_accessed=8 * 10**6, transcendentals=0
        ),
        name="local",
    )(features, cotangent, short_taps, long_taps)
    gated, feature_grad, sums = pl.pallas_call(
        main_kernel,
        grid=(steps,),
        in_specs=[
            blocks3(rows), blocks2(rows), blocks2(1), blocks3(rows), blocks2(rows), blocks2(rows),
            pl.BlockSpec((128, 256), lambda b: (b, 0)),
            pl.BlockSpec((128, 256), lambda b: (b, 0)),
            blocks2(24), blocks2(160), blocks2(160),
        ],
        out_specs=[blocks2(rows), blocks3(rows), whole((96, LANES))],
        out_shape=[
            shape((rows, width), BF16), shape((3, rows, width), BF16), shape((96, LANES), F32),
        ],
        scratch_shapes=[
            pltpu.VMEM((3, rows + 16, LANES), F32),
            pltpu.VMEM((3, rows + 16, LANES), F32),
            pltpu.VMEM((rows + 144, LANES), BF16),
            pltpu.VMEM((rows + 144, LANES), BF16),
            pltpu.VMEM((3, rows + 16, LANES), F32),
            pltpu.VMEM((rows + 16, LANES), F32),
            pltpu.VMEM((2, 128, LANES), F32),
        ],
        compiler_params=params,
        cost_estimate=pl.CostEstimate(
            flops=10**8, bytes_accessed=10**7, transcendentals=0
        ),
        name="main",
    )(
        features, cotangent, skip_gain.reshape(1, width), mixed, product, inner, ahead, behind,
        taps, from_last, from_next,
    )
    total = summed(sums)
    tokens = rows * lax.axis_size(CTX)
    group_scale = 1.0 / math.sqrt(16.0 * tokens)
    token_scale = 1.0 / math.sqrt(1.0 * tokens)
    short = total[72:96].reshape(3, 8, LANES)[:, :7, :groups].transpose(0, 2, 1)
    return (
        gated,
        feature_grad,
        short * group_scale,
        total[:groups] * group_scale,
        total[64 : 64 + steps].reshape(width) * token_scale,
    )


def solution(mesh):
    torus = Mesh(mesh.devices.reshape(*SPLIT, mesh.shape["tp"]), CTX + ("tp",))
    return jax.shard_map(
        body,
        mesh=torus,
        in_specs=(P(None, CTX, "tp"), P(None, "tp", None), P("tp", None), P("tp"), P(CTX, "tp")),
        out_specs=(P(CTX, "tp"), P(None, CTX, "tp"), P(None, "tp", None), P("tp", None), P("tp")),
        check_vma=False,
    )
```

time: 374 us -> 81.1 us (0.22)
  local copies, waits for them, and re-layouts: 214 us -> 3.16 us
  other arithmetic: 62.9 us -> 1.84 us
  blocking collectives: 68.5 us -> 45 us
  Pallas kernels: 0 us -> 20.8 us
  matrix products: 19 us -> 0 us
  waiting for transfers between devices: 0.01 us -> 4.52 us
    gather x2 -> x0, local copies, waits for them, and re-layouts: 124 us -> none  [toeplitz_blocks(): return jnp.take(extra, picks, axis=1)]
    psum x3 -> x0, blocking collectives: 68.5 us -> none  [one_axis_at_a_time(): return functools.reduce(lax.psum, axes, shard)]
    all_to_all x0 -> x3, blocking collectives: none -> 45 us  [swap(): return lax.all_to_all(values, axes, 0, 0, tiled=True)]
    reshape x8 -> x1, local copies, waits for them, and re-layouts: 42.9 us -> 0.01 us  [body(): skip_gain.reshape(1, width)]
    convert_element_type x6 -> x0, other arithmetic: 29.8 us -> none  [the longest x1 14.9 us: body(): short_filter(wide, taps, rows + 127).astype(jnp.bfloat16)]
    pallas_call x0 -> x3, Pallas kernels: none -> 20.8 us  [the longest x1 12.8 us: body(): pl.pallas_call(main_kernel, grid=(steps,), in_specs=[blocks3(rows), block...]
    pad x2 -> x0, local copies, waits for them, and re-layouts: 19.5 us -> none  [the longest x1 9.9 us: diagonal_sums(): flat = jnp.pad(padded.reshape(groups, 128 * 382), ((0, 0), (0, 128)))]
    dot_general x6 -> x0, matrix products: 19 us -> none  [the longest x1 3.79 us: body(): jnp.einsum('gts,gns->gnt', earlier, before, preferred_element_type=jnp.fl...]
  transfers between devices with their start and end apart: 3 -> 2, of which waited for: 0 -> 2; matrix products, arithmetic and copies ran while one was open for 60% -> 0% of each run, Pallas kernels for 0% -> 6%
where the time goes in v1:
time: 81.1 us; the launch traced here: 80.7 us
  blocking collectives  45 us (55%)
  Pallas kernels  20.8 us (26%)
  starting transfers between devices  4.79 us (6%)
  waiting for transfers between devices  4.52 us (6%)
  local copies, waits for them, and re-layouts  3.16 us (4%)
  other arithmetic  1.84 us (2%)
    all_to_all x3, blocking collectives, swap(): return lax.all_to_all(values, axes, 0, 0, tiled=True)  45 us
    pallas_call x1, Pallas kernels, body(): pl.pallas_call(main_kernel, grid=(steps,), in_specs=[blocks3(rows), block...  12.8 us
    pallas_call x1, Pallas kernels, body(): pl.pallas_call(local_kernel, grid=(steps,), in_specs=[blocks3(rows), bloc...  5.21 us
    ppermute x2, starting transfers between devices, passed_along(): return lax.ppermute(block, axis, route)  4.79 us
    ppermute x2, waiting for transfers between devices, passed_along(): return lax.ppermute(block, axis, route)  4.52 us
    unnamed x10, local copies, waits for them, and re-layouts  3.14 us
    pallas_call x1, Pallas kernels, body(): pl.pallas_call(edge_kernel, grid=(steps,), in_specs=[blocks3(rows), block...  2.74 us
  transfers between devices with their start and end apart: 2, of which 2 were waited for; matrix products, arithmetic and copies ran while one was open for 0% of the time, Pallas kernels for 6%

profile of v1, /device:TPU:192, one launch (start us, length us, event | category | flops | bytes accessed | tf_op | source)
XLA Modules:
  0.0 80.7 jit_solution(10411906914622138129)
XLA Ops:
  0.6 0.0 copy-start
  0.6 1.4 %copy-done = bf16[3,256,1024]{2,1,0:T(8,128)(2,1)S(1)} copy-done((bf16[3,256,1024]{2,1,0:T(8,128)(2,1)S(1)}, bf16[3,256,1024]{2,1,0:T(8,128)(2,1)}, u32[]{:S(2)}) %copy-start) | copy-done | bytes 1572888
  2.0 0.0 copy-start.1
  2.0 1.0 %copy-done.1 = bf16[256,1024]{1,0:T(8,128)(2,1)S(1)} copy-done((bf16[256,1024]{1,0:T(8,128)(2,1)S(1)}, bf16[256,1024]{1,0:T(8,128)(2,1)}, u32[]{:S(2)}) %copy-start.1) | copy-done | bytes 524312
  3.1 0.0 copy-start.2
  3.1 0.7 copy-done.2
  3.8 0.0 copy-start.4
  3.8 0.0 copy-start.3
  3.8 2.7 %edge.1 = (bf16[160,1024]{1,0:T(8,128)(2,1)S(1)}, bf16[160,1024]{1,0:T(8,128)(2,1)S(1)}) custom-call(bf16[3,256,1024]{2,1,0:T(8,128)(2,1)S(1)} %copy-done, bf16[256,1024]{1,0:T(8,128)(2,1)S(1)} %copy-done.1, bf16[3,7,64]{2,1,0:T(8,128)(2,1)S(1)} %bitcast.9), custom_call_target="tpu_custom_call" | custom-call | flops 10000000 | bytes 3000000 | tf_op jit(solution)/shard_map/edge/pallas_call | solution.py:280
  6.5 3.5 %collective-permute-start = (bf16[160,1024]{1,0:T(8,128)(2,1)S(1)}, bf16[160,1024]{1,0:T(8,128)(2,1)S(1)}, u32[]{:S(2)}, u32[]{:S(2)}) collective-permute-start(bf16[160,1024]{1,0:T(8,128)(2,1)S(1)} %get-tuple-element.22), channel_id=1, source_target_pairs={{0,8},{8,16},{16,24},{24,32},{32,40},{40,48},{48,56},{56,64},{64,7... | collective-permute-start | bytes 983048 | tf_op jit(solution)/shard_map/ppermute | solution.py:25
  10.0 1.3 %collective-permute-start.1 = (bf16[160,1024]{1,0:T(8,128)(2,1)S(1)}, bf16[160,1024]{1,0:T(8,128)(2,1)S(1)}, u32[]{:S(2)}, u32[]{:S(2)}) collective-permute-start(bf16[160,1024]{1,0:T(8,128)(2,1)S(1)} %get-tuple-element.23), channel_id=1, source_target_pairs={{8,0},{16,8},{24,16},{32,24},{40,32},{48,40},{56,48},{64,56},{72,6... | collective-permute-start | bytes 983048 | tf_op jit(solution)/shard_map/ppermute | solution.py:25
  11.3 0.0 copy-done.4
  11.4 0.0 copy-done.3
  11.4 5.2 %local.1 = (bf16[3,256,1024]{2,1,0:T(8,128)(2,1)S(1)}, bf16[256,1024]{1,0:T(8,128)(2,1)S(1)}, bf16[256,1024]{1,0:T(8,128)(2,1)S(1)}, bf16[1024,256]{1,0:T(8,128)...) custom-call(bf16[3,256,1024]{2,1,0:T(8,128)(2,1)S(1)} %copy-done, bf16[256,1024]{1,0:T(8,128)(2,1)S(1)} %copy-done.1, ...), custom_call_target="tpu_custom_call" | custom-call | flops 20000000 | bytes 8000000 | tf_op jit(solution)/shard_map/local/pallas_call | solution.py:293
  16.6 0.4 collective-permute-done.up_ref
  17.0 4.1 %collective-permute-done.1.down_ref = bf16[160,1024]{1,0:T(8,128)(2,1)S(1)} collective-permute-done((bf16[160,1024]{1,0:T(8,128)(2,1)S(1)}, bf16[160,1024]{1,0:T(8,128)(2,1)S(1)}, u32[]{:S(2)}, u32[]{:S(2)}) %collective-permute-start.1) | collective-permute-done | bytes 327712 | tf_op jit(solution)/shard_map/ppermute | solution.py:25
  21.1 12.8 %main.1 = (bf16[256,1024]{1,0:T(8,128)(2,1)}, bf16[3,256,1024]{2,1,0:T(8,128)(2,1)}, f32[96,128]{1,0:T(8,128)S(1)}) custom-call(bf16[3,256,1024]{2,1,0:T(8,128)(2,1)S(1)} %copy-done, bf16[256,1024]{1,0:T(8,128)(2,1)S(1)} %copy-done.1, bf16[1,1024]{1,0:T(2,128)(2,1)S(1)} %reshape.30.gain_ref, bf16[3,256,1024]{2,1,0:T(8,128)(2,1)S(1)} %get-tuple-element.16.mixed_ref, ...), custom_call_target="tpu_custom_call" | custom-call | flops 100000000 | bytes 10000000 | tf_op jit(solution)/shard_map/main/pallas_call | solution.py:321
  33.9 17.6 %all_to_all.15 = f32[12,8,128]{2,1,0:T(8,128)S(1)} all-to-all(f32[12,8,128]{2,1,0:T(8,128)S(1)} %bitcast.8), channel_id=1, replica_groups=mesh['ctx_0'=4,'ctx_1'=3,'ctx_2'=8,'tp'=8] {'ctx_0','ctx_1'}, dimensions={0} | all-to-all | bytes 98304 | tf_op jit(solution)/shard_map/all_to_all | solution.py:256
  51.5 16.3 %all_to_all.16 = f32[8,8,128]{2,1,0:T(8,128)S(1)} all-to-all(f32[8,8,128]{2,1,0:T(8,128)S(1)} %broadcast_in_dim.4), channel_id=1, replica_groups=mesh['ctx_0'=4,'ctx_1'=3,'ctx_2'=8,'tp'=8] {'ctx_2'}, dimensions={0} | all-to-all | bytes 65536 | tf_op jit(solution)/shard_map/all_to_all | solution.py:256
  67.9 11.1 %all_to_all.17 = f32[12,8,128]{2,1,0:T(8,128)S(1)} all-to-all(f32[12,8,128]{2,1,0:T(8,128)S(1)} %broadcast_in_dim.5), channel_id=1, replica_groups=mesh['ctx_0'=4,'ctx_1'=3,'ctx_2'=8,'tp'=8] {'ctx_0','ctx_1'}, dimensions={0} | all-to-all | bytes 98304 | tf_op jit(solution)/shard_map/all_to_all | solution.py:256
  78.9 0.6 fusion.2
  79.5 0.6 fusion.1
  80.1 0.6 fusion
  (5 shorter events, 0.0 us)
Async XLA Ops:
  0.6 1.4 %copy-start = (bf16[3,256,1024]{2,1,0:T(8,128)(2,1)S(1)}, bf16[3,256,1024]{2,1,0:T(8,128)(2,1)}, u32[]{:S(2)}) copy-start(bf16[3,256,1024]{2,1,0:T(8,128)(2,1)} %feat_ref.5) | copy-start | bytes 4718596
  2.0 1.0 %copy-start.1 = (bf16[256,1024]{1,0:T(8,128)(2,1)S(1)}, bf16[256,1024]{1,0:T(8,128)(2,1)}, u32[]{:S(2)}) copy-start(bf16[256,1024]{1,0:T(8,128)(2,1)} %cot_ref.5) | copy-start | bytes 1572868
  3.1 0.7 copy-start.2
  3.8 7.6 %copy-start.4 = (bf16[1024]{0:T(1024)(128)(2,1)S(1)}, bf16[1024]{0:T(1024)(128)(2,1)}, u32[]{:S(2)}) copy-start(bf16[1024]{0:T(1024)(128)(2,1)} %param.8) | copy-start | bytes 6148
  3.8 7.6 %copy-start.3 = (bf16[64,128]{1,0:T(8,128)(2,1)S(1)}, bf16[64,128]{1,0:T(8,128)(2,1)}, u32[]{:S(2)}) copy-start(bf16[64,128]{1,0:T(8,128)(2,1)} %long_ref.1) | copy-start | bytes 49156
  6.5 10.4 %collective-permute-start = (bf16[160,1024]{1,0:T(8,128)(2,1)S(1)}, bf16[160,1024]{1,0:T(8,128)(2,1)S(1)}, u32[]{:S(2)}, u32[]{:S(2)}) collective-permute-start(bf16[160,1024]{1,0:T(8,128)(2,1)S(1)} %get-tuple-element.22), channel_id=1, source_target_pairs={{0,8},{8,16},{16,24},{24,32},{32,40},{40,48},{48,56},{56,64},{64,7... | collective-permute-start | bytes 983048 | tf_op jit(solution)/shard_map/ppermute | solution.py:25
  10.0 11.1 %collective-permute-start.1 = (bf16[160,1024]{1,0:T(8,128)(2,1)S(1)}, bf16[160,1024]{1,0:T(8,128)(2,1)S(1)}, u32[]{:S(2)}, u32[]{:S(2)}) collective-permute-start(bf16[160,1024]{1,0:T(8,128)(2,1)S(1)} %get-tuple-element.23), channel_id=1, source_target_pairs={{8,0},{16,8},{24,16},{32,24},{40,32},{48,40},{56,48},{64,56},{72,6... | collective-permute-start | bytes 983048 | tf_op jit(solution)/shard_map/ppermute | solution.py:25

commit v2 on v1

v2 whole, which is shorter than its diff:
```python
import functools
import math

import jax
import jax.numpy as jnp
from jax import lax
from jax.experimental import pallas as pl
from jax.experimental.pallas import tpu as pltpu
from jax.sharding import Mesh
from jax.sharding import PartitionSpec as P

CTX = ("ctx_0", "ctx_1", "ctx_2")
SPLIT = (4, 3, 8)
LANES = 128
GROUPS = 8
STEP = 16
WINDOW = 144
BF16 = jnp.bfloat16
F32 = jnp.float32
SMALL = 4 * 2**20
WIDE, NARROW = 60 * 2**20, 56 * 2**20


def passed_along(block, axis, distance):
    devices = range(lax.axis_size(axis))
    route = [(i - distance, i) for i in devices if i - distance in devices]
    return lax.ppermute(block, axis, route)


def iota(shape, dim):
    return lax.broadcasted_iota(jnp.int32, shape, dim)


def channel_taps(taps_ref, out_ref, block):
    groups = taps_ref.shape[2]
    spread = iota((groups, LANES), 0) == GROUPS * block + iota((groups, LANES), 1) // 16
    spread = spread.astype(F32).astype(BF16)
    for i in range(3):
        out_ref[8 * i : 8 * i + 7, :] = jnp.dot(
            taps_ref[i], spread, preferred_element_type=F32
        )


def causal(ref, i, start, rows, taps):
    total = None
    for j in range(7):
        term = taps[8 * i + j : 8 * i + j + 1, :] * ref[i, start - j : start - j + rows, :]
        total = term if total is None else total + term
    return total.astype(BF16)


def edge_kernel(feat_ref, cot_ref, taps_ref, up_ref, down_ref, taps, raw):
    rows = feat_ref.shape[1]
    channel_taps(taps_ref, taps, pl.program_id(0))
    weights = taps[...]
    raw[0, 0:8, :] = jnp.zeros((8, LANES), F32)
    raw[0, 8:152, :] = feat_ref[0, 0:144, :].astype(F32)
    for i in (1, 2):
        raw[i, 0:144, :] = feat_ref[i, rows - 144 : rows, :].astype(F32)
    key = causal(raw, 1, 16, 128, weights).astype(F32)
    value = causal(raw, 2, 16, 128, weights).astype(F32)
    up_ref[0:128, :] = (key * value).astype(BF16)
    last = [feat_ref[i, rows - 16 : rows, :].astype(F32)[8:16] for i in range(3)]
    blank = jnp.zeros((8, LANES), F32)
    up_ref[128:160, :] = jnp.concatenate(last + [blank], axis=0).astype(BF16)
    query = causal(raw, 0, 8, 136, weights).astype(F32)
    grad = cot_ref[0:144, :].astype(F32)
    inner = grad[0:136] * query
    first = jnp.where(iota((8, LANES), 0) < 6, grad[0:8], inner[0:8])
    begin = [feat_ref[i, 0:16, :].astype(F32)[0:8] for i in range(3)]
    down_ref[...] = jnp.concatenate([first, inner[8:136]] + begin, axis=0).astype(BF16)


def pick_groups(full, masks):
    total = full[0:STEP]
    for g in range(1, GROUPS):
        total = jnp.where(masks[g], full[STEP * g : STEP * g + STEP], total)
    return total


def group_masks():
    group_of = iota((STEP, LANES), 1) // 16
    return [group_of == g for g in range(GROUPS)]


def filtered(matrix, ref, shift, chunks, masks):
    for at in range(0, len(chunks), 2):
        own = chunks[at : at + 2]
        parts = [ref[STEP * b + shift : STEP * b + shift + WINDOW, :] for b in own]
        parts = parts[0] if len(parts) == 1 else jnp.concatenate(parts, axis=1)
        full = jnp.dot(matrix, parts, preferred_element_type=F32)
        for n, b in enumerate(own):
            yield b, pick_groups(full[:, LANES * n : LANES * n + LANES], masks)


def inside(rows):
    chunks = rows // STEP
    return list(range(9, chunks)), list(range(1, chunks - 8))


def local_kernel(
    feat_ref, cot_ref, taps_ref, long_ref, gain_ref,
    mixed_ref, product_ref, inner_ref, ahead_ref, behind_ref, taps_out, conv_ref, back_ref,
    raw, filt, spread,
):
    step = pl.program_id(0)
    rows = feat_ref.shape[1]

    @pl.when(step == 0)
    def _():
        groups = long_ref.shape[0]
        flip = iota((128, 256), 0) + iota((128, 256), 1) == 128
        flip = flip.astype(F32).astype(BF16)
        filt[0] = jnp.dot(long_ref[...], flip, preferred_element_type=F32)
        filt[1, :, 0:128] = long_ref[...].astype(F32)
        filt[1, :, 128:256] = jnp.zeros((groups, 128), F32)

    taps_out[...] = jnp.zeros(taps_out.shape, F32)
    channel_taps(taps_ref, taps_out, step)
    taps_out[7:8, :] = gain_ref[...].astype(F32)
    weights = taps_out[...]
    for which, out in ((0, ahead_ref), (1, behind_ref)):
        base = filt[which, pl.ds(pl.multiple_of(GROUPS * step, GROUPS), GROUPS), :]
        for r in range(STEP):
            moved = base if r == 0 else pltpu.roll(base, r, 1)
            for half in (0, 1):
                lanes = moved[:, 128 * half : 128 * half + 128]
                spread[which, half, pl.ds(r, GROUPS, stride=STEP), :] = lanes
        for half in (0, 1):
            out[:, 128 * half : 128 * half + 128] = spread[which, half].astype(BF16)
    for i in range(3):
        raw[i, 0:8, :] = jnp.zeros((8, LANES), F32)
        raw[i, 8 : 8 + rows, :] = feat_ref[i].astype(F32)
    size = 64
    for lo in range(0, rows, size):
        query, key, value = [causal(raw, i, 8 + lo, size, weights) for i in range(3)]
        mixed_ref[0, lo : lo + size, :] = query
        mixed_ref[1, lo : lo + size, :] = key
        mixed_ref[2, lo : lo + size, :] = value
        product_ref[lo : lo + size, :] = (key.astype(F32) * value.astype(F32)).astype(BF16)
        grad = cot_ref[lo : lo + size, :].astype(F32)
        inner_ref[lo : lo + size, :] = (grad * query.astype(F32)).astype(BF16)
    masks = group_masks()
    convs, backs = inside(rows)
    for b, conv in filtered(ahead_ref[:, 0:WINDOW], product_ref, -128, convs, masks):
        conv_ref[STEP * (b - convs[0]) : STEP * (b - convs[0]) + STEP, :] = conv
    for b, back in filtered(behind_ref[:, 0:WINDOW], inner_ref, 0, backs, masks):
        back_ref[STEP * (b - backs[0]) : STEP * (b - backs[0]) + STEP, :] = back


def corr_kernel(
    feat_ref, cot_ref, mixed_ref, product_ref, inner_ref, taps_ref, up_ref, down_ref,
    prod, ginn, edges_ref, sums_ref, raw, corr,
):
    rows = feat_ref.shape[1]
    chunks = rows // STEP
    weights = taps_ref[...]
    masks = group_masks()
    before = up_ref[128:160, :].astype(F32)
    tail = down_ref[128:160, :].astype(F32)
    start, end = [], []
    for i in range(3):
        raw[i, 0:8, :] = before[8 * i : 8 * i + 8]
        raw[i, 8:24, :] = feat_ref[i, 0:16, :].astype(F32)
        raw[i, 24:40, :] = feat_ref[i, rows - 16 : rows, :].astype(F32)
        raw[i, 40:48, :] = tail[8 + 8 * i : 16 + 8 * i]
        first = causal(raw, i, 8, 8, weights).astype(F32)
        start.append(jnp.concatenate([first, mixed_ref[i, 0:16, :].astype(F32)[8:16]], axis=0))
        past_end = causal(raw, i, 40, 8, weights).astype(F32)
        end.append(jnp.concatenate([past_end, jnp.zeros((8, LANES), F32)], axis=0))
        edges_ref[i, 0:16, :] = start[i].astype(BF16)
        edges_ref[i, 16:32, :] = end[i].astype(BF16)
    opening = down_ref[0:16, :].astype(F32)
    past = iota((STEP, LANES), 0) < 6
    after = jnp.where(past, opening, 0.0)
    edges_ref[3, 0:16, :] = cot_ref[0:16, :]
    edges_ref[3, 16:32, :] = after.astype(BF16)

    prod[0:128, :] = up_ref[0:128, :]
    prod[128:144, :] = (start[1] * start[2]).astype(BF16)
    prod[144 : 128 + rows, :] = product_ref[16:rows, :]
    prod[128 + rows : 144 + rows, :] = (end[1] * end[2]).astype(BF16)
    ginn[0:16, :] = (cot_ref[0:16, :].astype(F32) * start[0]).astype(BF16)
    ginn[16:rows, :] = inner_ref[16:rows, :]
    ginn[rows : rows + 16, :] = jnp.where(past, after * end[0], opening).astype(BF16)
    ginn[rows + 16 : rows + 128, :] = down_ref[16:128, :]
    ginn[rows + 128 : rows + 144, :] = jnp.concatenate(
        [tail[0:8], jnp.zeros((8, LANES), F32)], axis=0
    ).astype(BF16)

    skip = jnp.zeros((STEP, LANES), F32)
    grid = jnp.zeros((LANES, WINDOW), F32)
    keep = [m.astype(F32).astype(BF16) for m in masks]
    for pair in range(0, chunks, 2):
        lo = STEP * pair
        pieces = [prod[128 + lo : 144 + lo, :], prod[144 + lo : 160 + lo, :]]
        right = jnp.concatenate(
            [ginn[lo : lo + WINDOW, :], ginn[lo + STEP : lo + STEP + WINDOW, :]], axis=1
        )
        left = jnp.concatenate(
            [jnp.concatenate([k * p for p in pieces], axis=1) for k in keep], axis=0
        )
        grid = grid + lax.dot_general(
            left, right, (((1,), (1,)), ((), ())), preferred_element_type=F32
        )
        for n, piece in enumerate(pieces):
            at = lo + STEP * n
            skip = skip + piece.astype(F32) * ginn[at : at + STEP, :].astype(F32)
    corr[0] = grid[:, 0:128]
    corr[1, :, 0 : WINDOW - 128] = grid[:, 128:WINDOW]
    corr[1, :, WINDOW - 128 : 128] = jnp.zeros((LANES, 256 - WINDOW), F32)
    total = None
    for r in range(STEP):
        line = jnp.concatenate(
            [corr[half, pl.ds(r, GROUPS, stride=STEP), :] for half in (0, 1)], axis=1
        )
        line = line if r == 0 else pltpu.roll(line, 256 - r, 1)
        total = line[:, 0:128] if total is None else total + line[:, 0:128]
    sums_ref[0, 0:8, :] = total
    sums_ref[0, 8:16, :] = jnp.broadcast_to(jnp.sum(skip, axis=0, keepdims=True), (8, LANES))


def main_kernel(
    feat_ref, cot_ref, taps_ref, mixed_ref, prod, ginn, edges_ref, ahead_ref, behind_ref,
    conv_ref, back_ref,
    gated_ref, gmix_ref, short_ref,
    gmix,
):
    step = pl.program_id(0)
    rows = feat_ref.shape[1]
    chunks = rows // STEP
    gain = taps_ref[7:8, :]
    masks = group_masks()

    def mixed(i, b):
        if b == 0 or b == chunks:
            return edges_ref[i, STEP * (b > 0) : STEP * (b > 0) + STEP, :].astype(F32)
        if i == 3:
            return cot_ref[STEP * b : STEP * b + STEP, :].astype(F32)
        return mixed_ref[i, STEP * b : STEP * b + STEP, :].astype(F32)

    def keep(i, b, values):
        values = values.astype(BF16)
        gmix_ref[i, STEP * b : STEP * b + STEP, :] = values
        gmix[i, STEP * b : STEP * b + STEP, :] = values.astype(F32)

    def with_conv(b, conv):
        inner = conv + gain * prod[128 + STEP * b : 144 + STEP * b, :].astype(F32)
        keep(0, b, mixed(3, b) * inner)
        if b < chunks:
            gated_ref[STEP * b : STEP * b + STEP, :] = (mixed(0, b) * inner).astype(BF16)

    def with_back(b, back):
        grad = back + gain * ginn[STEP * b : STEP * b + STEP, :].astype(F32)
        grad = grad.astype(BF16).astype(F32)
        keep(1, b, grad * mixed(2, b))
        keep(2, b, grad * mixed(1, b))

    convs, backs = inside(rows)
    everything = range(chunks + 1)
    outer = [b for b in everything if b not in convs]
    for b, conv in filtered(ahead_ref[:, 0:WINDOW], prod, 0, outer, masks):
        with_conv(b, conv)
    for b in convs:
        with_conv(b, conv_ref[STEP * (b - convs[0]) : STEP * (b - convs[0]) + STEP, :])
    outer = [b for b in everything if b not in backs]
    for b, back in filtered(behind_ref[:, 0:WINDOW], ginn, 0, outer, masks):
        with_back(b, back)
    for b in backs:
        with_back(b, back_ref[STEP * (b - backs[0]) : STEP * (b - backs[0]) + STEP, :])

    size = 64
    lines = []
    for i in range(3):
        totals = [None] * 7
        for lo in range(0, rows, size):
            own = feat_ref[i, lo : lo + size, :].astype(F32)
            for j in range(7):
                both = gmix[i, lo + j : lo + j + size, :] * own
                both = both.reshape(size // 8, 8, LANES).sum(axis=0)
                totals[j] = both if totals[j] is None else totals[j] + both
        lines += [jnp.sum(total, axis=0, keepdims=True) for total in totals]
        lines.append(jnp.zeros((1, LANES), F32))
    group = GROUPS * step + iota((LANES, LANES), 0) // 16
    lane = iota((LANES, LANES), 1)
    short = None
    for part, shift in ((lines[0:16], 0), (lines[16:24] + [jnp.zeros((8, LANES), F32)], 64)):
        gather = (lane == group + shift).astype(F32)
        term = jnp.dot(
            jnp.concatenate(part, axis=0), gather,
            precision=lax.Precision.HIGHEST, preferred_element_type=F32,
        )
        short = term if short is None else short + term

    @pl.when(step == 0)
    def _():
        short_ref[...] = short

    @pl.when(step > 0)
    def _():
        short_ref[...] += short


def feature_kernel(gmix_ref, taps_ref, out_ref, wide):
    rows = out_ref.shape[1]
    weights = taps_ref[...]
    size = 64
    for i in range(3):
        wide[i] = gmix_ref[i].astype(F32)
    for i in range(3):
        for lo in range(0, rows, size):
            total = None
            for j in range(7):
                term = weights[8 * i + j : 8 * i + j + 1, :] * wide[i, lo + j : lo + j + size, :]
                total = term if total is None else total + term
            out_ref[i, lo : lo + size, :] = total.astype(BF16)


def join_kernel(long_ref, short_ref, out_ref):
    share = jnp.sum(long_ref[...], axis=0)
    long, skip = share[0:8], share[8:16]
    row = iota((8, LANES), 0)
    upper = iota((8, LANES), 1) >= 64
    swapped = pltpu.roll(skip, 64, 1)
    skip = jnp.where(row == 0, swapped, skip)
    low = jnp.where(upper & (row < 2), skip, short_ref[8:16, :])
    for n in range(out_ref.shape[0]):
        out_ref[n, 0:8, :] = short_ref[0:8, :]
        out_ref[n, 8:16, :] = low
        out_ref[n, 16:24, :] = long


def spread_kernel(in_ref, out_ref):
    total = jnp.sum(in_ref[...], axis=0)
    for n in range(out_ref.shape[0]):
        out_ref[n] = total


def final_kernel(group_scale, token_scale, in_ref, short_ref, long_ref, skip_ref):
    values = in_ref[...]
    sent = values.shape[0]
    short = jnp.sum(values[:, 0:16, :], axis=0)
    groups = short_ref.shape[2]
    moved = pltpu.roll(short, 64, 1)
    short_ref[0] = short[0:7, 0:groups] * group_scale
    short_ref[1] = short[8:15, 0:groups] * group_scale
    short_ref[2] = moved[0:7, 0:groups] * group_scale
    upper = iota((1, LANES), 1) >= 64
    for n in range(sent):
        long_ref[8 * n : 8 * n + 8, :] = values[n, 16:24, :] * group_scale
        pair = values[n, 8:16, :]
        turned = pltpu.roll(pair, 64, 1)
        skip_ref[n : n + 1, :] = jnp.where(upper, pair[1:2], turned[0:1]) * token_scale


def blocks3(rows):
    return pl.BlockSpec((3, rows, LANES), lambda b: (0, 0, b))


def blocks2(rows):
    return pl.BlockSpec((rows, LANES), lambda b: (0, b))


def whole(shape):
    return pl.BlockSpec(shape, lambda b: (0,) * len(shape))


def swap(values, axes):
    return lax.all_to_all(values, axes, 0, 0, tiled=True)


def body(features, short_taps, long_taps, skip_gain, cotangent):
    rows, width = features.shape[1:]
    groups = width // 16
    steps = width // LANES
    near, far = CTX[:2], CTX[2]
    shape = jax.ShapeDtypeStruct
    short_taps = short_taps.transpose(0, 2, 1)

    def call(kernel, name, ins, outs, scratch, bytes_accessed, limit=WIDE, grid=(steps,)):
        return pl.pallas_call(
            kernel,
            grid=grid,
            in_specs=ins,
            out_specs=[spec for spec, _ in outs],
            out_shape=[out for _, out in outs],
            scratch_shapes=scratch,
            compiler_params=pltpu.CompilerParams(
                dimension_semantics=("arbitrary",) * len(grid), vmem_limit_bytes=limit
            ),
            cost_estimate=pl.CostEstimate(
                flops=bytes_accessed, bytes_accessed=bytes_accessed, transcendentals=0
            ),
            name=name,
        )

    up, down = call(
        edge_kernel,
        "edge",
        [blocks3(rows), blocks2(rows), whole((3, 7, groups))],
        [
            (blocks2(160), shape((160, width), BF16)),
            (blocks2(160), shape((160, width), BF16)),
        ],
        [pltpu.VMEM((24, LANES), F32), pltpu.VMEM((3, 152, LANES), F32)],
        5 * 10**6,
    )(features, cotangent, short_taps)
    from_last = passed_along(up, CTX, 1)
    from_next = passed_along(down, CTX, -1)
    matrix = pl.BlockSpec((128, 256), lambda b: (b, 0))
    convs, backs = inside(rows)
    near_conv, near_back = STEP * len(convs), STEP * len(backs)
    mixed, product, inner, ahead, behind, taps, conv, back = call(
        local_kernel,
        "local",
        [
            blocks3(rows), blocks2(rows), whole((3, 7, groups)), whole((groups, 128)), blocks2(1),
        ],
        [
            (blocks3(rows), shape((3, rows, width), BF16)),
            (blocks2(rows), shape((rows, width), BF16)),
            (blocks2(rows), shape((rows, width), BF16)),
            (matrix, shape((groups * 16, 256), BF16)),
            (matrix, shape((groups * 16, 256), BF16)),
            (blocks2(24), shape((24, width), F32)),
            (blocks2(near_conv), shape((near_conv, width), F32)),
            (blocks2(near_back), shape((near_back, width), F32)),
        ],
        [
            pltpu.VMEM((3, rows + 8, LANES), F32),
            pltpu.VMEM((2, groups, 256), F32),
            pltpu.VMEM((2, 2, 128, LANES), F32),
        ],
        2 * 10**7,
    )(features, cotangent, short_taps, long_taps, skip_gain.reshape(1, width))
    prod, ginn, edges, sums = call(
        corr_kernel,
        "corr",
        [
            blocks3(rows), blocks2(rows), blocks3(rows), blocks2(rows), blocks2(rows), blocks2(24),
            blocks2(160), blocks2(160),
        ],
        [
            (blocks2(rows + 144), shape((rows + 144, width), BF16)),
            (blocks2(rows + 144), shape((rows + 144, width), BF16)),
            (pl.BlockSpec((4, 32, LANES), lambda b: (0, 0, b)), shape((4, 32, width), BF16)),
            (pl.BlockSpec((1, 16, LANES), lambda b: (b, 0, 0)), shape((steps, 16, LANES), F32)),
        ],
        [pltpu.VMEM((3, 48, LANES), F32), pltpu.VMEM((2, 128, LANES), F32)],
        10**7,
        NARROW,
    )(features, cotangent, mixed, product, inner, taps, from_last, from_next)
    sums = swap(sums, far)
    gated, gmix, short = call(
        main_kernel,
        "main",
        [
            blocks3(rows), blocks2(rows), blocks2(24), blocks3(rows), blocks2(rows + 144),
            blocks2(rows + 144), pl.BlockSpec((4, 32, LANES), lambda b: (0, 0, b)), matrix, matrix,
            blocks2(near_conv), blocks2(near_back),
        ],
        [
            (blocks2(rows), shape((rows, width), BF16)),
            (blocks3(rows + 16), shape((3, rows + 16, width), BF16)),
            (whole((16, LANES)), shape((16, LANES), F32)),
        ],
        [pltpu.VMEM((3, rows + 16, LANES), F32)],
        2 * 10**7,
    )(
        features, cotangent, taps, mixed, prod, ginn, edges, ahead, behind, conv, back,
    )
    parts = lax.axis_size(near)
    size = lax.axis_size(far)
    (joined,) = call(
        join_kernel,
        "join",
        [whole((size, 16, LANES)), whole((16, LANES))],
        [(whole((parts, 24, LANES)), shape((parts, 24, LANES), F32))],
        [],
        10**5,
        SMALL,
        grid=(1,),
    )(sums, short)
    joined = swap(joined, near)
    (feature_grad,) = call(
        feature_kernel,
        "features",
        [blocks3(rows + 16), blocks2(24)],
        [(blocks3(rows), shape((3, rows, width), BF16))],
        [pltpu.VMEM((3, rows + 16, LANES), F32)],
        10**7,
    )(gmix, taps)
    (every,) = call(
        spread_kernel,
        "spread",
        [whole((parts, 24, LANES))],
        [(whole((size, 24, LANES)), shape((size, 24, LANES), F32))],
        [],
        10**5,
        SMALL,
        grid=(1,),
    )(joined)
    every = swap(every, far)
    tokens = rows * lax.axis_size(CTX)
    group_scale = 1.0 / math.sqrt(16.0 * tokens)
    token_scale = 1.0 / math.sqrt(1.0 * tokens)
    short, long, skip = call(
        functools.partial(final_kernel, group_scale, token_scale),
        "final",
        [whole((size, 24, LANES))],
        [
            (whole((3, 7, groups)), shape((3, 7, groups), F32)),
            (whole((groups, LANES)), shape((groups, LANES), F32)),
            (whole((steps, LANES)), shape((steps, LANES), F32)),
        ],
        [],
        10**5,
        SMALL,
        grid=(1,),
    )(every)
    return gated, feature_grad, short.transpose(0, 2, 1), long, skip.reshape(width)


def solution(mesh):
    torus = Mesh(mesh.devices.reshape(*SPLIT, mesh.shape["tp"]), CTX + ("tp",))
    return jax.shard_map(
        body,
        mesh=torus,
        in_specs=(P(None, CTX, "tp"), P(None, "tp", None), P("tp", None), P("tp"), P(CTX, "tp")),
        out_specs=(P(CTX, "tp"), P(None, CTX, "tp"), P(None, "tp", None), P("tp", None), P("tp")),
        check_vma=False,
    )
```

time: 81.1 us -> 86.1 us (1.062)
  blocking collectives: 45 us -> 17.4 us
  Pallas kernels: 20.8 us -> 39.8 us
  starting transfers between devices: 4.79 us -> 21.3 us
  other arithmetic: 1.84 us -> 0 us
  local copies, waits for them, and re-layouts: 3.16 us -> 2.01 us
    all_to_all x3 -> x1, blocking collectives: 45 us -> 17.4 us  [swap(): return lax.all_to_all(values, axes, 0, 0, tiled=True)]
    pallas_call x3 -> x8, Pallas kernels: 20.8 us -> 39.8 us  [the longest x1 10.3 us: body(): call(main_kernel, 'main', [blocks3(rows), blocks2(rows), blocks2(24), blo...]
    all_to_all x0 -> x2, starting transfers between devices: none -> 16.5 us  [swap(): return lax.all_to_all(values, axes, 0, 0, tiled=True)]
    ppermute x2, waiting for transfers between devices: 4.52 us -> 1.23 us  [passed_along(): return lax.ppermute(block, axis, route)]
    all_to_all x0 -> x2, waiting for transfers between devices: none -> 2.6 us  [swap(): return lax.all_to_all(values, axes, 0, 0, tiled=True)]
    mul x3 -> x0, other arithmetic: 1.81 us -> none  [the longest x1 0.62 us: body(): total[:groups] * group_scale]
    unnamed x10 -> x8, local copies, waits for them, and re-layouts: 3.14 us -> 1.42 us
  transfers between devices with their start and end apart: 2 -> 4, of which waited for: 2 -> 2; matrix products, arithmetic and copies ran while one was open for 0% -> 1% of each run, Pallas kernels for 6% -> 29%
where the time goes in v2:
time: 86.1 us; the launch traced here: 85 us
  Pallas kernels  39.8 us (46%)
  starting transfers between devices  21.3 us (25%)
  blocking collectives  17.4 us (20%)
  waiting for transfers between devices  3.83 us (4%)
  local copies, waits for them, and re-layouts  2.01 us (2%)
    all_to_all x1, blocking collectives, swap(): return lax.all_to_all(values, axes, 0, 0, tiled=True)  17.4 us
    all_to_all x2, starting transfers between devices, swap(): return lax.all_to_all(values, axes, 0, 0, tiled=True)  16.5 us
    pallas_call x1, Pallas kernels, body(): call(main_kernel, 'main', [blocks3(rows), blocks2(rows), blocks2(24), blo...  10.3 us
    pallas_call x1, Pallas kernels, body(): call(local_kernel, 'local', [blocks3(rows), blocks2(rows), whole((3, 7, g...  8.13 us
    pallas_call x1, Pallas kernels, body(): call(corr_kernel, 'corr', [blocks3(rows), blocks2(rows), blocks3(rows), b...  7.71 us
    pallas_call x1, Pallas kernels, body(): call(feature_kernel, 'features', [blocks3(rows + 16), blocks2(24)], [(blo...  6.13 us
    pallas_call x1, Pallas kernels, body(): call(edge_kernel, 'edge', [blocks3(rows), blocks2(rows), whole((3, 7, gro...  6.12 us
    ppermute x2, starting transfers between devices, passed_along(): return lax.ppermute(block, axis, route)  4.78 us
  transfers between devices with their start and end apart: 4, of which 2 were waited for; matrix products, arithmetic and copies ran while one was open for 1% of the time, Pallas kernels for 29%

profile of v2, /device:TPU:192, one launch (start us, length us, event | category | flops | bytes accessed | tf_op | source)
XLA Modules:
  0.0 85.0 jit_solution(852527568383719370)
XLA Ops:
  0.6 0.0 copy-start.3
  0.6 6.1 %edge.1 = (bf16[160,1024]{1,0:T(8,128)(2,1)}, bf16[160,1024]{1,0:T(8,128)(2,1)}) custom-call(bf16[3,256,1024]{2,1,0:T(8,128)(2,1)} %feat_ref.7, bf16[256,1024]{1,0:T(8,128)(2,1)} %cot_ref.7, bf16[3,7,64]{2,1,0:T(8,128)(2,1)} %bitcast.3), custom_call_target="tpu_custom_call" | custom-call | flops 5000000 | bytes 5000000 | tf_op jit(solution)/shard_map/edge/pallas_call | solution.py:397
  6.8 3.5 %collective-permute-start = (bf16[160,1024]{1,0:T(8,128)(2,1)}, bf16[160,1024]{1,0:T(8,128)(2,1)S(1)}, u32[]{:S(2)}, u32[]{:S(2)}) collective-permute-start(bf16[160,1024]{1,0:T(8,128)(2,1)} %get-tuple-element.29), channel_id=1, source_target_pairs={{0,8},{8,16},{16,24},{24,32},{32,40},{40,48},{48,56},{56,64},{64,7... | collective-permute-start | bytes 983048 | tf_op jit(solution)/shard_map/ppermute | solution.py:27
  10.3 1.3 %collective-permute-start.1 = (bf16[160,1024]{1,0:T(8,128)(2,1)}, bf16[160,1024]{1,0:T(8,128)(2,1)S(1)}, u32[]{:S(2)}, u32[]{:S(2)}) collective-permute-start(bf16[160,1024]{1,0:T(8,128)(2,1)} %get-tuple-element.30), channel_id=1, source_target_pairs={{8,0},{16,8},{24,16},{32,24},{40,32},{48,40},{56,48},{64,56},{72,6... | collective-permute-start | bytes 983048 | tf_op jit(solution)/shard_map/ppermute | solution.py:27
  11.6 0.0 copy-done.3
  11.6 0.6 reshape.16.gain_ref
  12.2 8.1 %local.1 = (bf16[3,256,1024]{2,1,0:T(8,128)(2,1)}, bf16[256,1024]{1,0:T(8,128)(2,1)}, bf16[256,1024]{1,0:T(8,128)(2,1)}, bf16[1024,256]{1,0:T(8,128)(2,1)}, bf16...) custom-call(bf16[3,256,1024]{2,1,0:T(8,128)(2,1)} %feat_ref.7, ...), custom_call_target="tpu_custom_call" | custom-call | flops 20000000 | bytes 20000000 | tf_op jit(solution)/shard_map/local/pallas_call | solution.py:413
  20.3 0.0 collective-permute-done.up_ref
  20.3 0.0 copy-start.1
  20.3 1.2 %collective-permute-done.1.down_ref = bf16[160,1024]{1,0:T(8,128)(2,1)S(1)} collective-permute-done((bf16[160,1024]{1,0:T(8,128)(2,1)}, bf16[160,1024]{1,0:T(8,128)(2,1)S(1)}, u32[]{:S(2)}, u32[]{:S(2)}) %collective-permute-start.1) | collective-permute-done | bytes 327712 | tf_op jit(solution)/shard_map/ppermute | solution.py:27
  21.5 0.0 copy-start.2
  21.5 0.0 copy-done.1
  21.5 0.7 copy-done.2
  22.3 7.7 %corr.1 = (bf16[400,1024]{1,0:T(8,128)(2,1)}, bf16[400,1024]{1,0:T(8,128)(2,1)}, bf16[4,32,1024]{2,1,0:T(8,128)(2,1)}, f32[8,16,128]{2,1,0:T(8,128)}) custom-call(bf16[3,256,1024]{2,1,0:T(8,128)(2,1)} %feat_ref.7, bf16[256,1024]{1,0:T(8,128)(2,1)} %cot_ref.7, bf16[3,256,1024]{2,1,0:T(8,128)(2,1)} %get-tuple-element.26.mixed_ref, ...), custom_call_target="tpu_custom_call" | custom-call | flops 10000000 | bytes 10000000 | tf_op jit(solution)/shard_map/corr/pallas_call | solution.py:436
  30.0 9.3 %all-to-all-start = ((f32[8,16,128]{2,1,0:T(8,128)}), f32[8,16,128]{2,1,0:T(8,128)S(1)}, u32[]{:S(2)}, u32[]{:S(2)}) async-start(f32[8,16,128]{2,1,0:T(8,128)} %get-tuple-element.40), calls=%async_computation | async-start | bytes 131072 | tf_op jit(solution)/shard_map/all_to_all | solution.py:369
  39.2 10.3 %main.1 = (bf16[256,1024]{1,0:T(8,128)(2,1)}, bf16[3,272,1024]{2,1,0:T(8,128)(2,1)}, f32[16,128]{1,0:T(8,128)}) custom-call(bf16[3,256,1024]{2,1,0:T(8,128)(2,1)} %feat_ref.7, bf16[256,1024]{1,0:T(8,128)(2,1)} %cot_ref.7, f32[24,1024]{1,0:T(8,128)} %get-tuple-element.25.taps_ref, bf16[3,256,1024]{2,1,0:T(8,128)(2,1)} %get-tuple-element.26.mixed_ref, ...), custom_call_target="tpu_custom_call" | custom-call | flops 20000000 | bytes 20000000 | tf_op jit(solution)/shard_map/main/pallas_call | solution.py:454
  49.5 0.0 all-to-all-done.long_ref
  49.5 0.0 copy-start
  49.6 0.7 copy-done
  50.2 0.1 join.1
  50.3 17.4 %all_to_all.15.in_ref = f32[12,24,128]{2,1,0:T(8,128)S(1)} all-to-all(f32[12,24,128]{2,1,0:T(8,128)S(1)} %join.1), channel_id=1, replica_groups=mesh['ctx_0'=4,'ctx_1'=3,'ctx_2'=8,'tp'=8] {'ctx_0','ctx_1'}, dimensions={0} | all-to-all | bytes 294912 | tf_op jit(solution)/shard_map/all_to_all | solution.py:369
  67.7 0.7 spread.1
  68.4 7.2 %all-to-all-start.2 = ((f32[8,24,128]{2,1,0:T(8,128)}), f32[8,24,128]{2,1,0:T(8,128)S(1)}, u32[]{:S(2)}, u32[]{:S(2)}) async-start(f32[8,24,128]{2,1,0:T(8,128)} %spread.1), calls=%async_computation.2 | async-start | bytes 196608 | tf_op jit(solution)/shard_map/all_to_all | solution.py:369
  75.6 6.1 %features.1 = bf16[3,256,1024]{2,1,0:T(8,128)(2,1)} custom-call(bf16[3,272,1024]{2,1,0:T(8,128)(2,1)} %get-tuple-element.39.gmix_ref, f32[24,1024]{1,0:T(8,128)} %get-tuple-element.25.taps_ref), custom_call_target="tpu_custom_call" | custom-call | flops 10000000 | bytes 10000000 | tf_op jit(solution)/shard_map/features/pallas_call | solution.py:485
  81.7 2.6 %all-to-all-done.2.in_ref = f32[8,24,128]{2,1,0:T(8,128)S(1)} async-done(((f32[8,24,128]{2,1,0:T(8,128)}), f32[8,24,128]{2,1,0:T(8,128)S(1)}, u32[]{:S(2)}, u32[]{:S(2)}) %all-to-all-start.2) | async-done | bytes 98336 | tf_op jit(solution)/shard_map/all_to_all | solution.py:369
  84.3 0.7 final.1
Async XLA Ops:
  0.6 10.9 %copy-start.3 = (bf16[1024]{0:T(1024)(128)(2,1)S(1)}, bf16[1024]{0:T(1024)(128)(2,1)}, u32[]{:S(2)}) copy-start(bf16[1024]{0:T(1024)(128)(2,1)} %param.8) | copy-start | bytes 6148
  6.8 13.5 %collective-permute-start = (bf16[160,1024]{1,0:T(8,128)(2,1)}, bf16[160,1024]{1,0:T(8,128)(2,1)S(1)}, u32[]{:S(2)}, u32[]{:S(2)}) collective-permute-start(bf16[160,1024]{1,0:T(8,128)(2,1)} %get-tuple-element.29), channel_id=1, source_target_pairs={{0,8},{8,16},{16,24},{24,32},{32,40},{40,48},{48,56},{56,64},{64,7... | collective-permute-start | bytes 983048 | tf_op jit(solution)/shard_map/ppermute | solution.py:27
  10.3 11.3 %collective-permute-start.1 = (bf16[160,1024]{1,0:T(8,128)(2,1)}, bf16[160,1024]{1,0:T(8,128)(2,1)S(1)}, u32[]{:S(2)}, u32[]{:S(2)}) collective-permute-start(bf16[160,1024]{1,0:T(8,128)(2,1)} %get-tuple-element.30), channel_id=1, source_target_pairs={{8,0},{16,8},{24,16},{32,24},{40,32},{48,40},{56,48},{64,56},{72,6... | collective-permute-start | bytes 983048 | tf_op jit(solution)/shard_map/ppermute | solution.py:27
  20.3 1.2 %copy-start.1 = (bf16[160,1024]{1,0:T(8,128)(2,1)}, bf16[160,1024]{1,0:T(8,128)(2,1)S(1)}, u32[]{:S(2)}) copy-start(bf16[160,1024]{1,0:T(8,128)(2,1)S(1)} %collective-permute-done.up_ref) | copy-start | bytes 983044
  21.5 0.7 copy-start.2
  30.0 19.6 %all-to-all-start = ((f32[8,16,128]{2,1,0:T(8,128)}), f32[8,16,128]{2,1,0:T(8,128)S(1)}, u32[]{:S(2)}, u32[]{:S(2)}) async-start(f32[8,16,128]{2,1,0:T(8,128)} %get-tuple-element.40), calls=%async_computation | async-start | bytes 131072 | tf_op jit(solution)/shard_map/all_to_all | solution.py:369
  49.5 0.7 copy-start
  68.4 15.9 %all-to-all-start.2 = ((f32[8,24,128]{2,1,0:T(8,128)}), f32[8,24,128]{2,1,0:T(8,128)S(1)}, u32[]{:S(2)}, u32[]{:S(2)}) async-start(f32[8,24,128]{2,1,0:T(8,128)} %spread.1), calls=%async_computation.2 | async-start | bytes 196608 | tf_op jit(solution)/shard_map/all_to_all | solution.py:369

commit v3 on v0

v3 whole, which is shorter than its diff:
```python
import functools
import math

import jax
import jax.numpy as jnp
from jax import lax
from jax.experimental import pallas as pl
from jax.experimental.pallas import tpu as pltpu
from jax.sharding import Mesh
from jax.sharding import PartitionSpec as P

CTX = ("ctx_0", "ctx_1", "ctx_2")
SPLIT = (4, 3, 8)
LANES = 128
GROUPS = 8
STEP = 16
WINDOW = 144
BF16 = jnp.bfloat16
F32 = jnp.float32
LIMIT = 16 * 2**20
EDGE_LIMIT = 60000 * 2**10


def passed_along(block, axis, distance):
    devices = range(lax.axis_size(axis))
    route = [(i - distance, i) for i in devices if i - distance in devices]
    return lax.ppermute(block, axis, route)


def iota(shape, dim):
    return lax.broadcasted_iota(jnp.int32, shape, dim)


def lanes_of(step):
    return pl.ds(pl.multiple_of(LANES * step, LANES), LANES)


def channel_taps(taps_ref, out_ref, block):
    groups = taps_ref.shape[2]
    spread = iota((groups, LANES), 0) == GROUPS * block + iota((groups, LANES), 1) // 16
    spread = spread.astype(F32).astype(BF16)
    for i in range(3):
        out_ref[8 * i : 8 * i + 7, :] = jnp.dot(
            taps_ref[i], spread, preferred_element_type=F32
        )


def causal(ref, i, start, rows, taps):
    total = None
    for j in range(7):
        term = taps[8 * i + j : 8 * i + j + 1, :] * ref[i, start - j : start - j + rows, :]
        total = term if total is None else total + term
    return total.astype(BF16)


def pick_groups(full, masks):
    total = full[0:STEP]
    for g in range(1, GROUPS):
        total = jnp.where(masks[g], full[STEP * g : STEP * g + STEP], total)
    return total


def group_masks():
    group_of = iota((STEP, LANES), 1) // 16
    return [group_of == g for g in range(GROUPS)]


def filtered(matrix, ref, shift, chunks, masks, lanes):
    for at in range(0, len(chunks), 2):
        own = chunks[at : at + 2]
        parts = [ref[STEP * b + shift : STEP * b + shift + WINDOW, lanes] for b in own]
        parts = parts[0] if len(parts) == 1 else jnp.concatenate(parts, axis=1)
        full = jnp.dot(matrix, parts, preferred_element_type=F32)
        for n, b in enumerate(own):
            yield b, pick_groups(full[:, LANES * n : LANES * n + LANES], masks)


def inside(rows):
    chunks = rows // STEP
    return list(range(9, chunks)), list(range(1, chunks - 8))


def correlated(grid, products, inners, chunks, keep):
    for at in range(0, len(chunks), 2):
        own = chunks[at : at + 2]
        pieces = [products(b) for b in own]
        windows = [inners(b) for b in own]
        right = windows[0] if len(own) == 1 else jnp.concatenate(windows, axis=1)
        left = []
        for k in keep:
            masked = [k * p for p in pieces]
            left.append(masked[0] if len(own) == 1 else jnp.concatenate(masked, axis=1))
        term = lax.dot_general(
            jnp.concatenate(left, axis=0), right, (((1,), (1,)), ((), ())),
            preferred_element_type=F32,
        )
        grid = term if grid is None else grid + term
    return grid


def short_pass(gmix, i, own, weights, totals, lo, size):
    grad = None
    for j in range(7):
        moved = gmix[i, lo + j : lo + j + size, :]
        term = weights[8 * i + j : 8 * i + j + 1, :] * moved
        grad = term if grad is None else grad + term
        both = (moved * own).reshape(size // 8, 8, LANES).sum(axis=0)
        totals[j] = both if totals[j] is None else totals[j] + both
    return grad.astype(BF16)


def settled(rows):
    return [rows - 112, 16, 16]


def edge_kernel(
    feat_hbm, cot_hbm, taps_hbm, up_ref, down_ref, taps, opens, closes, cot_ref, taps_ref, raw, sems,
):
    rows = cot_hbm.shape[0]
    pairs = [
        (taps_hbm, taps_ref),
        (feat_hbm.at[1, rows - 144 : rows], closes.at[1]),
        (feat_hbm.at[2, rows - 144 : rows], closes.at[2]),
        (feat_hbm.at[0, 0:144], opens.at[0]),
        (cot_hbm.at[0:144], cot_ref),
        (feat_hbm.at[0, rows - 16 : rows], closes.at[0, 128:144]),
        (feat_hbm.at[1, 0:16], opens.at[1, 0:16]),
        (feat_hbm.at[2, 0:16], opens.at[2, 0:16]),
    ]
    copies = [
        pltpu.make_async_copy(source, target, sems.at[n])
        for n, (source, target) in enumerate(pairs)
    ]
    for copy in copies:
        copy.start()
    for copy in copies:
        copy.wait()

    @pl.loop(0, cot_ref.shape[1] // LANES)
    def _(step):
        lanes = lanes_of(step)
        channel_taps(taps_ref, taps.at[:, lanes], step)
        weights = taps[:, lanes]
        raw[0, 0:8, :] = jnp.zeros((8, LANES), F32)
        raw[0, 8:152, :] = opens[0, :, lanes].astype(F32)
        for i in (1, 2):
            raw[i, 0:144, :] = closes[i, :, lanes].astype(F32)
        for lo in (0, 64):
            key = causal(raw, 1, 16 + lo, 64, weights).astype(F32)
            value = causal(raw, 2, 16 + lo, 64, weights).astype(F32)
            up_ref[lo : lo + 64, lanes] = (key * value).astype(BF16)
        last = [closes[i, 128:144, lanes].astype(F32)[8:16] for i in range(3)]
        blank = jnp.zeros((8, LANES), F32)
        up_ref[128:160, lanes] = jnp.concatenate(last + [blank], axis=0).astype(BF16)
        for lo in (0, 64):
            inner = causal(raw, 0, 8 + lo, 64, weights).astype(F32)
            grad = cot_ref[lo : lo + 64, lanes].astype(F32)
            inner = grad * inner
            if lo == 0:
                first = jnp.where(iota((8, LANES), 0) < 6, grad[0:8], inner[0:8])
                inner = jnp.concatenate([first, inner[8:64]], axis=0)
            down_ref[lo : lo + 64, lanes] = inner.astype(BF16)
        query = causal(raw, 0, 136, 8, weights).astype(F32)
        rest = cot_ref[128:144, lanes].astype(F32)[0:8] * query
        begin = [opens[i, 0:16, lanes].astype(F32)[0:8] for i in range(3)]
        down_ref[128:160, lanes] = jnp.concatenate([rest] + begin, axis=0).astype(BF16)


def local_kernel(
    feat_ref, cot_ref, taps_ref, long_ref, gain_ref,
    mixed_ref, product_ref, inner_ref, ahead_ref, behind_ref,
    gated_ref, grad_ref, gmix_ref, lines_ref, grid_ref,
    raw, filt, spread, gmix,
):
    rows = cot_ref.shape[0]
    groups = long_ref.shape[0]
    flip = iota((128, 256), 0) + iota((128, 256), 1) == 128
    flip = flip.astype(F32).astype(BF16)
    filt[0] = jnp.dot(long_ref[...], flip, preferred_element_type=F32)
    filt[1, :, 0:128] = long_ref[...].astype(F32)
    filt[1, :, 128:256] = jnp.zeros((groups, 128), F32)

    @pl.loop(0, cot_ref.shape[1] // LANES)
    def _(step):
        lanes = lanes_of(step)
        block = pl.ds(pl.multiple_of(LANES * step, LANES), LANES)
        gain = gain_ref[:, lanes].astype(F32)
        weights = taps_ref[:, lanes]
        for which, out in ((0, ahead_ref), (1, behind_ref)):
            base = filt[which, pl.ds(pl.multiple_of(GROUPS * step, GROUPS), GROUPS), :]
            for r in range(STEP):
                moved = base if r == 0 else pltpu.roll(base, r, 1)
                for half in (0, 1):
                    part = moved[:, 128 * half : 128 * half + 128]
                    spread[which, half, pl.ds(r, GROUPS, stride=STEP), :] = part
            for half in (0, 1):
                out[block, 128 * half : 128 * half + 128] = spread[which, half].astype(BF16)
        for i in range(3):
            raw[i, 0:8, :] = jnp.zeros((8, LANES), F32)
            raw[i, 8 : 8 + rows, :] = feat_ref[i, :, lanes].astype(F32)
        size = 64
        for lo in range(0, rows, size):
            query, key, value = [causal(raw, i, 8 + lo, size, weights) for i in range(3)]
            mixed_ref[0, lo : lo + size, lanes] = query
            mixed_ref[1, lo : lo + size, lanes] = key
            mixed_ref[2, lo : lo + size, lanes] = value
            both = key.astype(F32) * value.astype(F32)
            product_ref[lo : lo + size, lanes] = both.astype(BF16)
            grad = cot_ref[lo : lo + size, lanes].astype(F32)
            inner_ref[lo : lo + size, lanes] = (grad * query.astype(F32)).astype(BF16)
        masks = group_masks()
        keep = [m.astype(F32).astype(BF16) for m in masks]
        convs, backs = inside(rows)
        starts = settled(rows)
        matrix = ahead_ref[block, 0:WINDOW]
        for b, conv in filtered(matrix, product_ref, -128, convs, masks, lanes):
            at = slice(STEP * b, STEP * b + STEP)
            to = slice(STEP * (b - convs[0]), STEP * (b - convs[0]) + STEP)
            inner = conv + gain * product_ref[at, lanes].astype(F32)
            grad = (cot_ref[at, lanes].astype(F32) * inner).astype(BF16)
            gmix[0, to, :] = grad.astype(F32)
            gated_ref[to, lanes] = (mixed_ref[0, at, lanes].astype(F32) * inner).astype(BF16)
            if b == convs[0] or b == convs[-1]:
                half = STEP * (b == convs[-1])
                gmix_ref[0, half : half + STEP, lanes] = grad
        matrix = behind_ref[block, 0:WINDOW]
        for b, back in filtered(matrix, inner_ref, 0, backs, masks, lanes):
            at = slice(STEP * b, STEP * b + STEP)
            to = slice(STEP * (b - backs[0]), STEP * (b - backs[0]) + STEP)
            grad = back + gain * inner_ref[at, lanes].astype(F32)
            grad = grad.astype(BF16).astype(F32)
            for i, other in ((1, 2), (2, 1)):
                value = (grad * mixed_ref[other, at, lanes].astype(F32)).astype(BF16)
                gmix[i, to, :] = value.astype(F32)
                if b == backs[0] or b == backs[-1]:
                    half = STEP * (b == backs[-1])
                    gmix_ref[i, half : half + STEP, lanes] = value
        for i in range(3):
            totals = [None] * 7
            for lo in (0, 48):
                at = starts[i] + lo
                own = feat_ref[i, at : at + 48, lanes].astype(F32)
                grad_ref[i, lo : lo + 48, lanes] = short_pass(
                    gmix, i, own, weights, totals, lo, 48
                )
            lines = [jnp.sum(total, axis=0, keepdims=True) for total in totals]
            lines.append(jnp.zeros((1, LANES), F32))
            lines_ref[8 * i : 8 * i + 8, lanes] = jnp.concatenate(lines, axis=0)
        grid_ref[block, 0:WINDOW] = correlated(
            None,
            lambda b: product_ref[STEP * b : STEP * b + STEP, lanes],
            lambda b: inner_ref[STEP * b : STEP * b + WINDOW, lanes],
            backs,
            keep,
        )


def main_kernel(
    feat_ref, cot_ref, taps_ref, gain_ref, mixed_ref, product_ref, inner_ref, ahead_ref, behind_ref,
    near_gated, near_grad, near_gmix, lines_ref, grid_ref, up_ref, down_ref,
    gated_ref, grad_ref, sums_ref,
    prod, ginn, gmix, raw, edges, corr,
):
    step = pl.program_id(0)
    rows = cot_ref.shape[0]
    chunks = rows // STEP
    lanes = lanes_of(step)
    block = pl.ds(pl.multiple_of(LANES * step, LANES), LANES)
    every = pl.ds(0, LANES)
    weights = taps_ref[:, lanes]
    gain = gain_ref[:, lanes].astype(F32)
    masks = group_masks()
    keep = [m.astype(F32).astype(BF16) for m in masks]

    before = up_ref[128:160, lanes].astype(F32)
    tail = down_ref[128:160, lanes].astype(F32)
    start, end = [], []
    for i in range(3):
        raw[i, 0:8, :] = before[8 * i : 8 * i + 8]
        raw[i, 8:24, :] = feat_ref[i, 0:16, lanes].astype(F32)
        raw[i, 24:40, :] = feat_ref[i, rows - 16 : rows, lanes].astype(F32)
        raw[i, 40:48, :] = tail[8 + 8 * i : 16 + 8 * i]
        first = causal(raw, i, 8, 8, weights).astype(F32)
        second = mixed_ref[i, 0:16, lanes].astype(F32)[8:16]
        start.append(jnp.concatenate([first, second], axis=0))
        past_end = causal(raw, i, 40, 8, weights).astype(F32)
        end.append(jnp.concatenate([past_end, jnp.zeros((8, LANES), F32)], axis=0))
        edges[i, 0:16, :] = start[i]
        edges[i, 16:32, :] = end[i]
    opening = down_ref[0:16, lanes].astype(F32)
    past = iota((STEP, LANES), 0) < 6
    after = jnp.where(past, opening, 0.0)
    edges[3, 0:16, :] = cot_ref[0:16, lanes].astype(F32)
    edges[3, 16:32, :] = after

    prod[0:128, :] = up_ref[0:128, lanes]
    prod[128:144, :] = (start[1] * start[2]).astype(BF16)
    prod[144 : 128 + rows, :] = product_ref[16:rows, lanes]
    prod[128 + rows : 144 + rows, :] = (end[1] * end[2]).astype(BF16)
    ginn[0:16, :] = (cot_ref[0:16, lanes].astype(F32) * start[0]).astype(BF16)
    ginn[16:rows, :] = inner_ref[16:rows, lanes]
    ginn[rows : rows + 16, :] = jnp.where(past, after * end[0], opening).astype(BF16)
    ginn[rows + 16 : rows + 128, :] = down_ref[16:128, lanes]
    ginn[rows + 128 : rows + 144, :] = jnp.concatenate(
        [tail[0:8], jnp.zeros((8, LANES), F32)], axis=0
    ).astype(BF16)

    convs, backs = inside(rows)
    grid = correlated(
        grid_ref[block, 0:WINDOW],
        lambda b: prod[128 + STEP * b : 144 + STEP * b, :],
        lambda b: ginn[STEP * b : STEP * b + WINDOW, :],
        [b for b in range(chunks) if b not in backs],
        keep,
    )
    corr[0] = grid[:, 0:128]
    corr[1, :, 0 : WINDOW - 128] = grid[:, 128:WINDOW]
    corr[1, :, WINDOW - 128 : 128] = jnp.zeros((LANES, 256 - WINDOW), F32)

    def mixed(i, b):
        if b == 0 or b == chunks:
            return edges[i, STEP * (b > 0) : STEP * (b > 0) + STEP, :]
        if i == 3:
            return cot_ref[STEP * b : STEP * b + STEP, lanes].astype(F32)
        return mixed_ref[i, STEP * b : STEP * b + STEP, lanes].astype(F32)

    def put(i, b, values):
        gmix[i, STEP * b : STEP * b + STEP, :] = values.astype(BF16).astype(F32)

    outer = [b for b in range(chunks + 1) if b not in convs]
    for b, conv in filtered(ahead_ref[block, 0:WINDOW], prod, 0, outer, masks, every):
        inner = conv + gain * prod[128 + STEP * b : 144 + STEP * b, :].astype(F32)
        put(0, b, mixed(3, b) * inner)
        if b < chunks:
            gated_ref[STEP * b : STEP * b + STEP, :] = (mixed(0, b) * inner).astype(BF16)
    gated_ref[STEP * convs[0] : STEP * chunks, :] = near_gated[:, lanes]
    outer = [b for b in range(chunks + 1) if b not in backs]
    for b, back in filtered(behind_ref[block, 0:WINDOW], ginn, 0, outer, masks, every):
        grad = back + gain * ginn[STEP * b : STEP * b + STEP, :].astype(F32)
        grad = grad.astype(BF16).astype(F32)
        put(1, b, grad * mixed(2, b))
        put(2, b, grad * mixed(1, b))
    for i, known in ((0, convs), (1, backs), (2, backs)):
        put(i, known[0], near_gmix[i, 0:16, lanes])
        put(i, known[-1], near_gmix[i, 16:32, lanes])

    skip = jnp.zeros((STEP, LANES), F32)
    for b in range(chunks):
        p = prod[128 + STEP * b : 144 + STEP * b, :].astype(F32)
        skip = skip + p * ginn[STEP * b : STEP * b + STEP, :].astype(F32)
    sums_ref[pl.ds(64 + step, 1), :] = jnp.sum(skip, axis=0, keepdims=True)
    total = None
    for r in range(STEP):
        line = jnp.concatenate(
            [corr[half, pl.ds(r, GROUPS, stride=STEP), :] for half in (0, 1)], axis=1
        )
        line = line if r == 0 else pltpu.roll(line, 256 - r, 1)
        total = line[:, 0:128] if total is None else total + line[:, 0:128]
    sums_ref[pl.ds(pl.multiple_of(GROUPS * step, GROUPS), GROUPS), :] = total

    lines = []
    for i, first in enumerate(settled(rows)):
        totals = [None] * 7
        todo = [(0, first), (first + 96, rows)]
        for low, high in todo:
            for lo in range(low, high, 48):
                size = min(48, high - lo)
                own = feat_ref[i, lo : lo + size, lanes].astype(F32)
                grad_ref[i, lo : lo + size, :] = short_pass(
                    gmix, i, own, weights, totals, lo, size
                )
        grad_ref[i, first : first + 96, :] = near_grad[i, :, lanes]
        lines += [jnp.sum(part, axis=0, keepdims=True) for part in totals]
        lines.append(jnp.zeros((1, LANES), F32))
    lines = jnp.concatenate(lines, axis=0) + lines_ref[:, lanes]
    gather = iota((LANES, LANES), 1) == GROUPS * step + iota((LANES, LANES), 0) // 16
    gather = gather.astype(F32)
    short = jnp.dot(lines, gather, precision=lax.Precision.HIGHEST, preferred_element_type=F32)

    @pl.when(step == 0)
    def _():
        sums_ref[72:96, :] = short

    @pl.when(step > 0)
    def _():
        sums_ref[72:96, :] += short


def final_kernel(group_scale, token_scale, sums_ref, short_ref, long_ref, skip_ref):
    groups = long_ref.shape[0]
    values = sums_ref[...]
    long_ref[...] = values[0:groups] * group_scale
    skip_ref[...] = values[64 : 64 + skip_ref.shape[0]] * token_scale
    for i in range(3):
        short_ref[i] = values[72 + 8 * i : 79 + 8 * i, 0:groups] * group_scale


def blocks3(rows):
    return pl.BlockSpec((3, rows, LANES), lambda b: (0, 0, b))


def blocks2(rows):
    return pl.BlockSpec((rows, LANES), lambda b: (0, b))


def swap(values, axes):
    return lax.all_to_all(values, axes, 0, 0, tiled=True)


def summed(local):
    near, far = CTX[:2], CTX[2]
    parts = lax.axis_size(near)
    size = lax.axis_size(far)
    share = local.reshape(parts, -1, LANES)
    share = swap(share, near).sum(axis=0)
    every = jnp.broadcast_to(share[None], (size,) + share.shape)
    share = swap(every, far).sum(axis=0)
    every = jnp.broadcast_to(share[None], (parts,) + share.shape)
    return swap(every, near).reshape(local.shape)


def body(features, short_taps, long_taps, skip_gain, cotangent):
    rows, width = features.shape[1:]
    groups = width // 16
    steps = width // LANES
    inside_vmem = pl.BlockSpec(memory_space=pltpu.VMEM)
    outside = pl.BlockSpec(memory_space=pltpu.HBM)
    short_taps = short_taps.transpose(0, 2, 1)
    shape = jax.ShapeDtypeStruct

    def call(kernel, name, ins, outs, scratch, cost, grid=(), limit=LIMIT):
        return pl.pallas_call(
            kernel,
            grid=grid,
            in_specs=ins,
            out_specs=[spec for spec, _ in outs],
            out_shape=[out for _, out in outs],
            scratch_shapes=scratch,
            compiler_params=pltpu.CompilerParams(
                dimension_semantics=("arbitrary",) * len(grid), vmem_limit_bytes=limit
            ),
            cost_estimate=pl.CostEstimate(flops=cost, bytes_accessed=cost, transcendentals=0),
            name=name,
        )

    def held(*dims, dtype=BF16):
        return inside_vmem, shape(dims, dtype)

    up, down, taps = call(
        edge_kernel,
        "edge",
        [outside] * 3,
        [
            held(160, width),
            held(160, width),
            held(24, width, dtype=F32),
        ],
        [
            pltpu.VMEM((3, 144, width), BF16),
            pltpu.VMEM((3, 144, width), BF16),
            pltpu.VMEM((144, width), BF16),
            pltpu.VMEM(short_taps.shape, BF16),
            pltpu.VMEM((3, 152, LANES), F32),
            pltpu.SemaphoreType.DMA((8,)),
        ],
        5 * 10**6,
        limit=EDGE_LIMIT,
    )(features, cotangent, short_taps)
    from_last = passed_along(up, CTX, 1)
    from_next = passed_along(down, CTX, -1)
    convs, backs = inside(rows)
    gain = skip_gain.reshape(1, width)
    near = call(
        local_kernel,
        "local",
        [inside_vmem] * 5,
        [
            held(3, rows, width),
            held(rows, width),
            held(rows, width),
            held(groups * 16, 256),
            held(groups * 16, 256),
            held(STEP * len(convs), width),
            held(3, 96, width),
            held(3, 32, width),
            held(24, width, dtype=F32),
            held(groups * 16, 256, dtype=F32),
        ],
        [
            pltpu.VMEM((3, rows + 8, LANES), F32),
            pltpu.VMEM((2, groups, 256), F32),
            pltpu.VMEM((2, 2, 128, LANES), F32),
            pltpu.VMEM((3, STEP * len(convs), LANES), F32),
        ],
        2 * 10**7,
    )(features, cotangent, taps, long_taps, gain)
    gated, feature_grad, sums = call(
        main_kernel,
        "main",
        [inside_vmem] * 16,
        [
            (blocks2(rows), shape((rows, width), BF16)),
            (blocks3(rows), shape((3, rows, width), BF16)),
            (inside_vmem, shape((96, LANES), F32)),
        ],
        [
            pltpu.VMEM((rows + 144, LANES), BF16),
            pltpu.VMEM((rows + 144, LANES), BF16),
            pltpu.VMEM((3, rows + 16, LANES), F32),
            pltpu.VMEM((3, 48, LANES), F32),
            pltpu.VMEM((4, 32, LANES), F32),
            pltpu.VMEM((2, 128, LANES), F32),
        ],
        2 * 10**7,
        (steps,),
    )(features, cotangent, taps, gain, *near, from_last, from_next)
    tokens = rows * lax.axis_size(CTX)
    group_scale = 1.0 / math.sqrt(16.0 * tokens)
    token_scale = 1.0 / math.sqrt(1.0 * tokens)
    short, long, skip = call(
        functools.partial(final_kernel, group_scale, token_scale),
        "final",
        [inside_vmem],
        [
            held(3, 7, groups, dtype=F32),
            held(groups, LANES, dtype=F32),
            held(steps, LANES, dtype=F32),
        ],
        [],
        10**5,
    )(summed(sums))
    return gated, feature_grad, short.transpose(0, 2, 1), long, skip.reshape(width)


def solution(mesh):
    torus = Mesh(mesh.devices.reshape(*SPLIT, mesh.shape["tp"]), CTX + ("tp",))
    return jax.shard_map(
        body,
        mesh=torus,
        in_specs=(P(None, CTX, "tp"), P(None, "tp", None), P("tp", None), P("tp"), P(CTX, "tp")),
        out_specs=(P(CTX, "tp"), P(None, CTX, "tp"), P(None, "tp", None), P("tp", None), P("tp")),
        check_vma=False,
    )
```

time: 374 us -> 73.5 us (0.20)
  local copies, waits for them, and re-layouts: 214 us -> 0.92 us
  other arithmetic: 62.9 us -> 0.02 us
  blocking collectives: 68.5 us -> 45 us
  matrix products: 19 us -> 0 us
  Pallas kernels: 0 us -> 19 us
    gather x2 -> x0, local copies, waits for them, and re-layouts: 124 us -> none  [toeplitz_blocks(): return jnp.take(extra, picks, axis=1)]
    psum x3 -> x0, blocking collectives: 68.5 us -> none  [one_axis_at_a_time(): return functools.reduce(lax.psum, axes, shard)]
    all_to_all x0 -> x3, blocking collectives: none -> 45 us  [swap(): return lax.all_to_all(values, axes, 0, 0, tiled=True)]
    reshape x8 -> x1, local copies, waits for them, and re-layouts: 42.9 us -> 0.01 us  [body(): gain = skip_gain.reshape(1, width)]
    convert_element_type x6 -> x0, other arithmetic: 29.8 us -> none  [the longest x1 14.9 us: body(): short_filter(wide, taps, rows + 127).astype(jnp.bfloat16)]
    pad x2 -> x0, local copies, waits for them, and re-layouts: 19.5 us -> none  [the longest x1 9.9 us: diagonal_sums(): flat = jnp.pad(padded.reshape(groups, 128 * 382), ((0, 0), (0, 128)))]
    pallas_call x0 -> x4, Pallas kernels: none -> 19 us  [the longest x1 7.92 us: body(): call(main_kernel, 'main', [inside_vmem] * 16, [(blocks2(rows), shape((row...]
    dot_general x6 -> x0, matrix products: 19 us -> none  [the longest x1 3.79 us: body(): jnp.einsum('gts,gns->gnt', earlier, before, preferred_element_type=jnp.fl...]
  transfers between devices with their start and end apart: 3 -> 2, of which waited for: 0 -> 1; matrix products, arithmetic and copies ran while one was open for 60% -> 0% of each run, Pallas kernels for 0% -> 9%
where the time goes in v3:
time: 73.5 us; the launch traced here: 73.2 us
  blocking collectives  45 us (61%)
  Pallas kernels  19 us (26%)
  starting transfers between devices  4.79 us (7%)
  waiting for transfers between devices  2.79 us (4%)
  local copies, waits for them, and re-layouts  0.92 us (1%)
  between operations  0.76 us (1%)
    all_to_all x3, blocking collectives, swap(): return lax.all_to_all(values, axes, 0, 0, tiled=True)  45 us
    pallas_call x1, Pallas kernels, body(): call(main_kernel, 'main', [inside_vmem] * 16, [(blocks2(rows), shape((row...  7.92 us
    pallas_call x1, Pallas kernels, body(): call(local_kernel, 'local', [inside_vmem] * 5, [held(3, rows, width), hel...  6.22 us
    ppermute x2, starting transfers between devices, passed_along(): return lax.ppermute(block, axis, route)  4.79 us
    pallas_call x1, Pallas kernels, body(): call(edge_kernel, 'edge', [outside] * 3, [held(160, width), held(160, wid...  4.21 us
    ppermute x2, waiting for transfers between devices, passed_along(): return lax.ppermute(block, axis, route)  2.79 us
  transfers between devices with their start and end apart: 2, of which 1 were waited for; matrix products, arithmetic and copies ran while one was open for 0% of the time, Pallas kernels for 9%

profile of v3, /device:TPU:192, one launch (start us, length us, event | category | flops | bytes accessed | tf_op | source)
XLA Modules:
  0.0 73.2 jit_solution(11801080171345253126)
XLA Ops:
  0.6 0.0 copy-start.1
  0.6 0.0 copy-start
  0.7 0.0 copy-start.4
  0.7 0.0 copy-start.3
  0.7 4.2 %edge.1 = (bf16[160,1024]{1,0:T(8,128)(2,1)}, bf16[160,1024]{1,0:T(8,128)(2,1)}, f32[24,1024]{1,0:T(8,128)}) custom-call(bf16[3,256,1024]{2,1,0:T(8,128)(2,1)} %feat_ref.3, bf16[256,1024]{1,0:T(8,128)(2,1)} %cot_ref.3, bf16[3,7,64]{2,1,0:T(8,128)(2,1)} %bitcast.7), custom_call_target="tpu_custom_call" | custom-call | flops 5000000 | bytes 5000000 | tf_op jit(solution)/shard_map/edge/pallas_call | solution.py:449
  4.9 3.5 %collective-permute-start = (bf16[160,1024]{1,0:T(8,128)(2,1)}, bf16[160,1024]{1,0:T(8,128)(2,1)S(1)}, u32[]{:S(2)}, u32[]{:S(2)}) collective-permute-start(bf16[160,1024]{1,0:T(8,128)(2,1)} %get-tuple-element.35), channel_id=1, source_target_pairs={{0,8},{8,16},{16,24},{24,32},{32,40},{40,48},{48,56},{56,64},{64,7... | collective-permute-start | bytes 983048 | tf_op jit(solution)/shard_map/ppermute | solution.py:27
  8.4 1.3 %collective-permute-start.1 = (bf16[160,1024]{1,0:T(8,128)(2,1)}, bf16[160,1024]{1,0:T(8,128)(2,1)S(1)}, u32[]{:S(2)}, u32[]{:S(2)}) collective-permute-start(bf16[160,1024]{1,0:T(8,128)(2,1)} %get-tuple-element.36), channel_id=1, source_target_pairs={{8,0},{16,8},{24,16},{32,24},{40,32},{48,40},{56,48},{64,56},{72,6... | collective-permute-start | bytes 983048 | tf_op jit(solution)/shard_map/ppermute | solution.py:27
  9.7 0.0 copy-done.4
  9.7 0.0 copy-done.1
  9.7 0.0 copy-done
  9.7 0.0 copy-done.3
  9.7 0.0 copy-start.2
  9.8 0.9 %copy-done.2 = f32[24,1024]{1,0:T(8,128)S(1)} copy-done((f32[24,1024]{1,0:T(8,128)S(1)}, f32[24,1024]{1,0:T(8,128)}, u32[]{:S(2)}) %copy-start.2) | copy-done | bytes 98328
  10.6 6.2 %local.1 = (bf16[3,256,1024]{2,1,0:T(8,128)(2,1)S(1)}, bf16[256,1024]{1,0:T(8,128)(2,1)S(1)}, bf16[256,1024]{1,0:T(8,128)(2,1)S(1)}, bf16[1024,256]{1,0:T(8,128)...) custom-call(bf16[3,256,1024]{2,1,0:T(8,128)(2,1)S(1)} %copy-done, ...), custom_call_target="tpu_custom_call" | custom-call | flops 20000000 | bytes 20000000 | tf_op jit(solution)/shard_map/local/pallas_call | solution.py:473
  16.9 0.0 collective-permute-done.up_ref
  16.9 2.8 %collective-permute-done.1.down_ref = bf16[160,1024]{1,0:T(8,128)(2,1)S(1)} collective-permute-done((bf16[160,1024]{1,0:T(8,128)(2,1)}, bf16[160,1024]{1,0:T(8,128)(2,1)S(1)}, u32[]{:S(2)}, u32[]{:S(2)}) %collective-permute-start.1) | collective-permute-done | bytes 327712 | tf_op jit(solution)/shard_map/ppermute | solution.py:27
  19.7 7.9 %main.1 = (bf16[256,1024]{1,0:T(8,128)(2,1)}, bf16[3,256,1024]{2,1,0:T(8,128)(2,1)}, f32[96,128]{1,0:T(8,128)S(1)}) custom-call(bf16[3,256,1024]{2,1,0:T(8,128)(2,1)S(1)} %copy-done, bf16[256,1024]{1,0:T(8,128)(2,1)S(1)} %copy-done.1, f32[24,1024]{1,0:T(8,128)S(1)} %copy-done.2, bf16[1,1024]{1,0:T(2,128)(2,1)S(1)} %reshape.24.gain_ref, ...), custom_call_target="tpu_custom_call" | custom-call | flops 20000000 | bytes 20000000 | tf_op jit(solution)/shard_map/main/pallas_call | solution.py:497
  27.6 17.9 %all_to_all.15 = f32[12,8,128]{2,1,0:T(8,128)S(1)} all-to-all(f32[12,8,128]{2,1,0:T(8,128)S(1)} %bitcast.6), channel_id=1, replica_groups=mesh['ctx_0'=4,'ctx_1'=3,'ctx_2'=8,'tp'=8] {'ctx_0','ctx_1'}, dimensions={0} | all-to-all | bytes 98304 | tf_op jit(solution)/shard_map/all_to_all | solution.py:407
  45.6 16.0 %all_to_all.16 = f32[8,8,128]{2,1,0:T(8,128)S(1)} all-to-all(f32[8,8,128]{2,1,0:T(8,128)S(1)} %broadcast_in_dim.4), channel_id=1, replica_groups=mesh['ctx_0'=4,'ctx_1'=3,'ctx_2'=8,'tp'=8] {'ctx_2'}, dimensions={0} | all-to-all | bytes 65536 | tf_op jit(solution)/shard_map/all_to_all | solution.py:407
  61.5 11.1 %all_to_all.17 = f32[12,8,128]{2,1,0:T(8,128)S(1)} all-to-all(f32[12,8,128]{2,1,0:T(8,128)S(1)} %broadcast_in_dim.5), channel_id=1, replica_groups=mesh['ctx_0'=4,'ctx_1'=3,'ctx_2'=8,'tp'=8] {'ctx_0','ctx_1'}, dimensions={0} | all-to-all | bytes 98304 | tf_op jit(solution)/shard_map/all_to_all | solution.py:407
  72.6 0.6 final.1
  (5 shorter events, 0.0 us)
Async XLA Ops:
  0.6 9.1 %copy-start.1 = (bf16[256,1024]{1,0:T(8,128)(2,1)S(1)}, bf16[256,1024]{1,0:T(8,128)(2,1)}, u32[]{:S(2)}) copy-start(bf16[256,1024]{1,0:T(8,128)(2,1)} %cot_ref.3) | copy-start | bytes 1572868
  0.6 9.1 %copy-start = (bf16[3,256,1024]{2,1,0:T(8,128)(2,1)S(1)}, bf16[3,256,1024]{2,1,0:T(8,128)(2,1)}, u32[]{:S(2)}) copy-start(bf16[3,256,1024]{2,1,0:T(8,128)(2,1)} %feat_ref.3) | copy-start | bytes 4718596
  0.7 9.0 %copy-start.4 = (bf16[1024]{0:T(1024)(128)(2,1)S(1)}, bf16[1024]{0:T(1024)(128)(2,1)}, u32[]{:S(2)}) copy-start(bf16[1024]{0:T(1024)(128)(2,1)} %param.8) | copy-start | bytes 6148
  0.7 9.1 %copy-start.3 = (bf16[64,128]{1,0:T(8,128)(2,1)S(1)}, bf16[64,128]{1,0:T(8,128)(2,1)}, u32[]{:S(2)}) copy-start(bf16[64,128]{1,0:T(8,128)(2,1)} %long_ref.1) | copy-start | bytes 49156
  4.9 12.0 %collective-permute-start = (bf16[160,1024]{1,0:T(8,128)(2,1)}, bf16[160,1024]{1,0:T(8,128)(2,1)S(1)}, u32[]{:S(2)}, u32[]{:S(2)}) collective-permute-start(bf16[160,1024]{1,0:T(8,128)(2,1)} %get-tuple-element.35), channel_id=1, source_target_pairs={{0,8},{8,16},{16,24},{24,32},{32,40},{40,48},{48,56},{56,64},{64,7... | collective-permute-start | bytes 983048 | tf_op jit(solution)/shard_map/ppermute | solution.py:27
  8.4 11.3 %collective-permute-start.1 = (bf16[160,1024]{1,0:T(8,128)(2,1)}, bf16[160,1024]{1,0:T(8,128)(2,1)S(1)}, u32[]{:S(2)}, u32[]{:S(2)}) collective-permute-start(bf16[160,1024]{1,0:T(8,128)(2,1)} %get-tuple-element.36), channel_id=1, source_target_pairs={{8,0},{16,8},{24,16},{32,24},{40,32},{48,40},{56,48},{64,56},{72,6... | collective-permute-start | bytes 983048 | tf_op jit(solution)/shard_map/ppermute | solution.py:27
  9.7 0.9 %copy-start.2 = (f32[24,1024]{1,0:T(8,128)S(1)}, f32[24,1024]{1,0:T(8,128)}, u32[]{:S(2)}) copy-start(f32[24,1024]{1,0:T(8,128)} %get-tuple-element.24.taps_ref) | copy-start | bytes 294916

commit v4 on v3

--- a/solution.py
+++ b/solution.py
@@ -18,6 +18,7 @@
 BF16 = jnp.bfloat16
 F32 = jnp.float32
 LIMIT = 16 * 2**20
+TOGETHER, AT_EDGE, AT_LOCAL = 2, 4, 1
 EDGE_LIMIT = 60000 * 2**10
 
 
@@ -35,14 +36,18 @@
     return pl.ds(pl.multiple_of(LANES * step, LANES), LANES)
 
 
-def channel_taps(taps_ref, out_ref, block):
-    groups = taps_ref.shape[2]
-    spread = iota((groups, LANES), 0) == GROUPS * block + iota((groups, LANES), 1) // 16
+def channel_taps(taps_ref, out_ref):
+    shape = (taps_ref.shape[2], out_ref.shape[1])
+    spread = iota(shape, 0) == iota(shape, 1) // 16
     spread = spread.astype(F32).astype(BF16)
     for i in range(3):
         out_ref[8 * i : 8 * i + 7, :] = jnp.dot(
             taps_ref[i], spread, preferred_element_type=F32
         )
+
+
+def part(refs, u):
+    return [ref.at[u] for ref in refs]
 
 
 def causal(ref, i, start, rows, taps):
@@ -114,32 +119,12 @@
 
 
 def edge_kernel(
-    feat_hbm, cot_hbm, taps_hbm, up_ref, down_ref, taps, opens, closes, cot_ref, taps_ref, raw, sems,
+    feat_hbm, cot_hbm, taps_hbm, up_ref, down_ref, taps, opens, closes, cot_ref, taps_ref, raws, sems,
 ):
     rows = cot_hbm.shape[0]
-    pairs = [
-        (taps_hbm, taps_ref),
-        (feat_hbm.at[1, rows - 144 : rows], closes.at[1]),
-        (feat_hbm.at[2, rows - 144 : rows], closes.at[2]),
-        (feat_hbm.at[0, 0:144], opens.at[0]),
-        (cot_hbm.at[0:144], cot_ref),
-        (feat_hbm.at[0, rows - 16 : rows], closes.at[0, 128:144]),
-        (feat_hbm.at[1, 0:16], opens.at[1, 0:16]),
-        (feat_hbm.at[2, 0:16], opens.at[2, 0:16]),
-    ]
-    copies = [
-        pltpu.make_async_copy(source, target, sems.at[n])
-        for n, (source, target) in enumerate(pairs)
-    ]
-    for copy in copies:
-        copy.start()
-    for copy in copies:
-        copy.wait()
-
-    @pl.loop(0, cot_ref.shape[1] // LANES)
-    def _(step):
+
+    def block(step, raw):
         lanes = lanes_of(step)
-        channel_taps(taps_ref, taps.at[:, lanes], step)
         weights = taps[:, lanes]
         raw[0, 0:8, :] = jnp.zeros((8, LANES), F32)
         raw[0, 8:152, :] = opens[0, :, lanes].astype(F32)
@@ -165,12 +150,38 @@
         begin = [opens[i, 0:16, lanes].astype(F32)[0:8] for i in range(3)]
         down_ref[128:160, lanes] = jnp.concatenate([rest] + begin, axis=0).astype(BF16)
 
+    pairs = [
+        (taps_hbm, taps_ref),
+        (feat_hbm.at[1, rows - 144 : rows], closes.at[1]),
+        (feat_hbm.at[2, rows - 144 : rows], closes.at[2]),
+        (feat_hbm.at[0, 0:144], opens.at[0]),
+        (cot_hbm.at[0:144], cot_ref),
+        (feat_hbm.at[0, rows - 16 : rows], closes.at[0, 128:144]),
+        (feat_hbm.at[1, 0:16], opens.at[1, 0:16]),
+        (feat_hbm.at[2, 0:16], opens.at[2, 0:16]),
+    ]
+    copies = [
+        pltpu.make_async_copy(source, target, sems.at[n])
+        for n, (source, target) in enumerate(pairs)
+    ]
+    for copy in copies:
+        copy.start()
+    copies[0].wait()
+    channel_taps(taps_ref, taps)
+    for copy in copies[1:]:
+        copy.wait()
+
+    @pl.loop(0, cot_ref.shape[1] // LANES // AT_EDGE)
+    def _(step):
+        for u in range(AT_EDGE):
+            block(AT_EDGE * step + u, raws.at[u])
+
 
 def local_kernel(
     feat_ref, cot_ref, taps_ref, long_ref, gain_ref,
-    mixed_ref, product_ref, inner_ref, ahead_ref, behind_ref,
+    taps_out, mixed_ref, product_ref, inner_ref, ahead_ref, behind_ref,
     gated_ref, grad_ref, gmix_ref, lines_ref, grid_ref,
-    raw, filt, spread, gmix,
+    raws, filt, spreads, gmixes,
 ):
     rows = cot_ref.shape[0]
     groups = long_ref.shape[0]
@@ -180,12 +191,13 @@
     filt[1, :, 0:128] = long_ref[...].astype(F32)
     filt[1, :, 128:256] = jnp.zeros((groups, 128), F32)
 
-    @pl.loop(0, cot_ref.shape[1] // LANES)
-    def _(step):
+    channel_taps(taps_ref, taps_out)
+
+    def one(step, raw, spread, gmix):
         lanes = lanes_of(step)
         block = pl.ds(pl.multiple_of(LANES * step, LANES), LANES)
         gain = gain_ref[:, lanes].astype(F32)
-        weights = taps_ref[:, lanes]
+        weights = taps_out[:, lanes]
         for which, out in ((0, ahead_ref), (1, behind_ref)):
             base = filt[which, pl.ds(pl.multiple_of(GROUPS * step, GROUPS), GROUPS), :]
             for r in range(STEP):
@@ -254,15 +266,95 @@
             keep,
         )
 
-
-def main_kernel(
-    feat_ref, cot_ref, taps_ref, gain_ref, mixed_ref, product_ref, inner_ref, ahead_ref, behind_ref,
-    near_gated, near_grad, near_gmix, lines_ref, grid_ref, up_ref, down_ref,
-    gated_ref, grad_ref, sums_ref,
-    prod, ginn, gmix, raw, edges, corr,
+    @pl.loop(0, cot_ref.shape[1] // LANES // AT_LOCAL)
+    def _(step):
+        for u in range(AT_LOCAL):
+            one(AT_LOCAL * step + u, *part((raws, spreads, gmixes), u))
+
+
+def finish(gmix, i, low, high, shift, feat_ref, lanes, weights, totals, store):
+    for lo in range(low, high, 48):
+        size = min(48, high - lo)
+        own = feat_ref[i, lo : lo + size, lanes].astype(F32)
+        store(lo, size, short_pass(gmix, i, own, weights, totals, lo - shift, size))
+
+
+def summed_lines(totals):
+    lines = []
+    for parts in totals:
+        lines += [jnp.sum(part, axis=0, keepdims=True) for part in parts]
+        lines.append(jnp.zeros((1, LANES), F32))
+    return jnp.concatenate(lines, axis=0)
+
+
+def before_block(
+    step, feat_ref, cot_ref, taps_ref, gain_ref, mixed_ref, product_ref, inner_ref, ahead_ref, behind_ref,
+    near_gated, near_gmix, lines_ref, grid_ref, up_ref,
+    gated_ref, first_ref, grad_ref, lines_out, grid_out,
+    prod, ginn, gmix, raw,
 ):
-    step = pl.program_id(0)
     rows = cot_ref.shape[0]
+    lanes = lanes_of(step)
+    block = pl.ds(pl.multiple_of(LANES * step, LANES), LANES)
+    every = pl.ds(0, LANES)
+    weights = taps_ref[:, lanes]
+    gain = gain_ref[:, lanes].astype(F32)
+    masks = group_masks()
+    keep = [m.astype(F32).astype(BF16) for m in masks]
+    convs, backs = inside(rows)
+
+    before = up_ref[128:160, lanes].astype(F32)
+    start = []
+    for i in range(3):
+        raw[i, 0:8, :] = before[8 * i : 8 * i + 8]
+        raw[i, 8:24, :] = feat_ref[i, 0:16, lanes].astype(F32)
+        first = causal(raw, i, 8, 8, weights).astype(F32)
+        second = mixed_ref[i, 0:16, lanes].astype(F32)[8:16]
+        start.append(jnp.concatenate([first, second], axis=0))
+    product = (start[1] * start[2]).astype(BF16)
+    inners = (cot_ref[0:16, lanes].astype(F32) * start[0]).astype(BF16)
+    first_ref[0, :, lanes] = product
+    first_ref[1, :, lanes] = inners
+    prod[0:128, :] = up_ref[0:128, lanes]
+    prod[128:144, :] = product
+    prod[144:272, :] = product_ref[16:144, lanes]
+    ginn[0:16, :] = inners
+    ginn[16:144, :] = inner_ref[16:144, lanes]
+
+    grid_out[block, 0:WINDOW] = correlated(
+        grid_ref[block, 0:WINDOW], lambda b: product, lambda b: ginn[...], [0], keep
+    )
+    outer = list(range(convs[0]))
+    for b, conv in filtered(ahead_ref[block, 0:WINDOW], prod, 0, outer, masks, every):
+        at = slice(STEP * b, STEP * b + STEP)
+        inner = conv + gain * prod[128 + STEP * b : 144 + STEP * b, :].astype(F32)
+        query = start[0] if b == 0 else mixed_ref[0, at, lanes].astype(F32)
+        gmix[0, at, :] = (cot_ref[at, lanes].astype(F32) * inner).astype(BF16).astype(F32)
+        gated_ref[at, :] = (query * inner).astype(BF16)
+    gated_ref[STEP * convs[0] : rows, :] = near_gated[:, lanes]
+    for b, back in filtered(behind_ref[block, 0:WINDOW], ginn, 0, [0], masks, every):
+        grad = back + gain * inners.astype(F32)
+        grad = grad.astype(BF16).astype(F32)
+        gmix[1, 0:16, :] = (grad * start[2]).astype(BF16).astype(F32)
+        gmix[2, 0:16, :] = (grad * start[1]).astype(BF16).astype(F32)
+    totals = [[None] * 7 for _ in range(3)]
+    for i, known in enumerate(settled(rows)):
+        gmix[i, known : known + 16, :] = near_gmix[i, 0:16, lanes].astype(F32)
+
+        def store(lo, size, grad):
+            grad_ref[i, lo : lo + size, lanes] = grad
+
+        finish(gmix, i, 0, known, 0, feat_ref, lanes, weights, totals[i], store)
+    lines_out[:, lanes] = lines_ref[:, lanes] + summed_lines(totals)
+
+
+def after_block(
+    step, feat_ref, taps_ref, gain_ref, mixed_ref, product_ref, inner_ref, ahead_ref, behind_ref,
+    near_grad, near_gmix, first_ref, early_grad, lines_ref, grid_ref, down_ref,
+    grad_ref, sums_ref,
+    prod, ginn, gmix, raw, corr,
+):
+    rows = feat_ref.shape[1]
     chunks = rows // STEP
     lanes = lanes_of(step)
     block = pl.ds(pl.multiple_of(LANES * step, LANES), LANES)
@@ -271,83 +363,58 @@
     gain = gain_ref[:, lanes].astype(F32)
     masks = group_masks()
     keep = [m.astype(F32).astype(BF16) for m in masks]
-
-    before = up_ref[128:160, lanes].astype(F32)
+    convs, backs = inside(rows)
+    base = rows - 128
+
     tail = down_ref[128:160, lanes].astype(F32)
-    start, end = [], []
+    end = []
     for i in range(3):
-        raw[i, 0:8, :] = before[8 * i : 8 * i + 8]
-        raw[i, 8:24, :] = feat_ref[i, 0:16, lanes].astype(F32)
-        raw[i, 24:40, :] = feat_ref[i, rows - 16 : rows, lanes].astype(F32)
-        raw[i, 40:48, :] = tail[8 + 8 * i : 16 + 8 * i]
-        first = causal(raw, i, 8, 8, weights).astype(F32)
-        second = mixed_ref[i, 0:16, lanes].astype(F32)[8:16]
-        start.append(jnp.concatenate([first, second], axis=0))
-        past_end = causal(raw, i, 40, 8, weights).astype(F32)
+        raw[i, 0:16, :] = feat_ref[i, rows - 16 : rows, lanes].astype(F32)
+        raw[i, 16:24, :] = tail[8 + 8 * i : 16 + 8 * i]
+        past_end = causal(raw, i, 16, 8, weights).astype(F32)
         end.append(jnp.concatenate([past_end, jnp.zeros((8, LANES), F32)], axis=0))
-        edges[i, 0:16, :] = start[i]
-        edges[i, 16:32, :] = end[i]
     opening = down_ref[0:16, lanes].astype(F32)
     past = iota((STEP, LANES), 0) < 6
     after = jnp.where(past, opening, 0.0)
-    edges[3, 0:16, :] = cot_ref[0:16, lanes].astype(F32)
-    edges[3, 16:32, :] = after
-
-    prod[0:128, :] = up_ref[0:128, lanes]
-    prod[128:144, :] = (start[1] * start[2]).astype(BF16)
-    prod[144 : 128 + rows, :] = product_ref[16:rows, lanes]
-    prod[128 + rows : 144 + rows, :] = (end[1] * end[2]).astype(BF16)
-    ginn[0:16, :] = (cot_ref[0:16, lanes].astype(F32) * start[0]).astype(BF16)
-    ginn[16:rows, :] = inner_ref[16:rows, lanes]
-    ginn[rows : rows + 16, :] = jnp.where(past, after * end[0], opening).astype(BF16)
-    ginn[rows + 16 : rows + 128, :] = down_ref[16:128, lanes]
-    ginn[rows + 128 : rows + 144, :] = jnp.concatenate(
+    prod[0:128, :] = product_ref[base:rows, lanes]
+    prod[128:144, :] = (end[1] * end[2]).astype(BF16)
+    ginn[0:128, :] = inner_ref[base:rows, lanes]
+    ginn[128:144, :] = jnp.where(past, after * end[0], opening).astype(BF16)
+    ginn[144:256, :] = down_ref[16:128, lanes]
+    ginn[256:272, :] = jnp.concatenate(
         [tail[0:8], jnp.zeros((8, LANES), F32)], axis=0
     ).astype(BF16)
 
-    convs, backs = inside(rows)
+    outer = list(range(backs[-1] + 1, chunks))
     grid = correlated(
         grid_ref[block, 0:WINDOW],
-        lambda b: prod[128 + STEP * b : 144 + STEP * b, :],
-        lambda b: ginn[STEP * b : STEP * b + WINDOW, :],
-        [b for b in range(chunks) if b not in backs],
+        lambda b: prod[STEP * b - base : STEP * b - base + STEP, :],
+        lambda b: ginn[STEP * b - base : STEP * b - base + WINDOW, :],
+        outer,
         keep,
     )
     corr[0] = grid[:, 0:128]
     corr[1, :, 0 : WINDOW - 128] = grid[:, 128:WINDOW]
     corr[1, :, WINDOW - 128 : 128] = jnp.zeros((LANES, 256 - WINDOW), F32)
 
-    def mixed(i, b):
-        if b == 0 or b == chunks:
-            return edges[i, STEP * (b > 0) : STEP * (b > 0) + STEP, :]
-        if i == 3:
-            return cot_ref[STEP * b : STEP * b + STEP, lanes].astype(F32)
-        return mixed_ref[i, STEP * b : STEP * b + STEP, lanes].astype(F32)
-
-    def put(i, b, values):
-        gmix[i, STEP * b : STEP * b + STEP, :] = values.astype(BF16).astype(F32)
-
-    outer = [b for b in range(chunks + 1) if b not in convs]
-    for b, conv in filtered(ahead_ref[block, 0:WINDOW], prod, 0, outer, masks, every):
-        inner = conv + gain * prod[128 + STEP * b : 144 + STEP * b, :].astype(F32)
-        put(0, b, mixed(3, b) * inner)
-        if b < chunks:
-            gated_ref[STEP * b : STEP * b + STEP, :] = (mixed(0, b) * inner).astype(BF16)
-    gated_ref[STEP * convs[0] : STEP * chunks, :] = near_gated[:, lanes]
-    outer = [b for b in range(chunks + 1) if b not in backs]
-    for b, back in filtered(behind_ref[block, 0:WINDOW], ginn, 0, outer, masks, every):
-        grad = back + gain * ginn[STEP * b : STEP * b + STEP, :].astype(F32)
+    shift = base - STEP
+    for b, conv in filtered(ahead_ref[block, 0:WINDOW], prod, -base - 128, [chunks], masks, every):
+        inner = conv + gain * prod[128:144, :].astype(F32)
+        gmix[0, rows - shift : rows - shift + STEP, :] = (after * inner).astype(BF16).astype(F32)
+    outer.append(chunks)
+    for b, back in filtered(behind_ref[block, 0:WINDOW], ginn, -base, outer, masks, every):
+        at = slice(STEP * b, STEP * b + STEP)
+        to = slice(STEP * b - shift, STEP * b - shift + STEP)
+        grad = back + gain * ginn[STEP * b - base : STEP * b - base + STEP, :].astype(F32)
         grad = grad.astype(BF16).astype(F32)
-        put(1, b, grad * mixed(2, b))
-        put(2, b, grad * mixed(1, b))
-    for i, known in ((0, convs), (1, backs), (2, backs)):
-        put(i, known[0], near_gmix[i, 0:16, lanes])
-        put(i, known[-1], near_gmix[i, 16:32, lanes])
-
-    skip = jnp.zeros((STEP, LANES), F32)
-    for b in range(chunks):
-        p = prod[128 + STEP * b : 144 + STEP * b, :].astype(F32)
-        skip = skip + p * ginn[STEP * b : STEP * b + STEP, :].astype(F32)
+        for i, other in ((1, 2), (2, 1)):
+            value = end[other] if b == chunks else mixed_ref[other, at, lanes].astype(F32)
+            gmix[i, to, :] = (grad * value).astype(BF16).astype(F32)
+
+    skip = first_ref[0, :, lanes].astype(F32) * first_ref[1, :, lanes].astype(F32)
+    for lo in range(STEP, rows, STEP):
+        p = product_ref[lo : lo + STEP, lanes].astype(F32)
+        skip = skip + p * inner_ref[lo : lo + STEP, lanes].astype(F32)
     sums_ref[pl.ds(64 + step, 1), :] = jnp.sum(skip, axis=0, keepdims=True)
     total = None
     for r in range(STEP):
@@ -358,32 +425,40 @@
         total = line[:, 0:128] if total is None else total + line[:, 0:128]
     sums_ref[pl.ds(pl.multiple_of(GROUPS * step, GROUPS), GROUPS), :] = total
 
-    lines = []
-    for i, first in enumerate(settled(rows)):
-        totals = [None] * 7
-        todo = [(0, first), (first + 96, rows)]
-        for low, high in todo:
-            for lo in range(low, high, 48):
-                size = min(48, high - lo)
-                own = feat_ref[i, lo : lo + size, lanes].astype(F32)
-                grad_ref[i, lo : lo + size, :] = short_pass(
-                    gmix, i, own, weights, totals, lo, size
-                )
-        grad_ref[i, first : first + 96, :] = near_grad[i, :, lanes]
-        lines += [jnp.sum(part, axis=0, keepdims=True) for part in totals]
-        lines.append(jnp.zeros((1, LANES), F32))
-    lines = jnp.concatenate(lines, axis=0) + lines_ref[:, lanes]
+    totals = [[None] * 7 for _ in range(3)]
+    for i, known in enumerate(settled(rows)):
+        stop = known + 96
+        gmix[i, stop - shift : stop - shift + STEP, :] = near_gmix[i, 16:32, lanes].astype(F32)
+
+        def store(lo, size, grad):
+            grad_ref[i, lo : lo + size, :] = grad
+
+        finish(gmix, i, stop, rows, shift, feat_ref, lanes, weights, totals[i], store)
+        grad_ref[i, 0:known, :] = early_grad[i, 0:known, lanes]
+        grad_ref[i, known:stop, :] = near_grad[i, :, lanes]
+    lines = summed_lines(totals) + lines_ref[:, lanes]
     gather = iota((LANES, LANES), 1) == GROUPS * step + iota((LANES, LANES), 0) // 16
     gather = gather.astype(F32)
-    short = jnp.dot(lines, gather, precision=lax.Precision.HIGHEST, preferred_element_type=F32)
-
-    @pl.when(step == 0)
-    def _():
-        sums_ref[72:96, :] = short
-
-    @pl.when(step > 0)
-    def _():
-        sums_ref[72:96, :] += short
+    return jnp.dot(lines, gather, precision=lax.Precision.HIGHEST, preferred_element_type=F32)
+
+
+def before_kernel(*refs):
+    ins, (gated_ref, *outs), scratch = refs[:14], refs[14:19], refs[19:]
+    for u in range(TOGETHER):
+        gated = gated_ref.at[:, LANES * u : LANES * u + LANES]
+        step = TOGETHER * pl.program_id(0) + u
+        before_block(step, *ins, gated, *outs, *part(scratch, u))
+
+
+def after_kernel(*refs):
+    ins, (grad_ref, sums_ref), scratch = refs[:15], refs[15:17], refs[17:]
+    first = pl.program_id(0) == 0
+    short = jnp.where(first, 0.0, sums_ref[72:96, :])
+    for u in range(TOGETHER):
+        grad = grad_ref.at[:, :, LANES * u : LANES * u + LANES]
+        step = TOGETHER * pl.program_id(0) + u
+        short = short + after_block(step, *ins, grad, sums_ref, *part(scratch, u))
+    sums_ref[72:96, :] = short
 
 
 def final_kernel(group_scale, token_scale, sums_ref, short_ref, long_ref, skip_ref):
@@ -396,11 +471,11 @@
 
 
 def blocks3(rows):
-    return pl.BlockSpec((3, rows, LANES), lambda b: (0, 0, b))
+    return pl.BlockSpec((3, rows, TOGETHER * LANES), lambda b: (0, 0, b))
 
 
 def blocks2(rows):
-    return pl.BlockSpec((rows, LANES), lambda b: (0, b))
+    return pl.BlockSpec((rows, TOGETHER * LANES), lambda b: (0, b))
 
 
 def swap(values, axes):
@@ -446,21 +521,21 @@
     def held(*dims, dtype=BF16):
         return inside_vmem, shape(dims, dtype)
 
-    up, down, taps = call(
+    up, down = call(
         edge_kernel,
         "edge",
         [outside] * 3,
         [
             held(160, width),
             held(160, width),
-            held(24, width, dtype=F32),
         ],
         [
+            pltpu.VMEM((24, width), F32),
             pltpu.VMEM((3, 144, width), BF16),
             pltpu.VMEM((3, 144, width), BF16),
             pltpu.VMEM((144, width), BF16),
             pltpu.VMEM(short_taps.shape, BF16),
-            pltpu.VMEM((3, 152, LANES), F32),
+            pltpu.VMEM((AT_EDGE, 3, 152, LANES), F32),
             pltpu.SemaphoreType.DMA((8,)),
         ],
         5 * 10**6,
@@ -470,50 +545,74 @@
     from_next = passed_along(down, CTX, -1)
     convs, backs = inside(rows)
     gain = skip_gain.reshape(1, width)
-    near = call(
+    mixers = [
+        held(24, width, dtype=F32),
+        held(3, rows, width),
+        held(rows, width),
+        held(rows, width),
+        held(groups * 16, 256),
+        held(groups * 16, 256),
+    ]
+    sums_so_far = [held(24, width, dtype=F32), held(groups * 16, 256, dtype=F32)]
+    taps, mixed, product, inner, ahead, behind, near_gated, near_grad, near_gmix, *parts = call(
         local_kernel,
         "local",
         [inside_vmem] * 5,
-        [
-            held(3, rows, width),
-            held(rows, width),
-            held(rows, width),
-            held(groups * 16, 256),
-            held(groups * 16, 256),
-            held(STEP * len(convs), width),
-            held(3, 96, width),
-            held(3, 32, width),
-            held(24, width, dtype=F32),
-            held(groups * 16, 256, dtype=F32),
-        ],
-        [
-            pltpu.VMEM((3, rows + 8, LANES), F32),
+        mixers
+        + [held(STEP * len(convs), width), held(3, 96, width), held(3, 32, width)]
+        + sums_so_far,
+        [
+            pltpu.VMEM((AT_LOCAL, 3, rows + 8, LANES), F32),
             pltpu.VMEM((2, groups, 256), F32),
-            pltpu.VMEM((2, 2, 128, LANES), F32),
-            pltpu.VMEM((3, STEP * len(convs), LANES), F32),
+            pltpu.VMEM((AT_LOCAL, 2, 2, 128, LANES), F32),
+            pltpu.VMEM((AT_LOCAL, 3, STEP * len(convs), LANES), F32),
         ],
         2 * 10**7,
-    )(features, cotangent, taps, long_taps, gain)
-    gated, feature_grad, sums = call(
-        main_kernel,
-        "main",
-        [inside_vmem] * 16,
+    )(features, cotangent, short_taps, long_taps, gain)
+    most = STEP * convs[0]
+    gated, first, early_grad, *parts = call(
+        before_kernel,
+        "before",
+        [inside_vmem] * 14,
         [
             (blocks2(rows), shape((rows, width), BF16)),
+            held(2, STEP, width),
+            held(3, most, width),
+        ]
+        + sums_so_far,
+        [
+            pltpu.VMEM((TOGETHER, 272, LANES), BF16),
+            pltpu.VMEM((TOGETHER, WINDOW, LANES), BF16),
+            pltpu.VMEM((TOGETHER, 3, most + STEP, LANES), F32),
+            pltpu.VMEM((TOGETHER, 3, 24, LANES), F32),
+        ],
+        10**7,
+        (steps // TOGETHER,),
+    )(
+        features, cotangent, taps, gain, mixed, product, inner, ahead, behind, near_gated, near_gmix,
+        *parts, from_last,
+    )
+    feature_grad, sums = call(
+        after_kernel,
+        "after",
+        [inside_vmem] * 15,
+        [
             (blocks3(rows), shape((3, rows, width), BF16)),
             (inside_vmem, shape((96, LANES), F32)),
         ],
         [
-            pltpu.VMEM((rows + 144, LANES), BF16),
-            pltpu.VMEM((rows + 144, LANES), BF16),
-            pltpu.VMEM((3, rows + 16, LANES), F32),
-            pltpu.VMEM((3, 48, LANES), F32),
-            pltpu.VMEM((4, 32, LANES), F32),
-            pltpu.VMEM((2, 128, LANES), F32),
+            pltpu.VMEM((TOGETHER, WINDOW, LANES), BF16),
+            pltpu.VMEM((TOGETHER, 272, LANES), BF16),
+            pltpu.VMEM((TOGETHER, 3, 160, LANES), F32),
+            pltpu.VMEM((TOGETHER, 3, 24, LANES), F32),
+            pltpu.VMEM((TOGETHER, 2, 128, LANES), F32),
         ],
-        2 * 10**7,
-        (steps,),
-    )(features, cotangent, taps, gain, *near, from_last, from_next)
+        10**7,
+        (steps // TOGETHER,),
+    )(
+        features, taps, gain, mixed, product, inner, ahead, behind, near_grad, near_gmix, first,
+        early_grad, *parts, from_next,
+    )
     tokens = rows * lax.axis_size(CTX)
     group_scale = 1.0 / math.sqrt(16.0 * tokens)
     token_scale = 1.0 / math.sqrt(1.0 * tokens)

time: 73.5 us -> 71.5 us (0.973)
  waiting for transfers between devices: 2.79 us -> 0.01 us
  blocking collectives: 45 us -> 45.8 us
    ppermute x2, waiting for transfers between devices: 2.79 us -> 0.01 us  [passed_along(): return lax.ppermute(block, axis, route)]
    pallas_call x2 -> x3, Pallas kernels: 14.1 us -> 15.1 us  [the longest x1 6.21 us: body(): call(local_kernel, 'local', [inside_vmem] * 5, mixers + [held(STEP * len(...]
    pallas_call x1, Pallas kernels: 4.21 us -> 3.39 us  [body(): call(edge_kernel, 'edge', [outside] * 3, [held(160, width), held(160, wid...]
    all_to_all x3, blocking collectives: 45 us -> 45.8 us  [swap(): return lax.all_to_all(values, axes, 0, 0, tiled=True)]
  transfers between devices with their start and end apart: 2 -> 2, of which waited for: 1 -> 0; matrix products, arithmetic and copies ran while one was open for 0% -> 0% of each run, Pallas kernels for 9% -> 13%
where the time goes in v4:
time: 71.5 us; the launch traced here: 71.2 us
  blocking collectives  45.8 us (64%)
  Pallas kernels  19.1 us (27%)
  starting transfers between devices  4.79 us (7%)
  between operations  0.76 us (1%)
  local copies, waits for them, and re-layouts  0.75 us (1%)
    all_to_all x3, blocking collectives, swap(): return lax.all_to_all(values, axes, 0, 0, tiled=True)  45.8 us
    pallas_call x1, Pallas kernels, body(): call(local_kernel, 'local', [inside_vmem] * 5, mixers + [held(STEP * len(...  6.21 us
    pallas_call x1, Pallas kernels, body(): call(after_kernel, 'after', [inside_vmem] * 15, [(blocks3(rows), shape((3...  5.82 us
    ppermute x2, starting transfers between devices, passed_along(): return lax.ppermute(block, axis, route)  4.79 us
    pallas_call x1, Pallas kernels, body(): call(edge_kernel, 'edge', [outside] * 3, [held(160, width), held(160, wid...  3.39 us
    pallas_call x1, Pallas kernels, body(): call(before_kernel, 'before', [inside_vmem] * 14, [(blocks2(rows), shape(...  3.07 us
  transfers between devices with their start and end apart: 2, of which 0 were waited for; matrix products, arithmetic and copies ran while one was open for 0% of the time, Pallas kernels for 13%

profile of v4, /device:TPU:192, one launch (start us, length us, event | category | flops | bytes accessed | tf_op | source)
XLA Modules:
  0.0 71.2 jit_solution(3423780727915375542)
XLA Ops:
  0.6 0.0 copy-start
  0.6 0.0 copy-start.1
  0.7 0.0 copy-start.2
  0.7 0.0 copy-start.4
  0.7 3.4 %edge.1 = (bf16[160,1024]{1,0:T(8,128)(2,1)}, bf16[160,1024]{1,0:T(8,128)(2,1)}) custom-call(bf16[3,256,1024]{2,1,0:T(8,128)(2,1)} %refs_0_.3, bf16[256,1024]{1,0:T(8,128)(2,1)} %refs_1_.1, bf16[3,7,64]{2,1,0:T(8,128)(2,1)} %bitcast.7), custom_call_target="tpu_custom_call" | custom-call | flops 5000000 | bytes 5000000 | tf_op jit(solution)/shard_map/edge/pallas_call | solution.py:524
  4.1 3.5 %collective-permute-start = (bf16[160,1024]{1,0:T(8,128)(2,1)}, bf16[160,1024]{1,0:T(8,128)(2,1)S(1)}, u32[]{:S(2)}, u32[]{:S(2)}) collective-permute-start(bf16[160,1024]{1,0:T(8,128)(2,1)} %get-tuple-element.38), channel_id=1, source_target_pairs={{0,8},{8,16},{16,24},{24,32},{32,40},{40,48},{48,56},{56,64},{64,7... | collective-permute-start | bytes 983048 | tf_op jit(solution)/shard_map/ppermute | solution.py:28
  7.6 1.3 %collective-permute-start.1 = (bf16[160,1024]{1,0:T(8,128)(2,1)}, bf16[160,1024]{1,0:T(8,128)(2,1)S(1)}, u32[]{:S(2)}, u32[]{:S(2)}) collective-permute-start(bf16[160,1024]{1,0:T(8,128)(2,1)} %get-tuple-element.45), channel_id=1, source_target_pairs={{8,0},{16,8},{24,16},{32,24},{40,32},{48,40},{56,48},{64,56},{72,6... | collective-permute-start | bytes 983048 | tf_op jit(solution)/shard_map/ppermute | solution.py:28
  8.9 0.0 copy-done.4
  8.9 0.0 copy-done
  8.9 0.0 copy-done.1
  8.9 0.0 copy-done.2
  8.9 0.0 copy-start.3
  8.9 0.7 copy-done.3
  9.6 6.2 %local.1 = (f32[24,1024]{1,0:T(8,128)S(1)}, bf16[3,256,1024]{2,1,0:T(8,128)(2,1)S(1)}, bf16[256,1024]{1,0:T(8,128)(2,1)S(1)}, bf16[256,1024]{1,0:T(8,128)(2,1)S(...) custom-call(bf16[3,256,1024]{2,1,0:T(8,128)(2,1)S(1)} %copy-done, ...), custom_call_target="tpu_custom_call" | custom-call | flops 20000000 | bytes 20000000 | tf_op jit(solution)/shard_map/local/pallas_call | solution.py:557
  15.9 0.0 collective-permute-done.refs_13_
  15.9 3.1 %before.1 = (bf16[256,1024]{1,0:T(8,128)(2,1)}, bf16[2,16,1024]{2,1,0:T(8,128)(2,1)S(1)}, bf16[3,144,1024]{2,1,0:T(8,128)(2,1)S(1)}, f32[24,1024]{1,0:T(8,128)S(1)}, f32[1024,256]{1,0:T(8,128)S(1)}) custom-call(bf16[3,256,1024]{2,1,0:T(8,128)(2,1)S(1)} %copy-done, bf16[256,1024]{1,0:T(8,128)(2,1)S(1)} %copy-done.1, ...), custom_call_target="tpu_custom_call" | custom-call | flops 10000000 | bytes 10000000 | tf_op jit(solution)/shard_map/before/pallas_call | solution.py:573
  18.9 0.0 collective-permute-done.1.refs_14_
  18.9 5.8 %after.1 = (bf16[3,256,1024]{2,1,0:T(8,128)(2,1)}, f32[96,128]{1,0:T(8,128)S(1)}) custom-call(bf16[3,256,1024]{2,1,0:T(8,128)(2,1)S(1)} %copy-done, f32[24,1024]{1,0:T(8,128)S(1)} %get-tuple-element.28.refs_2_.refs_1_, bf16[1,1024]{1,0:T(2,128)(2,1)S(1)} %reshape.24.gain_ref.refs_3_.refs_2_, bf16[3,256,1024]{2,1,0:T(8,128)(2,1)S(1)} %get-tuple-element.29.refs_4_.refs_3_, ...), custom_call_target="tpu_custom_call" | custom-call | flops 10000000 | bytes 10000000 | tf_op jit(solution)/shard_map/after/pallas_call | solution.py:595
  24.8 20.7 %all_to_all.15 = f32[12,8,128]{2,1,0:T(8,128)S(1)} all-to-all(f32[12,8,128]{2,1,0:T(8,128)S(1)} %bitcast.6), channel_id=1, replica_groups=mesh['ctx_0'=4,'ctx_1'=3,'ctx_2'=8,'tp'=8] {'ctx_0','ctx_1'}, dimensions={0} | all-to-all | bytes 98304 | tf_op jit(solution)/shard_map/all_to_all | solution.py:482
  45.5 14.0 %all_to_all.16 = f32[8,8,128]{2,1,0:T(8,128)S(1)} all-to-all(f32[8,8,128]{2,1,0:T(8,128)S(1)} %broadcast_in_dim.4), channel_id=1, replica_groups=mesh['ctx_0'=4,'ctx_1'=3,'ctx_2'=8,'tp'=8] {'ctx_2'}, dimensions={0} | all-to-all | bytes 65536 | tf_op jit(solution)/shard_map/all_to_all | solution.py:482
  59.5 11.1 %all_to_all.17 = f32[12,8,128]{2,1,0:T(8,128)S(1)} all-to-all(f32[12,8,128]{2,1,0:T(8,128)S(1)} %broadcast_in_dim.5), channel_id=1, replica_groups=mesh['ctx_0'=4,'ctx_1'=3,'ctx_2'=8,'tp'=8] {'ctx_0','ctx_1'}, dimensions={0} | all-to-all | bytes 98304 | tf_op jit(solution)/shard_map/all_to_all | solution.py:482
  70.6 0.6 final.1
  (5 shorter events, 0.0 us)
Async XLA Ops:
  0.6 8.3 %copy-start = (bf16[3,256,1024]{2,1,0:T(8,128)(2,1)S(1)}, bf16[3,256,1024]{2,1,0:T(8,128)(2,1)}, u32[]{:S(2)}) copy-start(bf16[3,256,1024]{2,1,0:T(8,128)(2,1)} %refs_0_.3) | copy-start | bytes 4718596
  0.6 8.3 %copy-start.1 = (bf16[256,1024]{1,0:T(8,128)(2,1)S(1)}, bf16[256,1024]{1,0:T(8,128)(2,1)}, u32[]{:S(2)}) copy-start(bf16[256,1024]{1,0:T(8,128)(2,1)} %refs_1_.1) | copy-start | bytes 1572868
  0.7 8.3 %copy-start.2 = (bf16[3,64,7]{1,2,0:T(8,128)(2,1)S(1)}, bf16[3,64,7]{1,2,0:T(8,128)(2,1)}, u32[]{:S(2)}) copy-start(bf16[3,64,7]{1,2,0:T(8,128)(2,1)} %param.6) | copy-start | bytes 8068
  0.7 8.2 %copy-start.4 = (bf16[1024]{0:T(1024)(128)(2,1)S(1)}, bf16[1024]{0:T(1024)(128)(2,1)}, u32[]{:S(2)}) copy-start(bf16[1024]{0:T(1024)(128)(2,1)} %param.8) | copy-start | bytes 6148
  4.1 11.8 %collective-permute-start = (bf16[160,1024]{1,0:T(8,128)(2,1)}, bf16[160,1024]{1,0:T(8,128)(2,1)S(1)}, u32[]{:S(2)}, u32[]{:S(2)}) collective-permute-start(bf16[160,1024]{1,0:T(8,128)(2,1)} %get-tuple-element.38), channel_id=1, source_target_pairs={{0,8},{8,16},{16,24},{24,32},{32,40},{40,48},{48,56},{56,64},{64,7... | collective-permute-start | bytes 983048 | tf_op jit(solution)/shard_map/ppermute | solution.py:28
  7.6 11.4 %collective-permute-start.1 = (bf16[160,1024]{1,0:T(8,128)(2,1)}, bf16[160,1024]{1,0:T(8,128)(2,1)S(1)}, u32[]{:S(2)}, u32[]{:S(2)}) collective-permute-start(bf16[160,1024]{1,0:T(8,128)(2,1)} %get-tuple-element.45), channel_id=1, source_target_pairs={{8,0},{16,8},{24,16},{32,24},{40,32},{48,40},{56,48},{64,56},{72,6... | collective-permute-start | bytes 983048 | tf_op jit(solution)/shard_map/ppermute | solution.py:28
  8.9 0.7 %copy-start.3 = (bf16[64,128]{1,0:T(8,128)(2,1)S(1)}, bf16[64,128]{1,0:T(8,128)(2,1)}, u32[]{:S(2)}) copy-start(bf16[64,128]{1,0:T(8,128)(2,1)} %long_ref.1) | copy-start | bytes 49156

commit v5 on v4

--- a/solution.py
+++ b/solution.py
@@ -33,6 +33,8 @@
 
 
 def lanes_of(step):
+    if isinstance(step, int):
+        return pl.ds(LANES * step, LANES)
     return pl.ds(pl.multiple_of(LANES * step, LANES), LANES)
 
 
@@ -119,9 +121,11 @@
 
 
 def edge_kernel(
-    feat_hbm, cot_hbm, taps_hbm, up_ref, down_ref, taps, opens, closes, cot_ref, taps_ref, raws, sems,
+    feat_hbm, cot_hbm, taps_hbm, up_hbm, down_hbm,
+    up_ref, down_ref, taps, opens, closes, cot_ref, taps_ref, raws, sems, out_sems,
 ):
-    rows = cot_hbm.shape[0]
+    rows, width = cot_hbm.shape
+    span = AT_EDGE * LANES
 
     def block(step, raw):
         lanes = lanes_of(step)
@@ -150,36 +154,54 @@
         begin = [opens[i, 0:16, lanes].astype(F32)[0:8] for i in range(3)]
         down_ref[128:160, lanes] = jnp.concatenate([rest] + begin, axis=0).astype(BF16)
 
-    pairs = [
-        (taps_hbm, taps_ref),
-        (feat_hbm.at[1, rows - 144 : rows], closes.at[1]),
-        (feat_hbm.at[2, rows - 144 : rows], closes.at[2]),
-        (feat_hbm.at[0, 0:144], opens.at[0]),
-        (cot_hbm.at[0:144], cot_ref),
-        (feat_hbm.at[0, rows - 16 : rows], closes.at[0, 128:144]),
-        (feat_hbm.at[1, 0:16], opens.at[1, 0:16]),
-        (feat_hbm.at[2, 0:16], opens.at[2, 0:16]),
-    ]
-    copies = [
-        pltpu.make_async_copy(source, target, sems.at[n])
-        for n, (source, target) in enumerate(pairs)
-    ]
-    for copy in copies:
-        copy.start()
-    copies[0].wait()
+    def fetches(at):
+        lanes = pl.ds(span * at, span)
+        pairs = [
+            (feat_hbm.at[1, rows - 144 : rows, lanes], closes.at[1, :, lanes]),
+            (feat_hbm.at[2, rows - 144 : rows, lanes], closes.at[2, :, lanes]),
+            (feat_hbm.at[0, 0:144, lanes], opens.at[0, :, lanes]),
+            (cot_hbm.at[0:144, lanes], cot_ref.at[:, lanes]),
+            (feat_hbm.at[0, rows - 16 : rows, lanes], closes.at[0, 128:144, lanes]),
+            (feat_hbm.at[1, 0:16, lanes], opens.at[1, 0:16, lanes]),
+            (feat_hbm.at[2, 0:16, lanes], opens.at[2, 0:16, lanes]),
+        ]
+        return [
+            pltpu.make_async_copy(source, target, sems.at[at, n])
+            for n, (source, target) in enumerate(pairs)
+        ]
+
+    def stores(at):
+        lanes = pl.ds(span * at, span)
+        return [
+            pltpu.make_async_copy(up_ref.at[:, lanes], up_hbm.at[:, lanes], out_sems.at[at, 0]),
+            pltpu.make_async_copy(
+                down_ref.at[:, lanes], down_hbm.at[:, lanes], out_sems.at[at, 1]
+            ),
+        ]
+
+    turns = range(width // span)
+    first = pltpu.make_async_copy(taps_hbm, taps_ref, sems.at[0, 7])
+    first.start()
+    for at in turns:
+        for copy in fetches(at):
+            copy.start()
+    first.wait()
     channel_taps(taps_ref, taps)
-    for copy in copies[1:]:
-        copy.wait()
-
-    @pl.loop(0, cot_ref.shape[1] // LANES // AT_EDGE)
-    def _(step):
+    for at in turns:
+        for copy in fetches(at):
+            copy.wait()
         for u in range(AT_EDGE):
-            block(AT_EDGE * step + u, raws.at[u])
+            block(AT_EDGE * at + u, raws.at[u])
+        for copy in stores(at):
+            copy.start()
+    for at in turns:
+        for copy in stores(at):
+            copy.wait()
 
 
 def local_kernel(
     feat_ref, cot_ref, taps_ref, long_ref, gain_ref,
-    taps_out, mixed_ref, product_ref, inner_ref, ahead_ref, behind_ref,
+    taps_out, gain_out, mixed_ref, product_ref, inner_ref, ahead_ref, behind_ref,
     gated_ref, grad_ref, gmix_ref, lines_ref, grid_ref,
     raws, filt, spreads, gmixes,
 ):
@@ -192,11 +214,12 @@
     filt[1, :, 128:256] = jnp.zeros((groups, 128), F32)
 
     channel_taps(taps_ref, taps_out)
+    gain_out[...] = gain_ref[...].astype(F32)
 
     def one(step, raw, spread, gmix):
         lanes = lanes_of(step)
         block = pl.ds(pl.multiple_of(LANES * step, LANES), LANES)
-        gain = gain_ref[:, lanes].astype(F32)
+        gain = gain_out[pl.ds(step, 1), :]
         weights = taps_out[:, lanes]
         for which, out in ((0, ahead_ref), (1, behind_ref)):
             base = filt[which, pl.ds(pl.multiple_of(GROUPS * step, GROUPS), GROUPS), :]
@@ -298,7 +321,7 @@
     block = pl.ds(pl.multiple_of(LANES * step, LANES), LANES)
     every = pl.ds(0, LANES)
     weights = taps_ref[:, lanes]
-    gain = gain_ref[:, lanes].astype(F32)
+    gain = gain_ref[pl.ds(step, 1), :]
     masks = group_masks()
     keep = [m.astype(F32).astype(BF16) for m in masks]
     convs, backs = inside(rows)
@@ -360,7 +383,7 @@
     block = pl.ds(pl.multiple_of(LANES * step, LANES), LANES)
     every = pl.ds(0, LANES)
     weights = taps_ref[:, lanes]
-    gain = gain_ref[:, lanes].astype(F32)
+    gain = gain_ref[pl.ds(step, 1), :]
     masks = group_masks()
     keep = [m.astype(F32).astype(BF16) for m in masks]
     convs, backs = inside(rows)
@@ -525,18 +548,18 @@
         edge_kernel,
         "edge",
         [outside] * 3,
+        [(outside, shape((160, width), BF16)), (outside, shape((160, width), BF16))],
         [
-            held(160, width),
-            held(160, width),
-        ],
-        [
+            pltpu.VMEM((160, width), BF16),
+            pltpu.VMEM((160, width), BF16),
             pltpu.VMEM((24, width), F32),
             pltpu.VMEM((3, 144, width), BF16),
             pltpu.VMEM((3, 144, width), BF16),
             pltpu.VMEM((144, width), BF16),
             pltpu.VMEM(short_taps.shape, BF16),
             pltpu.VMEM((AT_EDGE, 3, 152, LANES), F32),
-            pltpu.SemaphoreType.DMA((8,)),
+            pltpu.SemaphoreType.DMA((steps // AT_EDGE, 8)),
+            pltpu.SemaphoreType.DMA((steps // AT_EDGE, 2)),
         ],
         5 * 10**6,
         limit=EDGE_LIMIT,
@@ -544,9 +567,10 @@
     from_last = passed_along(up, CTX, 1)
     from_next = passed_along(down, CTX, -1)
     convs, backs = inside(rows)
-    gain = skip_gain.reshape(1, width)
+    gain = skip_gain.reshape(steps, LANES)
     mixers = [
         held(24, width, dtype=F32),
+        held(steps, LANES, dtype=F32),
         held(3, rows, width),
         held(rows, width),
         held(rows, width),
@@ -554,7 +578,7 @@
         held(groups * 16, 256),
     ]
     sums_so_far = [held(24, width, dtype=F32), held(groups * 16, 256, dtype=F32)]
-    taps, mixed, product, inner, ahead, behind, near_gated, near_grad, near_gmix, *parts = call(
+    taps, scale, *mixers_out, near_gated, near_grad, near_gmix, lines, grid = call(
         local_kernel,
         "local",
         [inside_vmem] * 5,
@@ -589,8 +613,7 @@
         10**7,
         (steps // TOGETHER,),
     )(
-        features, cotangent, taps, gain, mixed, product, inner, ahead, behind, near_gated, near_gmix,
-        *parts, from_last,
+        features, cotangent, taps, scale, *mixers_out, near_gated, near_gmix, lines, grid, from_last,
     )
     feature_grad, sums = call(
         after_kernel,
@@ -610,8 +633,7 @@
         10**7,
         (steps // TOGETHER,),
     )(
-        features, taps, gain, mixed, product, inner, ahead, behind, near_grad, near_gmix, first,
-        early_grad, *parts, from_next,
+        features, taps, scale, *mixers_out, near_grad, near_gmix, first, early_grad, *parts, from_next,
     )
     tokens = rows * lax.axis_size(CTX)
     group_scale = 1.0 / math.sqrt(16.0 * tokens)

time: 71.5 us -> 71.4 us (level)
  no operation moved by 1% of the time
where the time goes in v5:
time: 71.4 us; the launch traced here: 71 us
  blocking collectives  45.7 us (64%)
  Pallas kernels  19 us (27%)
  starting transfers between devices  4.79 us (7%)
  between operations  0.75 us (1%)
  local copies, waits for them, and re-layouts  0.74 us (1%)
    all_to_all x3, blocking collectives, swap(): return lax.all_to_all(values, axes, 0, 0, tiled=True)  45.7 us
    pallas_call x1, Pallas kernels, body(): call(local_kernel, 'local', [inside_vmem] * 5, mixers + [held(STEP * len(...  6.24 us
    pallas_call x1, Pallas kernels, body(): call(after_kernel, 'after', [inside_vmem] * 15, [(blocks3(rows), shape((3...  5.82 us
    ppermute x2, starting transfers between devices, passed_along(): return lax.ppermute(block, axis, route)  4.79 us
    pallas_call x1, Pallas kernels, body(): call(edge_kernel, 'edge', [outside] * 3, [(outside, shape((160, width), B...  3.25 us
    pallas_call x1, Pallas kernels, body(): call(before_kernel, 'before', [inside_vmem] * 14, [(blocks2(rows), shape(...  3.04 us
  transfers between devices with their start and end apart: 2, of which 0 were waited for; matrix products, arithmetic and copies ran while one was open for 0% of the time, Pallas kernels for 13%

profile of v5, /device:TPU:192, one launch (start us, length us, event | category | flops | bytes accessed | tf_op | source)
XLA Modules:
  0.0 71.0 jit_solution(1138126126867066812)
XLA Ops:
  0.6 0.0 copy-start
  0.6 0.0 copy-start.1
  0.7 0.0 copy-start.2
  0.7 0.0 copy-start.4
  0.7 3.2 %edge.1 = (bf16[160,1024]{1,0:T(8,128)(2,1)}, bf16[160,1024]{1,0:T(8,128)(2,1)}) custom-call(bf16[3,256,1024]{2,1,0:T(8,128)(2,1)} %refs_0_.3, bf16[256,1024]{1,0:T(8,128)(2,1)} %refs_1_.1, bf16[3,7,64]{2,1,0:T(8,128)(2,1)} %bitcast.8), custom_call_target="tpu_custom_call" | custom-call | flops 5000000 | bytes 5000000 | tf_op jit(solution)/shard_map/edge/pallas_call | solution.py:547
  3.9 3.5 %collective-permute-start = (bf16[160,1024]{1,0:T(8,128)(2,1)}, bf16[160,1024]{1,0:T(8,128)(2,1)S(1)}, u32[]{:S(2)}, u32[]{:S(2)}) collective-permute-start(bf16[160,1024]{1,0:T(8,128)(2,1)} %get-tuple-element.40), channel_id=1, source_target_pairs={{0,8},{8,16},{16,24},{24,32},{32,40},{40,48},{48,56},{56,64},{64,7... | collective-permute-start | bytes 983048 | tf_op jit(solution)/shard_map/ppermute | solution.py:28
  7.4 1.3 %collective-permute-start.1 = (bf16[160,1024]{1,0:T(8,128)(2,1)}, bf16[160,1024]{1,0:T(8,128)(2,1)S(1)}, u32[]{:S(2)}, u32[]{:S(2)}) collective-permute-start(bf16[160,1024]{1,0:T(8,128)(2,1)} %get-tuple-element.47), channel_id=1, source_target_pairs={{8,0},{16,8},{24,16},{32,24},{40,32},{48,40},{56,48},{64,56},{72,6... | collective-permute-start | bytes 983048 | tf_op jit(solution)/shard_map/ppermute | solution.py:28
  8.7 0.0 copy-done
  8.7 0.0 copy-done.1
  8.8 0.0 copy-done.2
  8.8 0.0 copy-done.4
  8.8 0.0 copy-start.3
  8.8 0.7 copy-done.3
  9.5 6.2 %local.1 = (f32[24,1024]{1,0:T(8,128)S(1)}, f32[8,128]{1,0:T(8,128)S(1)}, bf16[3,256,1024]{2,1,0:T(8,128)(2,1)S(1)}, bf16[256,1024]{1,0:T(8,128)(2,1)S(1)}, bf16...) custom-call(bf16[3,256,1024]{2,1,0:T(8,128)(2,1)S(1)} %copy-done, ...), custom_call_target="tpu_custom_call" | custom-call | flops 20000000 | bytes 20000000 | tf_op jit(solution)/shard_map/local/pallas_call | solution.py:581
  15.7 0.0 collective-permute-done.refs_13_
  15.8 3.0 %before.1 = (bf16[256,1024]{1,0:T(8,128)(2,1)}, bf16[2,16,1024]{2,1,0:T(8,128)(2,1)S(1)}, bf16[3,144,1024]{2,1,0:T(8,128)(2,1)S(1)}, f32[24,1024]{1,0:T(8,128)S(1)}, f32[1024,256]{1,0:T(8,128)S(1)}) custom-call(bf16[3,256,1024]{2,1,0:T(8,128)(2,1)S(1)} %copy-done, bf16[256,1024]{1,0:T(8,128)(2,1)S(1)} %copy-done.1, ...), custom_call_target="tpu_custom_call" | custom-call | flops 10000000 | bytes 10000000 | tf_op jit(solution)/shard_map/before/pallas_call | solution.py:597
  18.8 0.0 collective-permute-done.1.refs_14_
  18.8 5.8 %after.1 = (bf16[3,256,1024]{2,1,0:T(8,128)(2,1)}, f32[96,128]{1,0:T(8,128)S(1)}) custom-call(bf16[3,256,1024]{2,1,0:T(8,128)(2,1)S(1)} %copy-done, f32[24,1024]{1,0:T(8,128)S(1)} %get-tuple-element.29.refs_2_.refs_1_, f32[8,128]{1,0:T(8,128)S(1)} %get-tuple-element.30.refs_3_.refs_2_, bf16[3,256,1024]{2,1,0:T(8,128)(2,1)S(1)} %get-tuple-element.31.refs_4_.refs_3_, ...), custom_call_target="tpu_custom_call" | custom-call | flops 10000000 | bytes 10000000 | tf_op jit(solution)/shard_map/after/pallas_call | solution.py:618
  24.6 20.7 %all_to_all.15 = f32[12,8,128]{2,1,0:T(8,128)S(1)} all-to-all(f32[12,8,128]{2,1,0:T(8,128)S(1)} %bitcast.7), channel_id=1, replica_groups=mesh['ctx_0'=4,'ctx_1'=3,'ctx_2'=8,'tp'=8] {'ctx_0','ctx_1'}, dimensions={0} | all-to-all | bytes 98304 | tf_op jit(solution)/shard_map/all_to_all | solution.py:505
  45.3 14.0 %all_to_all.16 = f32[8,8,128]{2,1,0:T(8,128)S(1)} all-to-all(f32[8,8,128]{2,1,0:T(8,128)S(1)} %broadcast_in_dim.4), channel_id=1, replica_groups=mesh['ctx_0'=4,'ctx_1'=3,'ctx_2'=8,'tp'=8] {'ctx_2'}, dimensions={0} | all-to-all | bytes 65536 | tf_op jit(solution)/shard_map/all_to_all | solution.py:505
  59.4 11.1 %all_to_all.17 = f32[12,8,128]{2,1,0:T(8,128)S(1)} all-to-all(f32[12,8,128]{2,1,0:T(8,128)S(1)} %broadcast_in_dim.5), channel_id=1, replica_groups=mesh['ctx_0'=4,'ctx_1'=3,'ctx_2'=8,'tp'=8] {'ctx_0','ctx_1'}, dimensions={0} | all-to-all | bytes 98304 | tf_op jit(solution)/shard_map/all_to_all | solution.py:505
  70.4 0.6 final.1
  (4 shorter events, 0.0 us)
Async XLA Ops:
  0.6 8.1 %copy-start = (bf16[3,256,1024]{2,1,0:T(8,128)(2,1)S(1)}, bf16[3,256,1024]{2,1,0:T(8,128)(2,1)}, u32[]{:S(2)}) copy-start(bf16[3,256,1024]{2,1,0:T(8,128)(2,1)} %refs_0_.3) | copy-start | bytes 4718596
  0.6 8.1 %copy-start.1 = (bf16[256,1024]{1,0:T(8,128)(2,1)S(1)}, bf16[256,1024]{1,0:T(8,128)(2,1)}, u32[]{:S(2)}) copy-start(bf16[256,1024]{1,0:T(8,128)(2,1)} %refs_1_.1) | copy-start | bytes 1572868
  0.7 8.1 %copy-start.2 = (bf16[3,64,7]{1,2,0:T(8,128)(2,1)S(1)}, bf16[3,64,7]{1,2,0:T(8,128)(2,1)}, u32[]{:S(2)}) copy-start(bf16[3,64,7]{1,2,0:T(8,128)(2,1)} %param.6) | copy-start | bytes 8068
  0.7 8.1 %copy-start.4 = (bf16[1024]{0:T(1024)(128)(2,1)S(1)}, bf16[1024]{0:T(1024)(128)(2,1)}, u32[]{:S(2)}) copy-start(bf16[1024]{0:T(1024)(128)(2,1)} %param.8) | copy-start | bytes 6148
  3.9 11.8 %collective-permute-start = (bf16[160,1024]{1,0:T(8,128)(2,1)}, bf16[160,1024]{1,0:T(8,128)(2,1)S(1)}, u32[]{:S(2)}, u32[]{:S(2)}) collective-permute-start(bf16[160,1024]{1,0:T(8,128)(2,1)} %get-tuple-element.40), channel_id=1, source_target_pairs={{0,8},{8,16},{16,24},{24,32},{32,40},{40,48},{48,56},{56,64},{64,7... | collective-permute-start | bytes 983048 | tf_op jit(solution)/shard_map/ppermute | solution.py:28
  7.4 11.4 %collective-permute-start.1 = (bf16[160,1024]{1,0:T(8,128)(2,1)}, bf16[160,1024]{1,0:T(8,128)(2,1)S(1)}, u32[]{:S(2)}, u32[]{:S(2)}) collective-permute-start(bf16[160,1024]{1,0:T(8,128)(2,1)} %get-tuple-element.47), channel_id=1, source_target_pairs={{8,0},{16,8},{24,16},{32,24},{40,32},{48,40},{56,48},{64,56},{72,6... | collective-permute-start | bytes 983048 | tf_op jit(solution)/shard_map/ppermute | solution.py:28
  8.8 0.7 %copy-start.3 = (bf16[64,128]{1,0:T(8,128)(2,1)S(1)}, bf16[64,128]{1,0:T(8,128)(2,1)}, u32[]{:S(2)}) copy-start(bf16[64,128]{1,0:T(8,128)(2,1)} %long_ref.1) | copy-start | bytes 49156

commit v6 on v5

--- a/solution.py
+++ b/solution.py
@@ -18,7 +18,8 @@
 BF16 = jnp.bfloat16
 F32 = jnp.float32
 LIMIT = 16 * 2**20
-TOGETHER, AT_EDGE, AT_LOCAL = 2, 4, 1
+TOGETHER, AT_EDGE, AT_LOCAL = 4, 4, 1
+LAG_LOCAL, LAG_BEFORE, LAG_AFTER = 1000, 4, 8
 EDGE_LIMIT = 60000 * 2**10
 
 
@@ -46,6 +47,22 @@
         out_ref[8 * i : 8 * i + 7, :] = jnp.dot(
             taps_ref[i], spread, preferred_element_type=F32
         )
+
+
+def staggered(blocks, lag):
+    waiting, running, results = list(enumerate(blocks)), [], [None] * len(blocks)
+    stage = 0
+    while waiting or running:
+        if waiting and (stage % lag == 0 or not running):
+            running.append(waiting.pop(0))
+        for item in list(running):
+            try:
+                next(item[1])
+            except StopIteration as stop:
+                results[item[0]] = stop.value
+                running.remove(item)
+        stage += 1
+    return results
 
 
 def part(refs, u):
@@ -230,6 +247,7 @@
                     spread[which, half, pl.ds(r, GROUPS, stride=STEP), :] = part
             for half in (0, 1):
                 out[block, 128 * half : 128 * half + 128] = spread[which, half].astype(BF16)
+            yield
         for i in range(3):
             raw[i, 0:8, :] = jnp.zeros((8, LANES), F32)
             raw[i, 8 : 8 + rows, :] = feat_ref[i, :, lanes].astype(F32)
@@ -243,6 +261,7 @@
             product_ref[lo : lo + size, lanes] = both.astype(BF16)
             grad = cot_ref[lo : lo + size, lanes].astype(F32)
             inner_ref[lo : lo + size, lanes] = (grad * query.astype(F32)).astype(BF16)
+            yield
         masks = group_masks()
         keep = [m.astype(F32).astype(BF16) for m in masks]
         convs, backs = inside(rows)
@@ -258,6 +277,7 @@
             if b == convs[0] or b == convs[-1]:
                 half = STEP * (b == convs[-1])
                 gmix_ref[0, half : half + STEP, lanes] = grad
+            yield
         matrix = behind_ref[block, 0:WINDOW]
         for b, back in filtered(matrix, inner_ref, 0, backs, masks, lanes):
             at = slice(STEP * b, STEP * b + STEP)
@@ -270,6 +290,7 @@
                 if b == backs[0] or b == backs[-1]:
                     half = STEP * (b == backs[-1])
                     gmix_ref[i, half : half + STEP, lanes] = value
+            yield
         for i in range(3):
             totals = [None] * 7
             for lo in (0, 48):
@@ -278,6 +299,7 @@
                 grad_ref[i, lo : lo + 48, lanes] = short_pass(
                     gmix, i, own, weights, totals, lo, 48
                 )
+                yield
             lines = [jnp.sum(total, axis=0, keepdims=True) for total in totals]
             lines.append(jnp.zeros((1, LANES), F32))
             lines_ref[8 * i : 8 * i + 8, lanes] = jnp.concatenate(lines, axis=0)
@@ -291,8 +313,13 @@
 
     @pl.loop(0, cot_ref.shape[1] // LANES // AT_LOCAL)
     def _(step):
-        for u in range(AT_LOCAL):
-            one(AT_LOCAL * step + u, *part((raws, spreads, gmixes), u))
+        staggered(
+            [
+                one(AT_LOCAL * step + u, *part((raws, spreads, gmixes), u))
+                for u in range(AT_LOCAL)
+            ],
+            LAG_LOCAL,
+        )
 
 
 def finish(gmix, i, low, high, shift, feat_ref, lanes, weights, totals, store):
@@ -300,6 +327,7 @@
         size = min(48, high - lo)
         own = feat_ref[i, lo : lo + size, lanes].astype(F32)
         store(lo, size, short_pass(gmix, i, own, weights, totals, lo - shift, size))
+        yield
 
 
 def summed_lines(totals):
@@ -347,6 +375,7 @@
     grid_out[block, 0:WINDOW] = correlated(
         grid_ref[block, 0:WINDOW], lambda b: product, lambda b: ginn[...], [0], keep
     )
+    yield
     outer = list(range(convs[0]))
     for b, conv in filtered(ahead_ref[block, 0:WINDOW], prod, 0, outer, masks, every):
         at = slice(STEP * b, STEP * b + STEP)
@@ -354,6 +383,7 @@
         query = start[0] if b == 0 else mixed_ref[0, at, lanes].astype(F32)
         gmix[0, at, :] = (cot_ref[at, lanes].astype(F32) * inner).astype(BF16).astype(F32)
         gated_ref[at, :] = (query * inner).astype(BF16)
+        yield
     gated_ref[STEP * convs[0] : rows, :] = near_gated[:, lanes]
     for b, back in filtered(behind_ref[block, 0:WINDOW], ginn, 0, [0], masks, every):
         grad = back + gain * inners.astype(F32)
@@ -367,7 +397,7 @@
         def store(lo, size, grad):
             grad_ref[i, lo : lo + size, lanes] = grad
 
-        finish(gmix, i, 0, known, 0, feat_ref, lanes, weights, totals[i], store)
+        yield from finish(gmix, i, 0, known, 0, feat_ref, lanes, weights, totals[i], store)
     lines_out[:, lanes] = lines_ref[:, lanes] + summed_lines(totals)
 
 
@@ -409,13 +439,17 @@
     ).astype(BF16)
 
     outer = list(range(backs[-1] + 1, chunks))
-    grid = correlated(
-        grid_ref[block, 0:WINDOW],
-        lambda b: prod[STEP * b - base : STEP * b - base + STEP, :],
-        lambda b: ginn[STEP * b - base : STEP * b - base + WINDOW, :],
-        outer,
-        keep,
-    )
+    yield
+    grid = grid_ref[block, 0:WINDOW]
+    for at in range(0, len(outer), 2):
+        grid = correlated(
+            grid,
+            lambda b: prod[STEP * b - base : STEP * b - base + STEP, :],
+            lambda b: ginn[STEP * b - base : STEP * b - base + WINDOW, :],
+            outer[at : at + 2],
+            keep,
+        )
+        yield
     corr[0] = grid[:, 0:128]
     corr[1, :, 0 : WINDOW - 128] = grid[:, 128:WINDOW]
     corr[1, :, WINDOW - 128 : 128] = jnp.zeros((LANES, 256 - WINDOW), F32)
@@ -433,6 +467,7 @@
         for i, other in ((1, 2), (2, 1)):
             value = end[other] if b == chunks else mixed_ref[other, at, lanes].astype(F32)
             gmix[i, to, :] = (grad * value).astype(BF16).astype(F32)
+        yield
 
     skip = first_ref[0, :, lanes].astype(F32) * first_ref[1, :, lanes].astype(F32)
     for lo in range(STEP, rows, STEP):
@@ -456,7 +491,7 @@
         def store(lo, size, grad):
             grad_ref[i, lo : lo + size, :] = grad
 
-        finish(gmix, i, stop, rows, shift, feat_ref, lanes, weights, totals[i], store)
+        yield from finish(gmix, i, stop, rows, shift, feat_ref, lanes, weights, totals[i], store)
         grad_ref[i, 0:known, :] = early_grad[i, 0:known, lanes]
         grad_ref[i, known:stop, :] = near_grad[i, :, lanes]
     lines = summed_lines(totals) + lines_ref[:, lanes]
@@ -467,20 +502,25 @@
 
 def before_kernel(*refs):
     ins, (gated_ref, *outs), scratch = refs[:14], refs[14:19], refs[19:]
+    blocks = []
     for u in range(TOGETHER):
         gated = gated_ref.at[:, LANES * u : LANES * u + LANES]
         step = TOGETHER * pl.program_id(0) + u
-        before_block(step, *ins, gated, *outs, *part(scratch, u))
+        blocks.append(before_block(step, *ins, gated, *outs, *part(scratch, u)))
+    staggered(blocks, LAG_BEFORE)
 
 
 def after_kernel(*refs):
     ins, (grad_ref, sums_ref), scratch = refs[:15], refs[15:17], refs[17:]
     first = pl.program_id(0) == 0
     short = jnp.where(first, 0.0, sums_ref[72:96, :])
+    blocks = []
     for u in range(TOGETHER):
         grad = grad_ref.at[:, :, LANES * u : LANES * u + LANES]
         step = TOGETHER * pl.program_id(0) + u
-        short = short + after_block(step, *ins, grad, sums_ref, *part(scratch, u))
+        blocks.append(after_block(step, *ins, grad, sums_ref, *part(scratch, u)))
+    for term in staggered(blocks, LAG_AFTER):
+        short = short + term
     sums_ref[72:96, :] = short
 
 

time: 71.4 us -> 70.3 us (0.985)
  Pallas kernels: 19 us -> 17.9 us
    pallas_call x1, Pallas kernels: 5.82 us -> 4.93 us  [body(): call(after_kernel, 'after', [inside_vmem] * 15, [(blocks3(rows), shape((3...]
  transfers between devices with their start and end apart: 2 -> 2, of which waited for: 0 -> 1; matrix products, arithmetic and copies ran while one was open for 0% -> 0% of each run, Pallas kernels for 13% -> 13%
where the time goes in v6:
time: 70.3 us; the launch traced here: 70 us
  blocking collectives  45.7 us (65%)
  Pallas kernels  17.9 us (25%)
  starting transfers between devices  4.79 us (7%)
  between operations  0.75 us (1%)
  local copies, waits for them, and re-layouts  0.74 us (1%)
    all_to_all x3, blocking collectives, swap(): return lax.all_to_all(values, axes, 0, 0, tiled=True)  45.7 us
    pallas_call x1, Pallas kernels, body(): call(local_kernel, 'local', [inside_vmem] * 5, mixers + [held(STEP * len(...  6.24 us
    pallas_call x1, Pallas kernels, body(): call(after_kernel, 'after', [inside_vmem] * 15, [(blocks3(rows), shape((3...  4.93 us
    ppermute x2, starting transfers between devices, passed_along(): return lax.ppermute(block, axis, route)  4.79 us
    pallas_call x1, Pallas kernels, body(): call(edge_kernel, 'edge', [outside] * 3, [(outside, shape((160, width), B...  3.25 us
    pallas_call x1, Pallas kernels, body(): call(before_kernel, 'before', [inside_vmem] * 14, [(blocks2(rows), shape(...  2.89 us
  transfers between devices with their start and end apart: 2, of which 1 were waited for; matrix products, arithmetic and copies ran while one was open for 0% of the time, Pallas kernels for 13%

profile of v6, /device:TPU:192, one launch (start us, length us, event | category | flops | bytes accessed | tf_op | source)
XLA Modules:
  0.0 70.0 jit_solution(6361529602578143640)
XLA Ops:
  0.6 0.0 copy-start
  0.6 0.0 copy-start.1
  0.7 0.0 copy-start.2
  0.7 0.0 copy-start.4
  0.7 3.2 %edge.1 = (bf16[160,1024]{1,0:T(8,128)(2,1)}, bf16[160,1024]{1,0:T(8,128)(2,1)}) custom-call(bf16[3,256,1024]{2,1,0:T(8,128)(2,1)} %refs_0_.3, bf16[256,1024]{1,0:T(8,128)(2,1)} %refs_1_.1, bf16[3,7,64]{2,1,0:T(8,128)(2,1)} %bitcast.8), custom_call_target="tpu_custom_call" | custom-call | flops 5000000 | bytes 5000000 | tf_op jit(solution)/shard_map/edge/pallas_call | solution.py:587
  3.9 3.5 %collective-permute-start = (bf16[160,1024]{1,0:T(8,128)(2,1)}, bf16[160,1024]{1,0:T(8,128)(2,1)S(1)}, u32[]{:S(2)}, u32[]{:S(2)}) collective-permute-start(bf16[160,1024]{1,0:T(8,128)(2,1)} %get-tuple-element.40), channel_id=1, source_target_pairs={{0,8},{8,16},{16,24},{24,32},{32,40},{40,48},{48,56},{56,64},{64,7... | collective-permute-start | bytes 983048 | tf_op jit(solution)/shard_map/ppermute | solution.py:29
  7.4 1.3 %collective-permute-start.1 = (bf16[160,1024]{1,0:T(8,128)(2,1)}, bf16[160,1024]{1,0:T(8,128)(2,1)S(1)}, u32[]{:S(2)}, u32[]{:S(2)}) collective-permute-start(bf16[160,1024]{1,0:T(8,128)(2,1)} %get-tuple-element.47), channel_id=1, source_target_pairs={{8,0},{16,8},{24,16},{32,24},{40,32},{48,40},{56,48},{64,56},{72,6... | collective-permute-start | bytes 983048 | tf_op jit(solution)/shard_map/ppermute | solution.py:29
  8.7 0.0 copy-done
  8.7 0.0 copy-done.1
  8.8 0.0 copy-done.2
  8.8 0.0 copy-done.4
  8.8 0.0 copy-start.3
  8.8 0.7 %copy-done.3 = bf16[64,128]{1,0:T(8,128)(2,1)S(1)} copy-done((bf16[64,128]{1,0:T(8,128)(2,1)S(1)}, bf16[64,128]{1,0:T(8,128)(2,1)}, u32[]{:S(2)}) %copy-start.3) | copy-done | bytes 16408
  9.5 6.2 %local.1 = (f32[24,1024]{1,0:T(8,128)S(1)}, f32[8,128]{1,0:T(8,128)S(1)}, bf16[3,256,1024]{2,1,0:T(8,128)(2,1)S(1)}, bf16[256,1024]{1,0:T(8,128)(2,1)S(1)}, bf16...) custom-call(bf16[3,256,1024]{2,1,0:T(8,128)(2,1)S(1)} %copy-done, ...), custom_call_target="tpu_custom_call" | custom-call | flops 20000000 | bytes 20000000 | tf_op jit(solution)/shard_map/local/pallas_call | solution.py:621
  15.7 0.0 collective-permute-done.refs_13_
  15.8 2.9 %before.1 = (bf16[256,1024]{1,0:T(8,128)(2,1)}, bf16[2,16,1024]{2,1,0:T(8,128)(2,1)S(1)}, bf16[3,144,1024]{2,1,0:T(8,128)(2,1)S(1)}, f32[24,1024]{1,0:T(8,128)S(1)}, f32[1024,256]{1,0:T(8,128)S(1)}) custom-call(bf16[3,256,1024]{2,1,0:T(8,128)(2,1)S(1)} %copy-done, bf16[256,1024]{1,0:T(8,128)(2,1)S(1)} %copy-done.1, ...), custom_call_target="tpu_custom_call" | custom-call | flops 10000000 | bytes 10000000 | tf_op jit(solution)/shard_map/before/pallas_call | solution.py:637
  18.6 0.1 collective-permute-done.1.refs_14_
  18.7 4.9 %after.1 = (bf16[3,256,1024]{2,1,0:T(8,128)(2,1)}, f32[96,128]{1,0:T(8,128)S(1)}) custom-call(bf16[3,256,1024]{2,1,0:T(8,128)(2,1)S(1)} %copy-done, f32[24,1024]{1,0:T(8,128)S(1)} %get-tuple-element.29.refs_2_.refs_1_, f32[8,128]{1,0:T(8,128)S(1)} %get-tuple-element.30.refs_3_.refs_2_, bf16[3,256,1024]{2,1,0:T(8,128)(2,1)S(1)} %get-tuple-element.31.refs_4_.refs_3_, ...), custom_call_target="tpu_custom_call" | custom-call | flops 10000000 | bytes 10000000 | tf_op jit(solution)/shard_map/after/pallas_call | solution.py:658
  23.6 20.6 %all_to_all.15 = f32[12,8,128]{2,1,0:T(8,128)S(1)} all-to-all(f32[12,8,128]{2,1,0:T(8,128)S(1)} %bitcast.7), channel_id=1, replica_groups=mesh['ctx_0'=4,'ctx_1'=3,'ctx_2'=8,'tp'=8] {'ctx_0','ctx_1'}, dimensions={0} | all-to-all | bytes 98304 | tf_op jit(solution)/shard_map/all_to_all | solution.py:545
  44.3 14.0 %all_to_all.16 = f32[8,8,128]{2,1,0:T(8,128)S(1)} all-to-all(f32[8,8,128]{2,1,0:T(8,128)S(1)} %broadcast_in_dim.4), channel_id=1, replica_groups=mesh['ctx_0'=4,'ctx_1'=3,'ctx_2'=8,'tp'=8] {'ctx_2'}, dimensions={0} | all-to-all | bytes 65536 | tf_op jit(solution)/shard_map/all_to_all | solution.py:545
  58.3 11.1 %all_to_all.17 = f32[12,8,128]{2,1,0:T(8,128)S(1)} all-to-all(f32[12,8,128]{2,1,0:T(8,128)S(1)} %broadcast_in_dim.5), channel_id=1, replica_groups=mesh['ctx_0'=4,'ctx_1'=3,'ctx_2'=8,'tp'=8] {'ctx_0','ctx_1'}, dimensions={0} | all-to-all | bytes 98304 | tf_op jit(solution)/shard_map/all_to_all | solution.py:545
  69.4 0.6 final.1
  (4 shorter events, 0.0 us)
Async XLA Ops:
  0.6 8.1 %copy-start = (bf16[3,256,1024]{2,1,0:T(8,128)(2,1)S(1)}, bf16[3,256,1024]{2,1,0:T(8,128)(2,1)}, u32[]{:S(2)}) copy-start(bf16[3,256,1024]{2,1,0:T(8,128)(2,1)} %refs_0_.3) | copy-start | bytes 4718596
  0.6 8.1 %copy-start.1 = (bf16[256,1024]{1,0:T(8,128)(2,1)S(1)}, bf16[256,1024]{1,0:T(8,128)(2,1)}, u32[]{:S(2)}) copy-start(bf16[256,1024]{1,0:T(8,128)(2,1)} %refs_1_.1) | copy-start | bytes 1572868
  0.7 8.1 %copy-start.2 = (bf16[3,64,7]{1,2,0:T(8,128)(2,1)S(1)}, bf16[3,64,7]{1,2,0:T(8,128)(2,1)}, u32[]{:S(2)}) copy-start(bf16[3,64,7]{1,2,0:T(8,128)(2,1)} %param.6) | copy-start | bytes 8068
  0.7 8.1 %copy-start.4 = (bf16[1024]{0:T(1024)(128)(2,1)S(1)}, bf16[1024]{0:T(1024)(128)(2,1)}, u32[]{:S(2)}) copy-start(bf16[1024]{0:T(1024)(128)(2,1)} %param.8) | copy-start | bytes 6148
  3.9 11.8 %collective-permute-start = (bf16[160,1024]{1,0:T(8,128)(2,1)}, bf16[160,1024]{1,0:T(8,128)(2,1)S(1)}, u32[]{:S(2)}, u32[]{:S(2)}) collective-permute-start(bf16[160,1024]{1,0:T(8,128)(2,1)} %get-tuple-element.40), channel_id=1, source_target_pairs={{0,8},{8,16},{16,24},{24,32},{32,40},{40,48},{48,56},{56,64},{64,7... | collective-permute-start | bytes 983048 | tf_op jit(solution)/shard_map/ppermute | solution.py:29
  7.4 11.3 %collective-permute-start.1 = (bf16[160,1024]{1,0:T(8,128)(2,1)}, bf16[160,1024]{1,0:T(8,128)(2,1)S(1)}, u32[]{:S(2)}, u32[]{:S(2)}) collective-permute-start(bf16[160,1024]{1,0:T(8,128)(2,1)} %get-tuple-element.47), channel_id=1, source_target_pairs={{8,0},{16,8},{24,16},{32,24},{40,32},{48,40},{56,48},{64,56},{72,6... | collective-permute-start | bytes 983048 | tf_op jit(solution)/shard_map/ppermute | solution.py:29
  8.8 0.7 %copy-start.3 = (bf16[64,128]{1,0:T(8,128)(2,1)S(1)}, bf16[64,128]{1,0:T(8,128)(2,1)}, u32[]{:S(2)}) copy-start(bf16[64,128]{1,0:T(8,128)(2,1)} %long_ref.1) | copy-start | bytes 49156
